TPU v7x, 256 devices: a whole 4x4x8 slice. The times are simulated.
256 devices in a mesh: grp: 8 (over y, core), tbl: 32 (over z, x).
Axes of the slice: x: 4, y: 4, z: 8, core: 2. Of those that a mesh axis runs over, the one named last changes fastest.
Arguments:
- user_feats: bfloat16 [4096, 128], P(('grp', 'tbl')), may hold values from -6 to 6
- tower_in: bfloat16 [128, 4096], replicated, may hold values from -0.5 to 0.5
- tower_out: bfloat16 [4096, 256], replicated, may hold values from -0.09375 to 0.09375
- table: bfloat16 [8192, 256], P('tbl'), may hold values from -3 to 3
- inter_weight: bfloat16 [256, 512], replicated, may hold values from -0.375 to 0.375
- out_weight: float32 [512], replicated, may hold values from -0.3 to 0.3
- ids: int32 [256, 32, 4, 32], P(('grp', 'tbl')), may hold values from 0 to 255
- live: int32 [256, 32], P(('grp', 'tbl')), may hold values from 1 to 32, as said below
- req_of: int32 [256, 32, 32], P(('grp', 'tbl')), may hold values from 0 to 511
- labels: float32 [256, 32, 32], P(('grp', 'tbl')), may hold values from 0 to 1
Outputs:
- scores: float32 [256, 32, 32], P(('grp', 'tbl'))
- grad_tower_in: float32 [128, 4096], replicated
- grad_tower_out: float32 [4096, 256], replicated
- grad_inter: float32 [256, 512], replicated
- grad_out: float32 [512], replicated
- grad_table: float32 [8192, 256], P('tbl')
Inputs may be any that keep to these rules, and one draw needn't show every extreme that they name: In every draw, in each group, some device gets 32 live slots from every owner; the others get between 1 and 32 live slots from each owner.
All inputs are finite; a program needn't handle non-finite values.
Results may differ from a plain program's by a relative error of at most 0.0067.
Values may be sent and summed in bfloat16 or wider, within the bound.
No kernel may reach another device: no remote copies, remote signals or barrier semaphores. Data moves between devices by JAX's collectives and lax.ppermute only.
A program may use at most 64 MiB of HBM per device.

v0:
```python
import math

import jax
import jax.numpy as jnp
from jax import lax
from jax.experimental import pallas as pl
from jax.experimental.pallas import tpu as pltpu
from jax.sharding import PartitionSpec as P


BF = jnp.bfloat16
F32 = jnp.float32


def mm(a, b):
    return jnp.dot(a, b, preferred_element_type=F32)


def mm_nt(a, b):
    return lax.dot_general(a, b, (((1,), (1,)), ((), ())), preferred_element_type=F32)


def slope_of(value, sig):
    return sig * (1.0 + value * (1.0 - sig))


def pool_kernel(ids_ref, table_ref, items_ref, counts_ref):
    rows, cands = counts_ref.shape
    row = lax.broadcasted_iota(jnp.int32, (rows, cands), 0)
    total = jnp.zeros((rows, cands), F32)
    for b in range(ids_ref.shape[0]):
        total = total + jnp.where(row == ids_ref[b : b + 1, :], 1.0, 0.0)
    counts = total.astype(BF)
    counts_ref[...] = counts
    items_ref[...] = mm(table_ref[...].astype(F32).T.astype(BF), counts).astype(BF)


def pool(ids, table):
    cands = ids.shape[1]
    rows, width = table.shape
    return pl.pallas_call(
        pool_kernel,
        out_shape=(
            jax.ShapeDtypeStruct((width, cands), BF),
            jax.ShapeDtypeStruct((rows, cands), BF),
        ),
        compiler_params=pltpu.CompilerParams(vmem_limit_bytes=8 << 20),
        cost_estimate=pl.CostEstimate(
            flops=2 * cands * rows * width, bytes_accessed=2 << 20, transcendentals=0
        ),
        name="pool",
    )(ids, table)


def sigmoid(value):
    return 0.5 * jnp.tanh(0.5 * value) + 0.5


def hbm(array):
    return pltpu.with_memory_space_constraint(array, pltpu.HBM)


def flat(ref):
    value = ref[...]
    if len(value.shape) == 3:
        return value.reshape(value.shape[0] * value.shape[1], value.shape[2])
    half = value.shape[1] // 2
    return jnp.concatenate([value[:, :half], value[:, half:]], axis=0)


def feats_spec(array, each, uf):
    if len(array.shape) == 3:
        return pl.BlockSpec((array.shape[0], each, uf), lambda i: (0, 0, 0))
    return pl.BlockSpec((array.shape[0] // 2, 2 * uf), lambda i: (0, 0))


def users_kernel(feats_ref, win_ref, wout_ref, users_ref, acc):
    step = pl.program_id(0)
    half = mm_nt(win_ref[...], flat(feats_ref))
    part = mm(wout_ref[...], (half * jnp.tanh(half) + half).astype(BF))

    @pl.when(step == 0)
    def _():
        acc[...] = part

    @pl.when(step > 0)
    def _():
        acc[...] += part

    @pl.when(step == pl.num_programs(0) - 1)
    def _():
        users_ref[...] = acc[...].astype(BF)


def user_vectors(feats, win_t, wout_t, each):
    width, wide = wout_t.shape
    uf = win_t.shape[1]
    reqs = feats.shape[0] * each
    block = 512
    return pl.pallas_call(
        users_kernel,
        grid=(wide // block,),
        in_specs=[
            feats_spec(feats, each, uf),
            pl.BlockSpec((block, uf), lambda i: (i, 0)),
            pl.BlockSpec((width, block), lambda i: (0, i)),
        ],
        out_specs=pl.BlockSpec((width, reqs), lambda i: (0, 0)),
        out_shape=jax.ShapeDtypeStruct((width, reqs), BF),
        scratch_shapes=[pltpu.VMEM((width, reqs), F32)],
        compiler_params=pltpu.CompilerParams(vmem_limit_bytes=12 << 20),
        cost_estimate=pl.CostEstimate(
            flops=2 * reqs * wide * (uf + width),
            bytes_accessed=4 << 20,
            transcendentals=reqs * wide,
        ),
        name="users",
    )(feats, hbm(win_t), hbm(wout_t))


def hidden_of(feats, half_win):
    half = mm_nt(half_win, feats)
    turn = jnp.tanh(half)
    hid = half * turn + half
    rest = 0.5 - 0.5 * turn
    return hid.astype(BF), (1.0 - rest) + hid * rest


def rank_kernel(
    factor, slots, users_ref, items_ref, counts_ref, came_ref, iw_ref, w_ref,
    sent_ref, share_ref, acc_u, acc_g, acc_t, acc_o, acc_s,
):
    cands = items_ref.shape[1]
    reqs = users_ref.shape[1]
    width, _ = iw_ref.shape
    step_c = 256
    iw = iw_ref[...]
    iw_t = iw.astype(F32).T.astype(BF)
    weight = w_ref[...]
    users = users_ref[...]
    shards, _, uf = came_ref.shape
    each = reqs // shards
    near = step_c // slots
    came = came_ref[:, each : 2 * each, :].astype(F32)
    line = lax.broadcasted_iota(jnp.int32, came.shape, 1)
    facts = [jnp.sum(jnp.where(line == n, came, 0.0), axis=1) for n in range(2)]
    src = lax.broadcasted_iota(jnp.int32, (uf, step_c), 0)
    dst = lax.broadcasted_iota(jnp.int32, (uf, step_c), 1) % slots
    spread = [jnp.where(src == dst + n * slots, 1.0, 0.0).astype(BF) for n in range(4)]
    src = lax.broadcasted_iota(jnp.int32, (step_c, width), 0) % slots
    dst = lax.broadcasted_iota(jnp.int32, (step_c, width), 1)
    gather = [jnp.where(src + n * slots == dst, 1.0, 0.0).astype(BF) for n in range(3)]
    mine = (
        lax.broadcasted_iota(jnp.int32, (near, step_c), 0)
        == lax.broadcasted_iota(jnp.int32, (near, step_c), 1) // slots
    )
    slot = lax.broadcasted_iota(jnp.int32, (1, step_c), 1) % slots
    for k in range(cands // step_c):
        cut = slice(k * step_c, (k + 1) * step_c)
        meta = []
        for n in range(6):
            part = facts[n // 4][k * near : (k + 1) * near, :].astype(BF)
            wide_part = jnp.where(mine, mm(part, spread[n % 4]), 0.0)
            meta.append(jnp.sum(wide_part, axis=0, keepdims=True))
        request = (meta[0] * 16.0 + meta[1]).astype(jnp.int32)
        target = meta[2] + meta[3] + meta[4]
        live = meta[5]
        row = lax.broadcasted_iota(jnp.int32, (reqs, step_c), 0)
        pick = jnp.where(row == request, 1.0, 0.0).astype(BF)
        chosen = mm(users, pick)
        item = items_ref[:, cut].astype(F32)
        cross = (item * chosen).astype(BF)
        inner = mm(iw_t, cross)
        sig = sigmoid(inner)
        act = inner * sig
        score = jnp.sum(act * weight, axis=0, keepdims=True)
        s_hi = score.astype(BF).astype(F32)
        s_mid = (score - s_hi).astype(BF).astype(F32)
        row_out = jnp.zeros((near, width), F32)
        for n, v in enumerate((s_hi, s_mid, (score - s_hi) - s_mid)):
            row_out = row_out + mm(jnp.where(mine, v, 0.0).astype(BF), gather[n])
        acc_s[k * near : (k + 1) * near, :] = row_out
        grad = jnp.where(slot.astype(F32) < live, sigmoid(score) - target, 0.0) * factor
        dz = (grad * weight * slope_of(inner, sig)).astype(BF)
        dcross = mm(iw, dz)
        d_item = (dcross * chosen).astype(BF)
        d_user = (dcross * item).astype(BF)
        terms = mm_nt(pick, d_user)
        g_in = mm_nt(cross, dz)
        g_t = mm_nt(counts_ref[:, cut], d_item)
        g_o = mm_nt(jnp.broadcast_to(grad, (8, step_c)), act)
        if k == 0:
            acc_u[...] = terms
            acc_g[...] = g_in
            acc_t[...] = g_t
            acc_o[...] = g_o
        else:
            acc_u[...] += terms
            acc_g[...] += g_in
            acc_t[...] += g_t
            acc_o[...] += g_o
    sent_ref[:, 0:each, :] = acc_u[...].astype(BF).reshape(shards, each, width)
    half = shards // 2
    sent_ref[0:half, each : 2 * each, :] = acc_g[:, 0:width].astype(BF).reshape(half, each, width)
    sent_ref[half:, each : 2 * each, :] = acc_g[:, width:].astype(BF).reshape(half, each, width)
    line = lax.broadcasted_iota(jnp.int32, (shards, 4, width), 1)
    tail = jnp.where(
        line == 0,
        acc_o[0:1, 0:width][None],
        jnp.where(
            line == 1,
            acc_o[0:1, width:][None],
            jnp.where(line == 2, acc_s[...][:, None, :], 0.0),
        ),
    )
    sent_ref[:, 2 * each : 2 * each + 4, :] = tail.astype(BF)
    feats = came_ref[:, 0:each, :].reshape(reqs, uf)
    top = reqs // 2
    share_ref[0:top, 0:uf] = feats[0:top]
    share_ref[0:top, uf:] = feats[top:]
    share_ref[top:, :] = acc_t[...].astype(BF)


def rank(factor, slots, users, items, counts, came, iw, weight):
    width, cands = items.shape
    reqs = users.shape[1]
    hi_units = iw.shape[1]
    rows = counts.shape[0]
    shards = came.shape[0]
    each = reqs // shards
    return pl.pallas_call(
        lambda *refs: rank_kernel(factor, slots, *refs),
        out_shape=(
            jax.ShapeDtypeStruct((shards, 2 * each + 4, width), BF),
            jax.ShapeDtypeStruct((reqs // 2 + rows, width), BF),
        ),
        scratch_shapes=[
            pltpu.VMEM((reqs, width), F32),
            pltpu.VMEM((width, hi_units), F32),
            pltpu.VMEM((rows, width), F32),
            pltpu.VMEM((8, hi_units), F32),
            pltpu.VMEM((shards, width), F32),
        ],
        compiler_params=pltpu.CompilerParams(vmem_limit_bytes=16 << 20),
        cost_estimate=pl.CostEstimate(
            flops=2 * cands * width * (reqs * 2 + hi_units * 3 + rows),
            bytes_accessed=4 << 20,
            transcendentals=cands * hi_units,
        ),
        name="rank",
    )(users, items, counts, came, iw, weight)


def fold_kernel(back_ref, own_ref, part_ref):
    each, _ = own_ref.shape
    total = back_ref[0, 0 : 2 * each + 4, :].astype(F32)
    for n in range(1, back_ref.shape[0]):
        total = total + back_ref[n, 0 : 2 * each + 4, :].astype(F32)
    own_ref[...] = total[0:each].astype(BF)
    part_ref[...] = total[each:].astype(BF)


def fold(back, each):
    width = back.shape[2]
    return pl.pallas_call(
        fold_kernel,
        out_shape=(
            jax.ShapeDtypeStruct((each, width), BF),
            jax.ShapeDtypeStruct((each + 4, width), BF),
        ),
        compiler_params=pltpu.CompilerParams(vmem_limit_bytes=6 << 20),
        name="fold",
    )(back)


def own_kernel(d_ref, feats_ref, win_ref, wout_ref, gout_ref, gin_ref):
    feats = flat(feats_ref)
    d = flat(d_ref)
    hid, slope = hidden_of(feats, win_ref[...])
    gout_ref[...] = mm(hid, d)
    d_pre = (mm_nt(wout_ref[...], d) * slope).astype(BF)
    gin_ref[...] = mm(d_pre, feats).T


def dense_own(d, feats, win_t, tower_out, each):
    wide, width = tower_out.shape
    uf = win_t.shape[1]
    reqs = each * feats.shape[0]
    block = 512
    return pl.pallas_call(
        own_kernel,
        grid=(wide // block,),
        in_specs=[
            feats_spec(d, each, width),
            feats_spec(feats, each, uf),
            pl.BlockSpec((block, uf), lambda i: (i, 0)),
            pl.BlockSpec((block, width), lambda i: (i, 0)),
        ],
        out_specs=(
            pl.BlockSpec((block, width), lambda i: (i, 0)),
            pl.BlockSpec((uf, block), lambda i: (0, i)),
        ),
        out_shape=(pltpu.HBM((wide, width), F32), pltpu.HBM((uf, wide), F32)),
        compiler_params=pltpu.CompilerParams(vmem_limit_bytes=14 << 20),
        cost_estimate=pl.CostEstimate(
            flops=2 * reqs * wide * (2 * width + 2 * uf),
            bytes_accessed=10 << 20,
            transcendentals=reqs * wide,
        ),
        name="dense_own",
    )(d, feats, hbm(win_t), hbm(tower_out))


def far_kernel(count, *refs):
    d, feats = refs[0:count], refs[count : 2 * count]
    win_ref, wout_ref, old_out, old_in, gout_ref, gin_ref = refs[2 * count :]
    wout = wout_ref[...]
    win = win_ref[...]
    out, back = old_out[...], None
    for k in range(count):
        d_k = d[k][...]
        feats_k = flat(feats[k])
        hid, slope = hidden_of(feats_k, win)
        out = out + mm(hid, d_k)
        d_pre = (mm_nt(wout, d_k) * slope).astype(BF)
        turn = mm(d_pre, feats_k)
        back = turn if back is None else back + turn
    gout_ref[...] = out.astype(BF)
    gin_ref[...] = (back.T + old_in[...]).astype(BF)


def dense_far(d, feats, win_t, tower_out, before, first, units):
    _, width = tower_out.shape
    reqs = d[0].shape[0]
    uf = win_t.shape[1]
    count = len(d)
    block = 512
    base = first // block
    return pl.pallas_call(
        lambda *refs: far_kernel(count, *refs),
        grid=(units // block,),
        in_specs=[pl.BlockSpec((reqs, width), lambda i: (0, 0))] * count
        + [pl.BlockSpec((reqs // 2, 2 * uf), lambda i: (0, 0))] * count
        + [
            pl.BlockSpec((block, uf), lambda i: (base + i, 0)),
            pl.BlockSpec((block, width), lambda i: (base + i, 0)),
            pl.BlockSpec((block, width), lambda i: (base + i, 0)),
            pl.BlockSpec((uf, block), lambda i: (0, base + i)),
        ],
        out_specs=(
            pl.BlockSpec((block, width), lambda i: (i, 0)),
            pl.BlockSpec((uf, block), lambda i: (0, i)),
        ),
        out_shape=(
            jax.ShapeDtypeStruct((units, width), BF),
            jax.ShapeDtypeStruct((uf, units), BF),
        ),
        compiler_params=pltpu.CompilerParams(vmem_limit_bytes=20 << 20),
        cost_estimate=pl.CostEstimate(
            flops=2 * count * reqs * units * (2 * width + 2 * uf),
            bytes_accessed=10 << 20,
            transcendentals=count * reqs * units,
        ),
        name="dense_far",
    )(*[hbm(x) for x in (*d, *feats, win_t, tower_out, *before)])


def finish_kernel(*refs):
    out_a, out_b, in_a, in_b = refs[0:4]
    gout_ref, gin_ref = refs[-2:]
    gout_ref[...] = out_a[...].astype(F32) + out_b[...].astype(F32)
    gin_ref[...] = in_a[...].astype(F32) + in_b[...].astype(F32)


def finish(outs, ins, before, first, wide):
    units, width = outs[0].shape
    uf = ins[0].shape[0]
    block = 512
    base = first // block
    spec_o = pl.BlockSpec((block, width), lambda i: (i, 0))
    spec_i = pl.BlockSpec((uf, block), lambda i: (0, i))
    extra = [] if before is None else [pl.BlockSpec(memory_space=pl.ANY)] * 2
    return pl.pallas_call(
        finish_kernel,
        grid=(units // block,),
        in_specs=[spec_o, spec_o, spec_i, spec_i] + extra,
        out_specs=(
            pl.BlockSpec((block, width), lambda i: (base + i, 0)),
            pl.BlockSpec((uf, block), lambda i: (0, base + i)),
        ),
        out_shape=(pltpu.HBM((wide, width), F32), pltpu.HBM((uf, wide), F32)),
        input_output_aliases={} if before is None else {4: 0, 5: 1},
        compiler_params=pltpu.CompilerParams(vmem_limit_bytes=8 << 20),
        name="finish",
    )(*outs, *ins, *(before or ()))


def pack_kernel(feats_ref, req_ref, lab_ref, live_ref, out_ref):
    shards, slots = req_ref.shape
    each, lanes = feats_ref.shape
    req = req_ref[...].astype(F32)
    high = jnp.floor(req * (1.0 / 16.0))
    lab = lab_ref[...]
    lab_hi = lab.astype(BF).astype(F32)
    lab_mid = (lab - lab_hi).astype(BF).astype(F32)
    eye = lax.broadcasted_iota(jnp.int32, (shards, shards), 0) == lax.broadcasted_iota(
        jnp.int32, (shards, shards), 1
    )
    live = jnp.sum(
        jnp.where(eye, live_ref[...].astype(F32), 0.0), axis=1, keepdims=True
    )
    rows = []
    for group in (
        (high, req - high * 16.0, lab_hi, lab_mid),
        (lab - lab_hi - lab_mid, jnp.broadcast_to(live, (shards, slots))),
    ):
        total = jnp.zeros((shards, lanes), F32)
        for k, v in enumerate(group):
            src = lax.broadcasted_iota(jnp.int32, (slots, lanes), 0) + k * slots
            dst = lax.broadcasted_iota(jnp.int32, (slots, lanes), 1)
            total = total + mm(v.astype(BF), jnp.where(src == dst, 1.0, 0.0).astype(BF))
        rows.append(total)
    line = lax.broadcasted_iota(jnp.int32, (shards, each, lanes), 1)
    facts = jnp.where(
        line == 0, rows[0][:, None, :], jnp.where(line == 1, rows[1][:, None, :], 0.0)
    )
    out_ref[:, 0:each, :] = jnp.broadcast_to(feats_ref[...][None], (shards, each, lanes))
    out_ref[:, each : 2 * each, :] = facts.astype(BF)


def pack(feats, req, lab, live):
    each, lanes = feats.shape
    shards = req.shape[0]
    return pl.pallas_call(
        pack_kernel,
        out_shape=jax.ShapeDtypeStruct((shards, 2 * each, lanes), BF),
        compiler_params=pltpu.CompilerParams(vmem_limit_bytes=16 << 20),
        name="pack",
    )(*[hbm(x) for x in (feats, req, lab, live)])


def body(
    user_feats, tower_in, tower_out, table, inter_weight, out_weight, ids, live, req_of, labels
):
    groups = lax.axis_size("grp")
    shards = lax.axis_size("tbl")
    slots = ids.shape[3]
    width = table.shape[1]
    each = user_feats.shape[0]
    reqs = each * shards
    chips = groups // 2

    def ring(turn, other):
        return [
            (y * 2 + c, ((y + turn) % chips) * 2 + (c + other) % 2)
            for y in range(chips)
            for c in range(2)
        ]

    def from_chips(x):
        return [lax.ppermute(x, "grp", ring(turn, 0)) for turn in (1, chips - 1, 2)]

    def swap(x):
        return lax.ppermute(x, "grp", ring(0, 1))

    def group_sum(x):
        pair = (x.astype(F32) + swap(x).astype(F32)).astype(BF)
        a, b, c = from_chips(pair)
        return (pair.astype(F32) + c.astype(F32)) + (a.astype(F32) + b.astype(F32))

    def exchange(x):
        return lax.all_to_all(x, "tbl", split_axis=0, concat_axis=0, tiled=True)

    arrived = exchange(pack(user_feats, req_of[0], labels[0], live))
    ids_rows = jnp.transpose(ids[0], (1, 0, 2)).reshape(ids.shape[2], shards * slots)
    items, counts = pool(ids_rows, table)
    win_t = tower_in.T * jnp.asarray(0.5, BF)
    wout_t = tower_out.T
    users = user_vectors(arrived, win_t, wout_t, each)
    factor = 1.0 / math.sqrt(groups * shards * shards * slots)
    sent, share = rank(
        factor, slots, users, items, counts, arrived, inter_weight, out_weight[:, None]
    )
    back = exchange(sent)
    far = from_chips(share)
    own, part = fold(back, each)
    third = exchange(jnp.broadcast_to(own, (shards, each, width)))
    total = group_sum(part)
    grad_out = total[each : each + 2].reshape(-1)
    s_back = back[:, 2 * each + 2, : 3 * slots].astype(F32)
    scores = (s_back[:, :slots] + s_back[:, slots : 2 * slots]) + s_back[:, 2 * slots :]
    top = reqs // 2
    a, b, c = (f[top:].astype(F32) for f in far)
    column = ((share[top:].astype(F32) + c) + (a + b)).astype(BF)
    grad_table = column.astype(F32) + swap(column).astype(F32)
    d_far = from_chips(third.reshape(reqs, width))
    inter_all = exchange(
        jnp.broadcast_to(total[:each].astype(BF), (shards, each, width))
    )
    before = dense_own(third, arrived, win_t, tower_out, each)
    half = shards // 2
    inter_flat = inter_all.astype(F32)
    grad_inter = jnp.concatenate(
        [inter_flat[:half].reshape(width, width), inter_flat[half:].reshape(width, width)],
        axis=1,
    )
    units = tower_out.shape[0] // 2
    sums = None
    pieces = []
    for k in range(2):
        g_out, g_in = dense_far(d_far, far, win_t, tower_out, before, k * units, units)
        pieces.append(((g_out, swap(g_out)), (g_in, swap(g_in))))
    for k in range(2):
        sums = finish(*pieces[k], sums, k * units, 2 * units)
    return (scores[None], sums[1], sums[0], grad_inter, grad_out, grad_table)


def solution(mesh):
    placed = (
        P(("grp", "tbl"), None),
        P(),
        P(),
        P("tbl", None),
        P(),
        P(),
        P(("grp", "tbl"), None, None, None),
        P(("grp", "tbl"), None),
        P(("grp", "tbl"), None, None),
        P(("grp", "tbl"), None, None),
    )
    return jax.shard_map(
        body,
        mesh=mesh,
        in_specs=placed,
        out_specs=(P(("grp", "tbl"), None, None), P(), P(), P(), P(), P("tbl", None)),
        check_vma=False,
    )
```

profile of v0, /device:TPU:8, one launch (start us, length us, event | category | flops | bytes accessed | tf_op | source)
XLA Modules:
  0.0 152.9 jit_solution(17347641802786949683)
XLA Ops:
  0.6 1.7 %pack.1 = bf16[32,32,128]{2,1,0:T(8,128)(2,1)} custom-call(bf16[16,128]{1,0:T(8,128)(2,1)} %feats_ref.1, s32[32,32]{1,0:T(8,128)} %bitcast.26, f32[32,32]{1,0:T(8,128)} %bitcast.27, s32[1,32]{1,0:T(1,128)} %live_ref.1), custom_call_target="tpu_custom_call" | custom-call | tf_op jit(solution)/shard_map/pack/pallas_call | solution.py:434
  2.3 11.3 %all-to-all-start = ((bf16[32,32,128]{2,1,0:T(8,128)(2,1)}), bf16[32,32,128]{2,1,0:T(8,128)(2,1)S(1)}, u32[]{:S(2)}, u32[]{:S(2)}) async-start(bf16[32,32,128]{2,1,0:T(8,128)(2,1)} %pack.1), calls=%async_computation | async-start | bytes 524288 | tf_op jit(solution)/shard_map/all_to_all | solution.py:472
  13.6 0.8 copy.23
  14.6 0.8 copy.24.refs_5_
  15.4 1.6 %copy.21 = bf16[128,4096]{0,1:T(8,128)(2,1)S(1)} copy(bf16[128,4096]{1,0:T(8,128)(2,1)} %param.11) | data formatting | bytes 2097152 | tf_op args[1]
  17.1 4.1 %copy.22 = bf16[4096,256]{0,1:T(8,128)(2,1)} copy(bf16[4096,256]{1,0:T(8,128)(2,1)} %refs_7_.3) | data formatting | bytes 4194304 | tf_op args[2]
  21.2 0.7 pool.1
  21.8 1.1 multiply_bitcast_fusion.win_ref.refs_6_
  22.9 3.5 %all-to-all-done.feats_ref.refs_3_ = bf16[32,32,128]{2,1,0:T(8,128)(2,1)S(1)} async-done(((bf16[32,32,128]{2,1,0:T(8,128)(2,1)}), bf16[32,32,128]{2,1,0:T(8,128)(2,1)S(1)}, u32[]{:S(2)}, u32[]{:S(2)}) %all-to-all-start) | async-done | bytes 262176 | tf_op jit(solution)/shard_map/all_to_all | solution.py:472
  26.5 7.1 %users.1.refs_0_ = bf16[256,512]{1,0:T(8,128)(2,1)S(1)} custom-call(bf16[32,32,128]{2,1,0:T(8,128)(2,1)S(1)} %all-to-all-done.feats_ref.refs_3_, bf16[4096,128]{1,0:T(8,128)(2,1)} %multiply_bitcast_fusion.win_ref.refs_6_, bf16[256,4096]{1,0:T(8,128)(2,1)} %bitcast.21), custom_call_target="tpu_custom_call" | custom-call | flops 1610612736 | bytes 4194304 | tf_op jit(solution)/shard_map/users/pallas_call | solution.py:100
  33.6 6.1 %rank.1 = (bf16[32,36,256]{2,1,0:T(8,128)(2,1)}, bf16[512,256]{1,0:T(8,128)(2,1)S(1)}) custom-call(bf16[256,512]{1,0:T(8,128)(2,1)S(1)} %users.1.refs_0_, bf16[256,1024]{1,0:T(8,128)(2,1)S(1)} %get-tuple-element.22.refs_1_, bf16[256,1024]{1,0:T(8,128)(2,1)S(1)} %get-tuple-element.23.refs_2_, bf16[32,32,128]{2,1,0:T(8,128)(2,1)S(1)} %all-to-all-done.feats_ref.refs_3_, ...), custom_call_target="tpu_custom_call" | custom-call | flops 1476395008 | bytes 4194304 | tf_op jit(solution)/shard_map/rank/pallas_call | solution.py:231
  39.6 6.2 %all-to-all-start.1 = ((bf16[32,36,256]{2,1,0:T(8,128)(2,1)}), bf16[32,36,256]{2,1,0:T(8,128)(2,1)S(1)}, u32[]{:S(2)}, u32[]{:S(2)}) async-start(bf16[32,36,256]{2,1,0:T(8,128)(2,1)} %get-tuple-element.24), calls=%async_computation.1 | async-start | bytes 1310720 | tf_op jit(solution)/shard_map/all_to_all | solution.py:472
  45.9 2.4 %collective-permute-start.5 = (bf16[512,256]{1,0:T(8,128)(2,1)S(1)}, bf16[512,256]{1,0:T(8,128)(2,1)S(1)}, u32[]{:S(2)}, u32[]{:S(2)}) collective-permute-start(bf16[512,256]{1,0:T(8,128)(2,1)S(1)} %get-tuple-element.26), channel_id=1, source_target_pairs={{0,128},{32,160},{64,192},{96,224},{128,0},{160,32},{192,64},{224,... | collective-permute-start | bytes 786440 | tf_op jit(solution)/shard_map/ppermute | solution.py:461
  48.2 1.3 collective-permute-start.4
  49.6 0.7 collective-permute-start.3
  50.3 6.4 %collective-permute-done.5.refs_5_ = bf16[512,256]{1,0:T(8,128)(2,1)S(1)} collective-permute-done((bf16[512,256]{1,0:T(8,128)(2,1)S(1)}, bf16[512,256]{1,0:T(8,128)(2,1)S(1)}, u32[]{:S(2)}, u32[]{:S(2)}) %collective-permute-start.5) | collective-permute-done | bytes 262176 | tf_op jit(solution)/shard_map/ppermute | solution.py:461
  56.7 3.6 %collective-permute-done.4.refs_4_ = bf16[512,256]{1,0:T(8,128)(2,1)S(1)} collective-permute-done((bf16[512,256]{1,0:T(8,128)(2,1)S(1)}, bf16[512,256]{1,0:T(8,128)(2,1)S(1)}, u32[]{:S(2)}, u32[]{:S(2)}) %collective-permute-start.4) | collective-permute-done | bytes 262176 | tf_op jit(solution)/shard_map/ppermute | solution.py:461
  60.3 0.2 collective-permute-done.3.refs_3_
  60.6 4.9 %all-to-all-done.1.back_ref = bf16[32,36,256]{2,1,0:T(8,128)(2,1)S(1)} async-done(((bf16[32,36,256]{2,1,0:T(8,128)(2,1)}), bf16[32,36,256]{2,1,0:T(8,128)(2,1)S(1)}, u32[]{:S(2)}, u32[]{:S(2)}) %all-to-all-start.1) | async-done | bytes 589856 | tf_op jit(solution)/shard_map/all_to_all | solution.py:472
  65.6 0.7 broadcast_in_dim.14
  66.3 5.0 %all-to-all-start.2 = ((bf16[32,16,256]{2,1,0:T(8,128)(2,1)}), bf16[32,16,256]{2,1,0:T(8,128)(2,1)S(1)}, u32[]{:S(2)}, u32[]{:S(2)}) async-start(bf16[32,16,256]{2,1,0:T(8,128)(2,1)} %broadcast_in_dim.14), calls=%async_computation.2 | async-start | bytes 524288 | tf_op jit(solution)/shard_map/all_to_all | solution.py:472
  71.5 0.7 convert_add_fusion
  72.2 0.4 collective-permute-done.10
  72.6 0.4 collective-permute-start.13
  73.1 1.6 %collective-permute-start.12 = (bf16[20,256]{1,0:T(8,128)(2,1)S(1)}, bf16[20,256]{1,0:T(8,128)(2,1)S(1)}, u32[]{:S(2)}, u32[]{:S(2)}) collective-permute-start(bf16[20,256]{1,0:T(8,128)(2,1)S(1)} %add_convert_fusion.1), channel_id=1, source_target_pairs={{0,64},{32,96},{64,128},{96,160},{128,192},{160,224},{192,0},{224,... | collective-permute-start | bytes 30728 | tf_op jit(solution)/shard_map/ppermute | solution.py:461
  74.6 9.9 %all-to-all-done.2.d_ref = bf16[32,16,256]{2,1,0:T(8,128)(2,1)S(1)} async-done(((bf16[32,16,256]{2,1,0:T(8,128)(2,1)}), bf16[32,16,256]{2,1,0:T(8,128)(2,1)S(1)}, u32[]{:S(2)}, u32[]{:S(2)}) %all-to-all-start.2) | async-done | bytes 262176 | tf_op jit(solution)/shard_map/all_to_all | solution.py:472
  84.5 2.0 %collective-permute-start.2 = (bf16[512,256]{1,0:T(8,128)(2,1)S(1)}, bf16[512,256]{1,0:T(8,128)(2,1)S(1)}, u32[]{:S(2)}, u32[]{:S(2)}) collective-permute-start(bf16[512,256]{1,0:T(8,128)(2,1)S(1)} %bitcast.18), channel_id=1, source_target_pairs={{0,128},{32,160},{64,192},{96,224},{128,0},{160,32},{192,64},{224,... | collective-permute-start | bytes 786440 | tf_op jit(solution)/shard_map/ppermute | solution.py:461
  86.6 1.3 collective-permute-start.1
  87.9 0.7 collective-permute-start
  88.6 9.7 %dense_own.1 = (f32[4096,256]{1,0:T(8,128)}, f32[128,4096]{1,0:T(8,128)}) custom-call(bf16[32,16,256]{2,1,0:T(8,128)(2,1)S(1)} %all-to-all-done.2.d_ref, bf16[32,32,128]{2,1,0:T(8,128)(2,1)S(1)} %all-to-all-done.feats_ref.refs_3_, bf16[4096,128]{1,0:T(8,128)(2,1)} %multiply_bitcast_fusion.win_ref.refs_6_, bf16[4096,256]{1,0:T(8,128)(2,1)} %refs_7_.3), custom_call_target="tpu_custom_call" | custom-call | flops 3221225472 | bytes 10485760 | tf_op jit(solution)/shard_map/dense_own/pallas_call | solution.py:290
  98.3 2.8 %collective-permute-start.11 = (bf16[20,256]{1,0:T(8,128)(2,1)S(1)}, bf16[20,256]{1,0:T(8,128)(2,1)S(1)}, u32[]{:S(2)}, u32[]{:S(2)}) collective-permute-start(bf16[20,256]{1,0:T(8,128)(2,1)S(1)} %add_convert_fusion.1), channel_id=1, source_target_pairs={{0,128},{32,160},{64,192},{96,224},{128,0},{160,32},{192,64},{224,... | collective-permute-start | bytes 30728 | tf_op jit(solution)/shard_map/ppermute | solution.py:461
  101.1 0.7 copy-done.9
  101.9 11.0 %dense_far.3 = (bf16[2048,256]{1,0:T(8,128)(2,1)S(1)}, bf16[128,2048]{1,0:T(8,128)(2,1)S(1)}) custom-call(bf16[512,256]{1,0:T(8,128)(2,1)} %copy-done.10, bf16[512,256]{1,0:T(8,128)(2,1)} %copy-done.9, bf16[512,256]{1,0:T(8,128)(2,1)} %copy-done.8, bf16[512,256]{1,0:T(8,128)(2,1)} %copy-done.6, bf16[512,256]{1,0:T(8,128)(2,1)} %copy-done.5, ...), custom_call_target="tpu_custom_call" | custom-call | flops 4831838208 | bytes 10485760 | tf_op jit(solution)/shard_map/dense_far/pallas_call | solution.py:339
  112.9 0.8 copy-done
  113.7 11.1 %dense_far.2 = (bf16[2048,256]{1,0:T(8,128)(2,1)S(1)}, bf16[128,2048]{1,0:T(8,128)(2,1)S(1)}) custom-call(bf16[512,256]{1,0:T(8,128)(2,1)} %copy-done.10, bf16[512,256]{1,0:T(8,128)(2,1)} %copy-done.9, bf16[512,256]{1,0:T(8,128)(2,1)} %copy-done.8, bf16[512,256]{1,0:T(8,128)(2,1)} %copy-done.6, bf16[512,256]{1,0:T(8,128)(2,1)} %copy-done.5, ...), custom_call_target="tpu_custom_call" | custom-call | flops 4831838208 | bytes 10485760 | tf_op jit(solution)/shard_map/dense_far/pallas_call | solution.py:339
  124.8 0.6 collective-permute-start.6
  125.4 0.6 copy-done.7
  126.0 0.7 broadcast_in_dim.15
  126.8 3.9 %all-to-all-start.3 = ((bf16[32,16,256]{2,1,0:T(8,128)(2,1)}), bf16[32,16,256]{2,1,0:T(8,128)(2,1)S(1)}, u32[]{:S(2)}, u32[]{:S(2)}) async-start(bf16[32,16,256]{2,1,0:T(8,128)(2,1)} %broadcast_in_dim.15), calls=%async_computation.3 | async-start | bytes 524288 | tf_op jit(solution)/shard_map/all_to_all | solution.py:472
  130.7 0.7 fusion
  131.4 0.5 collective-permute-start.7
  131.9 0.7 slice_bitcast_fusion
  132.5 0.6 copy.25
  133.1 11.0 %all-to-all-done.3 = bf16[32,16,256]{2,1,0:T(8,128)(2,1)S(1)} async-done(((bf16[32,16,256]{2,1,0:T(8,128)(2,1)}), bf16[32,16,256]{2,1,0:T(8,128)(2,1)S(1)}, u32[]{:S(2)}, u32[]{:S(2)}) %all-to-all-start.3) | async-done | bytes 262176 | tf_op jit(solution)/shard_map/all_to_all | solution.py:472
  144.2 0.9 pad_maximum_fusion
  145.0 0.2 copy-done.1
  145.2 3.9 %finish.2 = (f32[4096,256]{1,0:T(8,128)}, f32[128,4096]{1,0:T(8,128)}) custom-call(bf16[2048,256]{1,0:T(8,128)(2,1)S(1)} %get-tuple-element.31.refs_0_, bf16[2048,256]{1,0:T(8,128)(2,1)} %collective-permute-done.8.refs_1_, bf16[128,2048]{1,0:T(8,128)(2,1)S(1)} %copy-done.1, bf16[128,2048]{1,0:T(8,128)(2,1)} %collective-permute-done.9.refs_3_), custom_call_target="tpu_custom_call" | custom-call | tf_op jit(solution)/shard_map/finish/pallas_call | solution.py:383
  149.1 3.8 %finish.3 = (f32[4096,256]{1,0:T(8,128)}, f32[128,4096]{1,0:T(8,128)}) custom-call(bf16[2048,256]{1,0:T(8,128)(2,1)S(1)} %get-tuple-element.29.refs_0_, bf16[2048,256]{1,0:T(8,128)(2,1)} %collective-permute-done.6.refs_1_, bf16[128,2048]{1,0:T(8,128)(2,1)S(1)} %get-tuple-element.30.refs_2_, ...), custom_call_target="tpu_custom_call", output_to_operand_aliasing={{0}: (4, {}), {1}: (5, {})} | custom-call | tf_op jit(solution)/shard_map/finish/pallas_call | solution.py:383
  (41 shorter events, 0.7 us)
Async XLA Ops:
  2.3 24.1 %all-to-all-start = ((bf16[32,32,128]{2,1,0:T(8,128)(2,1)}), bf16[32,32,128]{2,1,0:T(8,128)(2,1)S(1)}, u32[]{:S(2)}, u32[]{:S(2)}) async-start(bf16[32,32,128]{2,1,0:T(8,128)(2,1)} %pack.1), calls=%async_computation | async-start | bytes 524288 | tf_op jit(solution)/shard_map/all_to_all | solution.py:472
  17.0 4.1 %copy-start.3 = (bf16[256,256]{1,0:T(8,128)(2,1)S(1)}, bf16[256,256]{1,0:T(8,128)(2,1)}, u32[]{:S(2)}) copy-start(bf16[256,256]{1,0:T(8,128)(2,1)} %table_ref.1) | copy-start | bytes 393220
  26.5 7.1 %copy-start.2 = (bf16[256,512]{1,0:T(8,128)(2,1)S(1)}, bf16[256,512]{1,0:T(8,128)(2,1)}, u32[]{:S(2)}) copy-start(bf16[256,512]{1,0:T(8,128)(2,1)} %refs_4_.1) | copy-start | bytes 786436
  39.6 25.9 %all-to-all-start.1 = ((bf16[32,36,256]{2,1,0:T(8,128)(2,1)}), bf16[32,36,256]{2,1,0:T(8,128)(2,1)S(1)}, u32[]{:S(2)}, u32[]{:S(2)}) async-start(bf16[32,36,256]{2,1,0:T(8,128)(2,1)} %get-tuple-element.24), calls=%async_computation.1 | async-start | bytes 1310720 | tf_op jit(solution)/shard_map/all_to_all | solution.py:472
  45.9 10.8 %collective-permute-start.5 = (bf16[512,256]{1,0:T(8,128)(2,1)S(1)}, bf16[512,256]{1,0:T(8,128)(2,1)S(1)}, u32[]{:S(2)}, u32[]{:S(2)}) collective-permute-start(bf16[512,256]{1,0:T(8,128)(2,1)S(1)} %get-tuple-element.26), channel_id=1, source_target_pairs={{0,128},{32,160},{64,192},{96,224},{128,0},{160,32},{192,64},{224,... | collective-permute-start | bytes 786440 | tf_op jit(solution)/shard_map/ppermute | solution.py:461
  48.2 12.0 %collective-permute-start.4 = (bf16[512,256]{1,0:T(8,128)(2,1)S(1)}, bf16[512,256]{1,0:T(8,128)(2,1)S(1)}, u32[]{:S(2)}, u32[]{:S(2)}) collective-permute-start(bf16[512,256]{1,0:T(8,128)(2,1)S(1)} %get-tuple-element.26), channel_id=1, source_target_pairs={{0,192},{32,224},{64,0},{96,32},{128,64},{160,96},{192,128},{224,1... | collective-permute-start | bytes 786440 | tf_op jit(solution)/shard_map/ppermute | solution.py:461
  49.6 10.9 %collective-permute-start.3 = (bf16[512,256]{1,0:T(8,128)(2,1)S(1)}, bf16[512,256]{1,0:T(8,128)(2,1)S(1)}, u32[]{:S(2)}, u32[]{:S(2)}) collective-permute-start(bf16[512,256]{1,0:T(8,128)(2,1)S(1)} %get-tuple-element.26), channel_id=1, source_target_pairs={{0,64},{32,96},{64,128},{96,160},{128,192},{160,224},{192,0},{224,... | collective-permute-start | bytes 786440 | tf_op jit(solution)/shard_map/ppermute | solution.py:461
  56.7 41.6 %copy-start.4 = (bf16[512,256]{1,0:T(8,128)(2,1)}, bf16[512,256]{1,0:T(8,128)(2,1)S(1)}, u32[]{:S(2)}) copy-start(bf16[512,256]{1,0:T(8,128)(2,1)S(1)} %collective-permute-done.5.refs_5_) | copy-start | bytes 786436
  60.3 38.0 %copy-start.5 = (bf16[512,256]{1,0:T(8,128)(2,1)}, bf16[512,256]{1,0:T(8,128)(2,1)S(1)}, u32[]{:S(2)}) copy-start(bf16[512,256]{1,0:T(8,128)(2,1)S(1)} %collective-permute-done.4.refs_4_) | copy-start | bytes 786436
  60.5 37.8 %copy-start.6 = (bf16[512,256]{1,0:T(8,128)(2,1)}, bf16[512,256]{1,0:T(8,128)(2,1)S(1)}, u32[]{:S(2)}) copy-start(bf16[512,256]{1,0:T(8,128)(2,1)S(1)} %collective-permute-done.3.refs_3_) | copy-start | bytes 786436
  60.5 10.9 %collective-permute-start.14 = (bf16[256,256]{1,0:T(8,128)(2,1)S(1)}, bf16[256,256]{1,0:T(8,128)(2,1)S(1)}, u32[]{:S(2)}, u32[]{:S(2)}) collective-permute-start(bf16[256,256]{1,0:T(8,128)(2,1)S(1)} %add_convert_fusion), channel_id=1, source_target_pairs={{0,32},{32,0},{64,96},{96,64},{128,160},{160,128},{192,224},{224,1... | collective-permute-start | bytes 393224 | tf_op jit(solution)/shard_map/ppermute | solution.py:464
  66.3 18.2 %all-to-all-start.2 = ((bf16[32,16,256]{2,1,0:T(8,128)(2,1)}), bf16[32,16,256]{2,1,0:T(8,128)(2,1)S(1)}, u32[]{:S(2)}, u32[]{:S(2)}) async-start(bf16[32,16,256]{2,1,0:T(8,128)(2,1)} %broadcast_in_dim.14), calls=%async_computation.2 | async-start | bytes 524288 | tf_op jit(solution)/shard_map/all_to_all | solution.py:472
  71.3 1.3 collective-permute-start.10
  72.6 52.8 %collective-permute-start.13 = (bf16[20,256]{1,0:T(8,128)(2,1)S(1)}, bf16[20,256]{1,0:T(8,128)(2,1)S(1)}, u32[]{:S(2)}, u32[]{:S(2)}) collective-permute-start(bf16[20,256]{1,0:T(8,128)(2,1)S(1)} %add_convert_fusion.1), channel_id=1, source_target_pairs={{0,192},{32,224},{64,0},{96,32},{128,64},{160,96},{192,128},{224,1... | collective-permute-start | bytes 30728 | tf_op jit(solution)/shard_map/ppermute | solution.py:461
  73.1 52.3 %collective-permute-start.12 = (bf16[20,256]{1,0:T(8,128)(2,1)S(1)}, bf16[20,256]{1,0:T(8,128)(2,1)S(1)}, u32[]{:S(2)}, u32[]{:S(2)}) collective-permute-start(bf16[20,256]{1,0:T(8,128)(2,1)S(1)} %add_convert_fusion.1), channel_id=1, source_target_pairs={{0,64},{32,96},{64,128},{96,160},{128,192},{160,224},{192,0},{224,... | collective-permute-start | bytes 30728 | tf_op jit(solution)/shard_map/ppermute | solution.py:461
  84.5 13.7 %collective-permute-start.2 = (bf16[512,256]{1,0:T(8,128)(2,1)S(1)}, bf16[512,256]{1,0:T(8,128)(2,1)S(1)}, u32[]{:S(2)}, u32[]{:S(2)}) collective-permute-start(bf16[512,256]{1,0:T(8,128)(2,1)S(1)} %bitcast.18), channel_id=1, source_target_pairs={{0,128},{32,160},{64,192},{96,224},{128,0},{160,32},{192,64},{224,... | collective-permute-start | bytes 786440 | tf_op jit(solution)/shard_map/ppermute | solution.py:461
  86.6 14.5 %collective-permute-start.1 = (bf16[512,256]{1,0:T(8,128)(2,1)S(1)}, bf16[512,256]{1,0:T(8,128)(2,1)S(1)}, u32[]{:S(2)}, u32[]{:S(2)}) collective-permute-start(bf16[512,256]{1,0:T(8,128)(2,1)S(1)} %bitcast.19), channel_id=1, source_target_pairs={{0,192},{32,224},{64,0},{96,32},{128,64},{160,96},{192,128},{224,1... | collective-permute-start | bytes 786440 | tf_op jit(solution)/shard_map/ppermute | solution.py:461
  87.9 13.2 %collective-permute-start = (bf16[512,256]{1,0:T(8,128)(2,1)S(1)}, bf16[512,256]{1,0:T(8,128)(2,1)S(1)}, u32[]{:S(2)}, u32[]{:S(2)}) collective-permute-start(bf16[512,256]{1,0:T(8,128)(2,1)S(1)} %bitcast.20), channel_id=1, source_target_pairs={{0,64},{32,96},{64,128},{96,160},{128,192},{160,224},{192,0},{224,... | collective-permute-start | bytes 786440 | tf_op jit(solution)/shard_map/ppermute | solution.py:461
  98.3 2.8 %copy-start.8 = (bf16[512,256]{1,0:T(8,128)(2,1)}, bf16[512,256]{1,0:T(8,128)(2,1)S(1)}, u32[]{:S(2)}) copy-start(bf16[512,256]{1,0:T(8,128)(2,1)S(1)} %collective-permute-done.2.refs_2_) | copy-start | bytes 786436
  98.3 27.1 %collective-permute-start.11 = (bf16[20,256]{1,0:T(8,128)(2,1)S(1)}, bf16[20,256]{1,0:T(8,128)(2,1)S(1)}, u32[]{:S(2)}, u32[]{:S(2)}) collective-permute-start(bf16[20,256]{1,0:T(8,128)(2,1)S(1)} %add_convert_fusion.1), channel_id=1, source_target_pairs={{0,128},{32,160},{64,192},{96,224},{128,0},{160,32},{192,64},{224,... | collective-permute-start | bytes 30728 | tf_op jit(solution)/shard_map/ppermute | solution.py:461
  101.1 0.7 copy-start.9
  101.1 0.8 copy-start.10
  112.9 0.8 copy-start
  113.7 31.3 %collective-permute-start.8 = (bf16[2048,256]{1,0:T(8,128)(2,1)S(1)}, bf16[2048,256]{1,0:T(8,128)(2,1)}, u32[]{:S(2)}, u32[]{:S(2)}) collective-permute-start(bf16[2048,256]{1,0:T(8,128)(2,1)S(1)} %get-tuple-element.31.refs_0_), channel_id=1, source_target_pairs={{0,32},{32,0},{64,96},{96,64},{128,160},{160,128},{192,224},{224,1... | collective-permute-start | bytes 3145736 | tf_op jit(solution)/shard_map/ppermute | solution.py:464
  124.8 24.2 %collective-permute-start.6 = (bf16[2048,256]{1,0:T(8,128)(2,1)S(1)}, bf16[2048,256]{1,0:T(8,128)(2,1)}, u32[]{:S(2)}, u32[]{:S(2)}) collective-permute-start(bf16[2048,256]{1,0:T(8,128)(2,1)S(1)} %get-tuple-element.29.refs_0_), channel_id=1, source_target_pairs={{0,32},{32,0},{64,96},{96,64},{128,160},{160,128},{192,224},{224,1... | collective-permute-start | bytes 3145736 | tf_op jit(solution)/shard_map/ppermute | solution.py:464
  125.4 0.6 copy-start.7
  126.8 17.3 %all-to-all-start.3 = ((bf16[32,16,256]{2,1,0:T(8,128)(2,1)}), bf16[32,16,256]{2,1,0:T(8,128)(2,1)S(1)}, u32[]{:S(2)}, u32[]{:S(2)}) async-start(bf16[32,16,256]{2,1,0:T(8,128)(2,1)} %broadcast_in_dim.15), calls=%async_computation.3 | async-start | bytes 524288 | tf_op jit(solution)/shard_map/all_to_all | solution.py:472
  131.3 13.7 %collective-permute-start.9 = (bf16[128,2048]{1,0:T(8,128)(2,1)}, bf16[128,2048]{1,0:T(8,128)(2,1)}, u32[]{:S(2)}, u32[]{:S(2)}) collective-permute-start(bf16[128,2048]{1,0:T(8,128)(2,1)} %copy-done), channel_id=1, source_target_pairs={{0,32},{32,0},{64,96},{96,64},{128,160},{160,128},{192,224},{224,1... | collective-permute-start | bytes 1572872 | tf_op jit(solution)/shard_map/ppermute | solution.py:464
  131.4 17.7 %collective-permute-start.7 = (bf16[128,2048]{1,0:T(8,128)(2,1)S(1)}, bf16[128,2048]{1,0:T(8,128)(2,1)S(1)}, u32[]{:S(2)}, u32[]{:S(2)}) collective-permute-start(bf16[128,2048]{1,0:T(8,128)(2,1)S(1)} %get-tuple-element.30.refs_2_), channel_id=1, source_target_pairs={{0,32},{32,0},{64,96},{96,64},{128,160},{160,128},{192,224},{224,1... | collective-permute-start | bytes 1572872 | tf_op jit(solution)/shard_map/ppermute | solution.py:464
  144.1 1.1 copy-start.1
where the time goes:
time: 154 us; the launch traced here: 153 us
  Pallas kernels  55 us (36%)
  starting transfers between devices  41 us (27%)
  waiting for transfers between devices  39.9 us (26%)
  local copies, waits for them, and re-layouts  12.6 us (8%)
  other arithmetic  3.45 us (2%)
    all_to_all x4, waiting for transfers between devices, exchange(): return lax.all_to_all(x, 'tbl', split_axis=0, concat_axis=0, tiled=True)  29.3 us
    all_to_all x4, starting transfers between devices, exchange(): return lax.all_to_all(x, 'tbl', split_axis=0, concat_axis=0, tiled=True)  26.4 us
    pallas_call x2, Pallas kernels, dense_far(): pl.pallas_call(lambda *refs: far_kernel(count, *refs), grid=(units // blo...  22.1 us
    ppermute x9, starting transfers between devices, from_chips(): return [lax.ppermute(x, 'grp', ring(turn, 0)) for turn in (1, chips - 1, 2)]  13.3 us
    ppermute x9, waiting for transfers between devices, from_chips(): return [lax.ppermute(x, 'grp', ring(turn, 0)) for turn in (1, chips - 1, 2)]  10.2 us
    pallas_call x1, Pallas kernels, dense_own(): pl.pallas_call(own_kernel, grid=(wide // block,), in_specs=[feats_spec(d,...  9.65 us
    unnamed x26, local copies, waits for them, and re-layouts  9.36 us
    pallas_call x2, Pallas kernels, finish(): pl.pallas_call(finish_kernel, grid=(units // block,), in_specs=[spec_o, s...  7.65 us
  transfers between devices with their start and end apart: 19, of which 8 were waited for; matrix products, arithmetic and copies ran while one was open for 9% of the time, Pallas kernels for 24%

commit v1 on v0

--- a/solution.py
+++ b/solution.py
@@ -18,10 +18,6 @@
 
 def mm_nt(a, b):
     return lax.dot_general(a, b, (((1,), (1,)), ((), ())), preferred_element_type=F32)
-
-
-def slope_of(value, sig):
-    return sig * (1.0 + value * (1.0 - sig))
 
 
 def pool_kernel(ids_ref, table_ref, items_ref, counts_ref):
@@ -76,8 +72,8 @@
 
 def users_kernel(feats_ref, win_ref, wout_ref, users_ref, acc):
     step = pl.program_id(0)
-    half = mm_nt(win_ref[...], flat(feats_ref))
-    part = mm(wout_ref[...], (half * jnp.tanh(half) + half).astype(BF))
+    half = mm(flat(feats_ref) * jnp.asarray(0.5, BF), win_ref[...])
+    part = mm((half * jnp.tanh(half) + half).astype(BF), wout_ref[...])
 
     @pl.when(step == 0)
     def _():
@@ -89,37 +85,37 @@
 
     @pl.when(step == pl.num_programs(0) - 1)
     def _():
-        users_ref[...] = acc[...].astype(BF)
-
-
-def user_vectors(feats, win_t, wout_t, each):
-    width, wide = wout_t.shape
-    uf = win_t.shape[1]
+        users_ref[...] = acc[...].T.astype(BF)
+
+
+def user_vectors(feats, tower_in, tower_out, each):
+    wide, width = tower_out.shape
+    uf = tower_in.shape[0]
     reqs = feats.shape[0] * each
-    block = 512
+    block = 2048
     return pl.pallas_call(
         users_kernel,
         grid=(wide // block,),
         in_specs=[
             feats_spec(feats, each, uf),
-            pl.BlockSpec((block, uf), lambda i: (i, 0)),
-            pl.BlockSpec((width, block), lambda i: (0, i)),
+            pl.BlockSpec((uf, block), lambda i: (0, i)),
+            pl.BlockSpec((block, width), lambda i: (i, 0)),
         ],
         out_specs=pl.BlockSpec((width, reqs), lambda i: (0, 0)),
         out_shape=jax.ShapeDtypeStruct((width, reqs), BF),
-        scratch_shapes=[pltpu.VMEM((width, reqs), F32)],
-        compiler_params=pltpu.CompilerParams(vmem_limit_bytes=12 << 20),
+        scratch_shapes=[pltpu.VMEM((reqs, width), F32)],
+        compiler_params=pltpu.CompilerParams(vmem_limit_bytes=16 << 20),
         cost_estimate=pl.CostEstimate(
             flops=2 * reqs * wide * (uf + width),
             bytes_accessed=4 << 20,
             transcendentals=reqs * wide,
         ),
         name="users",
-    )(feats, hbm(win_t), hbm(wout_t))
-
-
-def hidden_of(feats, half_win):
-    half = mm_nt(half_win, feats)
+    )(feats, hbm(tower_in), hbm(tower_out))
+
+
+def hidden_of(feats, win):
+    half = mm_nt(win, feats * jnp.asarray(0.5, BF))
     turn = jnp.tanh(half)
     hid = half * turn + half
     rest = 0.5 - 0.5 * turn
@@ -135,7 +131,7 @@
     width, _ = iw_ref.shape
     step_c = 256
     iw = iw_ref[...]
-    iw_t = iw.astype(F32).T.astype(BF)
+    iw_t = (iw.astype(F32) * 0.5).T.astype(BF)
     weight = w_ref[...]
     users = users_ref[...]
     shards, _, uf = came_ref.shape
@@ -170,9 +166,10 @@
         chosen = mm(users, pick)
         item = items_ref[:, cut].astype(F32)
         cross = (item * chosen).astype(BF)
-        inner = mm(iw_t, cross)
-        sig = sigmoid(inner)
-        act = inner * sig
+        half = mm(iw_t, cross)
+        turn = jnp.tanh(half)
+        act = half * turn + half
+        rest = 0.5 - 0.5 * turn
         score = jnp.sum(act * weight, axis=0, keepdims=True)
         s_hi = score.astype(BF).astype(F32)
         s_mid = (score - s_hi).astype(BF).astype(F32)
@@ -181,7 +178,7 @@
             row_out = row_out + mm(jnp.where(mine, v, 0.0).astype(BF), gather[n])
         acc_s[k * near : (k + 1) * near, :] = row_out
         grad = jnp.where(slot.astype(F32) < live, sigmoid(score) - target, 0.0) * factor
-        dz = (grad * weight * slope_of(inner, sig)).astype(BF)
+        dz = (grad * weight * ((1.0 - rest) + act * rest)).astype(BF)
         dcross = mm(iw, dz)
         d_item = (dcross * chosen).astype(BF)
         d_user = (dcross * item).astype(BF)
@@ -286,7 +283,7 @@
     wide, width = tower_out.shape
     uf = win_t.shape[1]
     reqs = each * feats.shape[0]
-    block = 512
+    block = 1024
     return pl.pallas_call(
         own_kernel,
         grid=(wide // block,),
@@ -301,7 +298,7 @@
             pl.BlockSpec((uf, block), lambda i: (0, i)),
         ),
         out_shape=(pltpu.HBM((wide, width), F32), pltpu.HBM((uf, wide), F32)),
-        compiler_params=pltpu.CompilerParams(vmem_limit_bytes=14 << 20),
+        compiler_params=pltpu.CompilerParams(vmem_limit_bytes=28 << 20),
         cost_estimate=pl.CostEstimate(
             flops=2 * reqs * wide * (2 * width + 2 * uf),
             bytes_accessed=10 << 20,
@@ -316,15 +313,16 @@
     win_ref, wout_ref, old_out, old_in, gout_ref, gin_ref = refs[2 * count :]
     wout = wout_ref[...]
     win = win_ref[...]
-    out, back = old_out[...], None
+    d_all = jnp.concatenate([x[...] for x in d], axis=0)
+    feats_all = jnp.concatenate([flat(x) for x in feats], axis=0)
+    reqs = d[0].shape[0]
+    hids, pres = [], []
     for k in range(count):
-        d_k = d[k][...]
-        feats_k = flat(feats[k])
-        hid, slope = hidden_of(feats_k, win)
-        out = out + mm(hid, d_k)
-        d_pre = (mm_nt(wout, d_k) * slope).astype(BF)
-        turn = mm(d_pre, feats_k)
-        back = turn if back is None else back + turn
+        hid, slope = hidden_of(feats_all[k * reqs : (k + 1) * reqs], win)
+        hids.append(hid)
+        pres.append((mm_nt(wout, d_all[k * reqs : (k + 1) * reqs]) * slope).astype(BF))
+    out = old_out[...] + mm(jnp.concatenate(hids, axis=1), d_all)
+    back = mm(jnp.concatenate(pres, axis=1), feats_all)
     gout_ref[...] = out.astype(BF)
     gin_ref[...] = (back.T + old_in[...]).astype(BF)
 
@@ -355,7 +353,7 @@
             jax.ShapeDtypeStruct((units, width), BF),
             jax.ShapeDtypeStruct((uf, units), BF),
         ),
-        compiler_params=pltpu.CompilerParams(vmem_limit_bytes=20 << 20),
+        compiler_params=pltpu.CompilerParams(vmem_limit_bytes=36 << 20),
         cost_estimate=pl.CostEstimate(
             flops=2 * count * reqs * units * (2 * width + 2 * uf),
             bytes_accessed=10 << 20,
@@ -474,9 +472,8 @@
     arrived = exchange(pack(user_feats, req_of[0], labels[0], live))
     ids_rows = jnp.transpose(ids[0], (1, 0, 2)).reshape(ids.shape[2], shards * slots)
     items, counts = pool(ids_rows, table)
-    win_t = tower_in.T * jnp.asarray(0.5, BF)
-    wout_t = tower_out.T
-    users = user_vectors(arrived, win_t, wout_t, each)
+    win_t = tower_in.T
+    users = user_vectors(arrived, tower_in, tower_out, each)
     factor = 1.0 / math.sqrt(groups * shards * shards * slots)
     sent, share = rank(
         factor, slots, users, items, counts, arrived, inter_weight, out_weight[:, None]

time: 154 us -> 145 us (0.942)
  Pallas kernels: 55 us -> 48.3 us
  waiting for transfers between devices: 39.9 us -> 44.2 us
  local copies, waits for them, and re-layouts: 12.6 us -> 8.84 us
  starting transfers between devices: 41 us -> 39.1 us
    all_to_all x4, waiting for transfers between devices: 29.3 us -> 33.9 us  [exchange(): return lax.all_to_all(x, 'tbl', split_axis=0, concat_axis=0, tiled=True)]
    unnamed x26 -> x27, local copies, waits for them, and re-layouts: 9.36 us -> 5.59 us
    pallas_call x1, Pallas kernels: 7.09 us -> 4.37 us  [user_vectors(): pl.pallas_call(users_kernel, grid=(wide // block,), in_specs=[feats_spec(...]
    all_to_all x4, starting transfers between devices: 26.4 us -> 24.4 us  [exchange(): return lax.all_to_all(x, 'tbl', split_axis=0, concat_axis=0, tiled=True)]
    pallas_call x2, Pallas kernels: 22.1 us -> 20.1 us  [dense_far(): pl.pallas_call(lambda *refs: far_kernel(count, *refs), grid=(units // blo...]
    pallas_call x1, Pallas kernels: 9.65 us -> 7.77 us  [dense_own(): pl.pallas_call(own_kernel, grid=(wide // block,), in_specs=[feats_spec(d,...]
  transfers between devices with their start and end apart: 19 -> 19, of which waited for: 8 -> 8; matrix products, arithmetic and copies ran while one was open for 9% -> 6% of each run, Pallas kernels for 24% -> 23%
where the time goes in v1:
time: 145 us; the launch traced here: 144 us
  Pallas kernels  48.3 us (33%)
  waiting for transfers between devices  44.2 us (30%)
  starting transfers between devices  39.1 us (27%)
  local copies, waits for them, and re-layouts  8.84 us (6%)
  other arithmetic  2.38 us (2%)
    all_to_all x4, waiting for transfers between devices, exchange(): return lax.all_to_all(x, 'tbl', split_axis=0, concat_axis=0, tiled=True)  33.9 us
    all_to_all x4, starting transfers between devices, exchange(): return lax.all_to_all(x, 'tbl', split_axis=0, concat_axis=0, tiled=True)  24.4 us
    pallas_call x2, Pallas kernels, dense_far(): pl.pallas_call(lambda *refs: far_kernel(count, *refs), grid=(units // blo...  20.1 us
    ppermute x9, starting transfers between devices, from_chips(): return [lax.ppermute(x, 'grp', ring(turn, 0)) for turn in (1, chips - 1, 2)]  13.3 us
    ppermute x9, waiting for transfers between devices, from_chips(): return [lax.ppermute(x, 'grp', ring(turn, 0)) for turn in (1, chips - 1, 2)]  9.97 us
    pallas_call x1, Pallas kernels, dense_own(): pl.pallas_call(own_kernel, grid=(wide // block,), in_specs=[feats_spec(d,...  7.77 us
    pallas_call x2, Pallas kernels, finish(): pl.pallas_call(finish_kernel, grid=(units // block,), in_specs=[spec_o, s...  7.65 us
    pallas_call x1, Pallas kernels, rank(): pl.pallas_call(lambda *refs: rank_kernel(factor, slots, *refs), out_shape...  5.93 us
  transfers between devices with their start and end apart: 19, of which 8 were waited for; matrix products, arithmetic and copies ran while one was open for 6% of the time, Pallas kernels for 23%

profile of v1, /device:TPU:8, one launch (start us, length us, event | category | flops | bytes accessed | tf_op | source)
XLA Modules:
  0.0 143.7 jit_solution(1923310306194271285)
XLA Ops:
  0.6 1.7 %pack.1 = bf16[32,32,128]{2,1,0:T(8,128)(2,1)} custom-call(bf16[16,128]{1,0:T(8,128)(2,1)} %feats_ref.1, s32[32,32]{1,0:T(8,128)} %bitcast.26, f32[32,32]{1,0:T(8,128)} %bitcast.27, s32[1,32]{1,0:T(1,128)} %live_ref.1), custom_call_target="tpu_custom_call" | custom-call | tf_op jit(solution)/shard_map/pack/pallas_call | solution.py:432
  2.3 11.3 %all-to-all-start = ((bf16[32,32,128]{2,1,0:T(8,128)(2,1)}), bf16[32,32,128]{2,1,0:T(8,128)(2,1)S(1)}, u32[]{:S(2)}, u32[]{:S(2)}) async-start(bf16[32,32,128]{2,1,0:T(8,128)(2,1)} %pack.1), calls=%async_computation | async-start | bytes 524288 | tf_op jit(solution)/shard_map/all_to_all | solution.py:470
  13.6 0.8 copy.20
  14.6 0.8 copy.21.refs_5_
  15.4 0.9 copy-done.3
  16.3 0.7 pool.1
  17.0 9.4 %all-to-all-done.feats_ref.refs_3_ = bf16[32,32,128]{2,1,0:T(8,128)(2,1)S(1)} async-done(((bf16[32,32,128]{2,1,0:T(8,128)(2,1)}), bf16[32,32,128]{2,1,0:T(8,128)(2,1)S(1)}, u32[]{:S(2)}, u32[]{:S(2)}) %all-to-all-start) | async-done | bytes 262176 | tf_op jit(solution)/shard_map/all_to_all | solution.py:470
  26.5 4.4 %users.1.refs_0_ = bf16[256,512]{1,0:T(8,128)(2,1)S(1)} custom-call(bf16[32,32,128]{2,1,0:T(8,128)(2,1)S(1)} %all-to-all-done.feats_ref.refs_3_, bf16[128,4096]{1,0:T(8,128)(2,1)} %win_ref.1, bf16[4096,256]{1,0:T(8,128)(2,1)} %refs_7_.3), custom_call_target="tpu_custom_call" | custom-call | flops 1610612736 | bytes 4194304 | tf_op jit(solution)/shard_map/users/pallas_call | solution.py:96
  30.8 5.9 %rank.1 = (bf16[32,36,256]{2,1,0:T(8,128)(2,1)}, bf16[512,256]{1,0:T(8,128)(2,1)S(1)}) custom-call(bf16[256,512]{1,0:T(8,128)(2,1)S(1)} %users.1.refs_0_, bf16[256,1024]{1,0:T(8,128)(2,1)S(1)} %get-tuple-element.22.refs_1_, bf16[256,1024]{1,0:T(8,128)(2,1)S(1)} %get-tuple-element.23.refs_2_, bf16[32,32,128]{2,1,0:T(8,128)(2,1)S(1)} %all-to-all-done.feats_ref.refs_3_, ...), custom_call_target="tpu_custom_call" | custom-call | flops 1476395008 | bytes 4194304 | tf_op jit(solution)/shard_map/rank/pallas_call | solution.py:228
  36.8 4.1 %all-to-all-start.1 = ((bf16[32,36,256]{2,1,0:T(8,128)(2,1)}), bf16[32,36,256]{2,1,0:T(8,128)(2,1)S(1)}, u32[]{:S(2)}, u32[]{:S(2)}) async-start(bf16[32,36,256]{2,1,0:T(8,128)(2,1)} %get-tuple-element.24), calls=%async_computation.1 | async-start | bytes 1310720 | tf_op jit(solution)/shard_map/all_to_all | solution.py:470
  40.9 2.4 %collective-permute-start.5 = (bf16[512,256]{1,0:T(8,128)(2,1)S(1)}, bf16[512,256]{1,0:T(8,128)(2,1)S(1)}, u32[]{:S(2)}, u32[]{:S(2)}) collective-permute-start(bf16[512,256]{1,0:T(8,128)(2,1)S(1)} %get-tuple-element.26), channel_id=1, source_target_pairs={{0,128},{32,160},{64,192},{96,224},{128,0},{160,32},{192,64},{224,... | collective-permute-start | bytes 786440 | tf_op jit(solution)/shard_map/ppermute | solution.py:459
  43.3 1.3 collective-permute-start.4
  44.6 0.7 collective-permute-start.3
  45.3 6.4 %collective-permute-done.5.refs_5_ = bf16[512,256]{1,0:T(8,128)(2,1)S(1)} collective-permute-done((bf16[512,256]{1,0:T(8,128)(2,1)S(1)}, bf16[512,256]{1,0:T(8,128)(2,1)S(1)}, u32[]{:S(2)}, u32[]{:S(2)}) %collective-permute-start.5) | collective-permute-done | bytes 262176 | tf_op jit(solution)/shard_map/ppermute | solution.py:459
  51.7 3.4 %collective-permute-done.4.refs_4_ = bf16[512,256]{1,0:T(8,128)(2,1)S(1)} collective-permute-done((bf16[512,256]{1,0:T(8,128)(2,1)S(1)}, bf16[512,256]{1,0:T(8,128)(2,1)S(1)}, u32[]{:S(2)}, u32[]{:S(2)}) %collective-permute-start.4) | collective-permute-done | bytes 262176 | tf_op jit(solution)/shard_map/ppermute | solution.py:459
  55.1 0.2 collective-permute-done.3.refs_3_
  55.2 0.5 copy-done.6
  56.0 4.4 %all-to-all-done.1.back_ref = bf16[32,36,256]{2,1,0:T(8,128)(2,1)S(1)} async-done(((bf16[32,36,256]{2,1,0:T(8,128)(2,1)}), bf16[32,36,256]{2,1,0:T(8,128)(2,1)S(1)}, u32[]{:S(2)}, u32[]{:S(2)}) %all-to-all-start.1) | async-done | bytes 589856 | tf_op jit(solution)/shard_map/all_to_all | solution.py:470
  60.4 0.7 broadcast_in_dim.14
  61.2 5.1 %all-to-all-start.2 = ((bf16[32,16,256]{2,1,0:T(8,128)(2,1)}), bf16[32,16,256]{2,1,0:T(8,128)(2,1)S(1)}, u32[]{:S(2)}, u32[]{:S(2)}) async-start(bf16[32,16,256]{2,1,0:T(8,128)(2,1)} %broadcast_in_dim.14), calls=%async_computation.2 | async-start | bytes 524288 | tf_op jit(solution)/shard_map/all_to_all | solution.py:470
  66.3 1.3 copy.22
  67.6 0.2 collective-permute-start.10
  67.8 0.7 convert_add_fusion
  68.6 0.2 collective-permute-done.10
  68.8 0.8 collective-permute-start.13
  69.6 1.2 collective-permute-start.12
  70.8 9.1 %all-to-all-done.2.d_ref = bf16[32,16,256]{2,1,0:T(8,128)(2,1)S(1)} async-done(((bf16[32,16,256]{2,1,0:T(8,128)(2,1)}), bf16[32,16,256]{2,1,0:T(8,128)(2,1)S(1)}, u32[]{:S(2)}, u32[]{:S(2)}) %all-to-all-start.2) | async-done | bytes 262176 | tf_op jit(solution)/shard_map/all_to_all | solution.py:470
  80.0 2.3 %collective-permute-start.2 = (bf16[512,256]{1,0:T(8,128)(2,1)S(1)}, bf16[512,256]{1,0:T(8,128)(2,1)S(1)}, u32[]{:S(2)}, u32[]{:S(2)}) collective-permute-start(bf16[512,256]{1,0:T(8,128)(2,1)S(1)} %bitcast.16), channel_id=1, source_target_pairs={{0,128},{32,160},{64,192},{96,224},{128,0},{160,32},{192,64},{224,... | collective-permute-start | bytes 786440 | tf_op jit(solution)/shard_map/ppermute | solution.py:459
  82.3 0.5 collective-permute-start.1
  82.7 1.6 %collective-permute-start = (bf16[512,256]{1,0:T(8,128)(2,1)S(1)}, bf16[512,256]{1,0:T(8,128)(2,1)S(1)}, u32[]{:S(2)}, u32[]{:S(2)}) collective-permute-start(bf16[512,256]{1,0:T(8,128)(2,1)S(1)} %bitcast.18), channel_id=1, source_target_pairs={{0,64},{32,96},{64,128},{96,160},{128,192},{160,224},{192,0},{224,... | collective-permute-start | bytes 786440 | tf_op jit(solution)/shard_map/ppermute | solution.py:459
  84.3 7.8 %dense_own.1 = (f32[4096,256]{1,0:T(8,128)}, f32[128,4096]{1,0:T(8,128)}) custom-call(bf16[32,16,256]{2,1,0:T(8,128)(2,1)S(1)} %all-to-all-done.2.d_ref, bf16[32,32,128]{2,1,0:T(8,128)(2,1)S(1)} %all-to-all-done.feats_ref.refs_3_, bf16[4096,128]{1,0:T(8,128)(2,1)} %bitcast.19, bf16[4096,256]{1,0:T(8,128)(2,1)} %refs_7_.3), custom_call_target="tpu_custom_call" | custom-call | flops 3221225472 | bytes 10485760 | tf_op jit(solution)/shard_map/dense_own/pallas_call | solution.py:287
  92.1 2.5 %collective-permute-start.11 = (bf16[20,256]{1,0:T(8,128)(2,1)S(1)}, bf16[20,256]{1,0:T(8,128)(2,1)S(1)}, u32[]{:S(2)}, u32[]{:S(2)}) collective-permute-start(bf16[20,256]{1,0:T(8,128)(2,1)S(1)} %add_convert_fusion.1), channel_id=1, source_target_pairs={{0,128},{32,160},{64,192},{96,224},{128,0},{160,32},{192,64},{224,... | collective-permute-start | bytes 30728 | tf_op jit(solution)/shard_map/ppermute | solution.py:459
  94.6 0.7 copy-done.10
  95.4 10.0 %dense_far.3 = (bf16[2048,256]{1,0:T(8,128)(2,1)S(1)}, bf16[128,2048]{1,0:T(8,128)(2,1)S(1)}) custom-call(bf16[512,256]{1,0:T(8,128)(2,1)} %copy-done.11, bf16[512,256]{1,0:T(8,128)(2,1)} %copy-done.10, bf16[512,256]{1,0:T(8,128)(2,1)} %copy-done.9, bf16[512,256]{1,0:T(8,128)(2,1)} %copy-done.7, bf16[512,256]{1,0:T(8,128)(2,1)} %copy-done.6, ...), custom_call_target="tpu_custom_call" | custom-call | flops 4831838208 | bytes 10485760 | tf_op jit(solution)/shard_map/dense_far/pallas_call | solution.py:337
  105.5 10.1 %dense_far.2 = (bf16[2048,256]{1,0:T(8,128)(2,1)S(1)}, bf16[128,2048]{1,0:T(8,128)(2,1)S(1)}) custom-call(bf16[512,256]{1,0:T(8,128)(2,1)} %copy-done.11, bf16[512,256]{1,0:T(8,128)(2,1)} %copy-done.10, bf16[512,256]{1,0:T(8,128)(2,1)} %copy-done.9, bf16[512,256]{1,0:T(8,128)(2,1)} %copy-done.7, bf16[512,256]{1,0:T(8,128)(2,1)} %copy-done.6, ...), custom_call_target="tpu_custom_call" | custom-call | flops 4831838208 | bytes 10485760 | tf_op jit(solution)/shard_map/dense_far/pallas_call | solution.py:337
  115.7 0.5 collective-permute-start.6
  116.2 0.6 copy-done.8
  116.8 0.7 broadcast_in_dim.15
  117.5 3.9 %all-to-all-start.3 = ((bf16[32,16,256]{2,1,0:T(8,128)(2,1)}), bf16[32,16,256]{2,1,0:T(8,128)(2,1)S(1)}, u32[]{:S(2)}, u32[]{:S(2)}) async-start(bf16[32,16,256]{2,1,0:T(8,128)(2,1)} %broadcast_in_dim.15), calls=%async_computation.3 | async-start | bytes 524288 | tf_op jit(solution)/shard_map/all_to_all | solution.py:470
  121.4 0.7 fusion
  122.2 0.4 collective-permute-start.7
  122.6 0.7 slice_bitcast_fusion
  123.3 0.6 copy.23
  123.9 11.0 %all-to-all-done.3 = bf16[32,16,256]{2,1,0:T(8,128)(2,1)S(1)} async-done(((bf16[32,16,256]{2,1,0:T(8,128)(2,1)}), bf16[32,16,256]{2,1,0:T(8,128)(2,1)S(1)}, u32[]{:S(2)}, u32[]{:S(2)}) %all-to-all-start.3) | async-done | bytes 262176 | tf_op jit(solution)/shard_map/all_to_all | solution.py:470
  135.0 0.9 pad_maximum_fusion
  135.8 0.2 copy-done.1
  136.0 3.9 %finish.2 = (f32[4096,256]{1,0:T(8,128)}, f32[128,4096]{1,0:T(8,128)}) custom-call(bf16[2048,256]{1,0:T(8,128)(2,1)S(1)} %get-tuple-element.31.refs_0_, bf16[2048,256]{1,0:T(8,128)(2,1)} %collective-permute-done.8.refs_1_, bf16[128,2048]{1,0:T(8,128)(2,1)S(1)} %copy-done.1, bf16[128,2048]{1,0:T(8,128)(2,1)} %collective-permute-done.9.refs_3_), custom_call_target="tpu_custom_call" | custom-call | tf_op jit(solution)/shard_map/finish/pallas_call | solution.py:381
  139.9 3.8 %finish.3 = (f32[4096,256]{1,0:T(8,128)}, f32[128,4096]{1,0:T(8,128)}) custom-call(bf16[2048,256]{1,0:T(8,128)(2,1)S(1)} %get-tuple-element.29.refs_0_, bf16[2048,256]{1,0:T(8,128)(2,1)} %collective-permute-done.6.refs_1_, bf16[128,2048]{1,0:T(8,128)(2,1)S(1)} %get-tuple-element.30.refs_2_, ...), custom_call_target="tpu_custom_call", output_to_operand_aliasing={{0}: (4, {}), {1}: (5, {})} | custom-call | tf_op jit(solution)/shard_map/finish/pallas_call | solution.py:381
  (41 shorter events, 0.8 us)
Async XLA Ops:
  2.3 24.1 %all-to-all-start = ((bf16[32,32,128]{2,1,0:T(8,128)(2,1)}), bf16[32,32,128]{2,1,0:T(8,128)(2,1)S(1)}, u32[]{:S(2)}, u32[]{:S(2)}) async-start(bf16[32,32,128]{2,1,0:T(8,128)(2,1)} %pack.1), calls=%async_computation | async-start | bytes 524288 | tf_op jit(solution)/shard_map/all_to_all | solution.py:470
  15.4 0.9 copy-start.3
  17.0 13.8 %copy-start.2 = (bf16[256,512]{1,0:T(8,128)(2,1)S(1)}, bf16[256,512]{1,0:T(8,128)(2,1)}, u32[]{:S(2)}) copy-start(bf16[256,512]{1,0:T(8,128)(2,1)} %refs_4_.1) | copy-start | bytes 786436
  36.8 29.5 %copy-start.4 = (bf16[128,4096]{1,0:T(8,128)(2,1)S(1)}, bf16[128,4096]{1,0:T(8,128)(2,1)}, u32[]{:S(2)}) copy-start(bf16[128,4096]{1,0:T(8,128)(2,1)} %win_ref.1) | copy-start | bytes 3145732
  36.8 23.6 %all-to-all-start.1 = ((bf16[32,36,256]{2,1,0:T(8,128)(2,1)}), bf16[32,36,256]{2,1,0:T(8,128)(2,1)S(1)}, u32[]{:S(2)}, u32[]{:S(2)}) async-start(bf16[32,36,256]{2,1,0:T(8,128)(2,1)} %get-tuple-element.24), calls=%async_computation.1 | async-start | bytes 1310720 | tf_op jit(solution)/shard_map/all_to_all | solution.py:470
  40.9 10.8 %collective-permute-start.5 = (bf16[512,256]{1,0:T(8,128)(2,1)S(1)}, bf16[512,256]{1,0:T(8,128)(2,1)S(1)}, u32[]{:S(2)}, u32[]{:S(2)}) collective-permute-start(bf16[512,256]{1,0:T(8,128)(2,1)S(1)} %get-tuple-element.26), channel_id=1, source_target_pairs={{0,128},{32,160},{64,192},{96,224},{128,0},{160,32},{192,64},{224,... | collective-permute-start | bytes 786440 | tf_op jit(solution)/shard_map/ppermute | solution.py:459
  43.3 11.8 %collective-permute-start.4 = (bf16[512,256]{1,0:T(8,128)(2,1)S(1)}, bf16[512,256]{1,0:T(8,128)(2,1)S(1)}, u32[]{:S(2)}, u32[]{:S(2)}) collective-permute-start(bf16[512,256]{1,0:T(8,128)(2,1)S(1)} %get-tuple-element.26), channel_id=1, source_target_pairs={{0,192},{32,224},{64,0},{96,32},{128,64},{160,96},{192,128},{224,1... | collective-permute-start | bytes 786440 | tf_op jit(solution)/shard_map/ppermute | solution.py:459
  44.6 10.6 %collective-permute-start.3 = (bf16[512,256]{1,0:T(8,128)(2,1)S(1)}, bf16[512,256]{1,0:T(8,128)(2,1)S(1)}, u32[]{:S(2)}, u32[]{:S(2)}) collective-permute-start(bf16[512,256]{1,0:T(8,128)(2,1)S(1)} %get-tuple-element.26), channel_id=1, source_target_pairs={{0,64},{32,96},{64,128},{96,160},{128,192},{160,224},{192,0},{224,... | collective-permute-start | bytes 786440 | tf_op jit(solution)/shard_map/ppermute | solution.py:459
  51.7 15.9 %copy-start.5 = (bf16[512,256]{1,0:T(8,128)(2,1)}, bf16[512,256]{1,0:T(8,128)(2,1)S(1)}, u32[]{:S(2)}) copy-start(bf16[512,256]{1,0:T(8,128)(2,1)S(1)} %collective-permute-done.5.refs_5_) | copy-start | bytes 786436
  55.1 0.7 copy-start.6
  55.8 11.8 %copy-start.7 = (bf16[512,256]{1,0:T(8,128)(2,1)}, bf16[512,256]{1,0:T(8,128)(2,1)S(1)}, u32[]{:S(2)}) copy-start(bf16[512,256]{1,0:T(8,128)(2,1)S(1)} %collective-permute-done.3.refs_3_) | copy-start | bytes 786436
  55.9 12.0 %collective-permute-start.14 = (bf16[256,256]{1,0:T(8,128)(2,1)S(1)}, bf16[256,256]{1,0:T(8,128)(2,1)S(1)}, u32[]{:S(2)}, u32[]{:S(2)}) collective-permute-start(bf16[256,256]{1,0:T(8,128)(2,1)S(1)} %add_convert_fusion), channel_id=1, source_target_pairs={{0,32},{32,0},{64,96},{96,64},{128,160},{160,128},{192,224},{224,1... | collective-permute-start | bytes 393224 | tf_op jit(solution)/shard_map/ppermute | solution.py:462
  61.2 18.8 %all-to-all-start.2 = ((bf16[32,16,256]{2,1,0:T(8,128)(2,1)}), bf16[32,16,256]{2,1,0:T(8,128)(2,1)S(1)}, u32[]{:S(2)}, u32[]{:S(2)}) async-start(bf16[32,16,256]{2,1,0:T(8,128)(2,1)} %broadcast_in_dim.14), calls=%async_computation.2 | async-start | bytes 524288 | tf_op jit(solution)/shard_map/all_to_all | solution.py:470
  67.6 1.2 collective-permute-start.10
  68.8 47.4 %collective-permute-start.13 = (bf16[20,256]{1,0:T(8,128)(2,1)S(1)}, bf16[20,256]{1,0:T(8,128)(2,1)S(1)}, u32[]{:S(2)}, u32[]{:S(2)}) collective-permute-start(bf16[20,256]{1,0:T(8,128)(2,1)S(1)} %add_convert_fusion.1), channel_id=1, source_target_pairs={{0,192},{32,224},{64,0},{96,32},{128,64},{160,96},{192,128},{224,1... | collective-permute-start | bytes 30728 | tf_op jit(solution)/shard_map/ppermute | solution.py:459
  69.6 46.5 %collective-permute-start.12 = (bf16[20,256]{1,0:T(8,128)(2,1)S(1)}, bf16[20,256]{1,0:T(8,128)(2,1)S(1)}, u32[]{:S(2)}, u32[]{:S(2)}) collective-permute-start(bf16[20,256]{1,0:T(8,128)(2,1)S(1)} %add_convert_fusion.1), channel_id=1, source_target_pairs={{0,64},{32,96},{64,128},{96,160},{128,192},{160,224},{192,0},{224,... | collective-permute-start | bytes 30728 | tf_op jit(solution)/shard_map/ppermute | solution.py:459
  80.0 12.1 %collective-permute-start.2 = (bf16[512,256]{1,0:T(8,128)(2,1)S(1)}, bf16[512,256]{1,0:T(8,128)(2,1)S(1)}, u32[]{:S(2)}, u32[]{:S(2)}) collective-permute-start(bf16[512,256]{1,0:T(8,128)(2,1)S(1)} %bitcast.16), channel_id=1, source_target_pairs={{0,128},{32,160},{64,192},{96,224},{128,0},{160,32},{192,64},{224,... | collective-permute-start | bytes 786440 | tf_op jit(solution)/shard_map/ppermute | solution.py:459
  82.3 12.3 %collective-permute-start.1 = (bf16[512,256]{1,0:T(8,128)(2,1)S(1)}, bf16[512,256]{1,0:T(8,128)(2,1)S(1)}, u32[]{:S(2)}, u32[]{:S(2)}) collective-permute-start(bf16[512,256]{1,0:T(8,128)(2,1)S(1)} %bitcast.17), channel_id=1, source_target_pairs={{0,192},{32,224},{64,0},{96,32},{128,64},{160,96},{192,128},{224,1... | collective-permute-start | bytes 786440 | tf_op jit(solution)/shard_map/ppermute | solution.py:459
  82.7 11.9 %collective-permute-start = (bf16[512,256]{1,0:T(8,128)(2,1)S(1)}, bf16[512,256]{1,0:T(8,128)(2,1)S(1)}, u32[]{:S(2)}, u32[]{:S(2)}) collective-permute-start(bf16[512,256]{1,0:T(8,128)(2,1)S(1)} %bitcast.18), channel_id=1, source_target_pairs={{0,64},{32,96},{64,128},{96,160},{128,192},{160,224},{192,0},{224,... | collective-permute-start | bytes 786440 | tf_op jit(solution)/shard_map/ppermute | solution.py:459
  92.1 2.6 %copy-start.9 = (bf16[512,256]{1,0:T(8,128)(2,1)}, bf16[512,256]{1,0:T(8,128)(2,1)S(1)}, u32[]{:S(2)}) copy-start(bf16[512,256]{1,0:T(8,128)(2,1)S(1)} %collective-permute-done.2.refs_2_) | copy-start | bytes 786436
  92.1 24.1 %collective-permute-start.11 = (bf16[20,256]{1,0:T(8,128)(2,1)S(1)}, bf16[20,256]{1,0:T(8,128)(2,1)S(1)}, u32[]{:S(2)}, u32[]{:S(2)}) collective-permute-start(bf16[20,256]{1,0:T(8,128)(2,1)S(1)} %add_convert_fusion.1), channel_id=1, source_target_pairs={{0,128},{32,160},{64,192},{96,224},{128,0},{160,32},{192,64},{224,... | collective-permute-start | bytes 30728 | tf_op jit(solution)/shard_map/ppermute | solution.py:459
  94.6 0.7 copy-start.10
  94.6 0.8 copy-start.11
  105.4 10.2 %copy-start = (bf16[128,2048]{1,0:T(8,128)(2,1)}, bf16[128,2048]{1,0:T(8,128)(2,1)S(1)}, u32[]{:S(2)}) copy-start(bf16[128,2048]{1,0:T(8,128)(2,1)S(1)} %get-tuple-element.32.refs_2_) | copy-start | bytes 1572868
  105.4 30.4 %collective-permute-start.8 = (bf16[2048,256]{1,0:T(8,128)(2,1)S(1)}, bf16[2048,256]{1,0:T(8,128)(2,1)}, u32[]{:S(2)}, u32[]{:S(2)}) collective-permute-start(bf16[2048,256]{1,0:T(8,128)(2,1)S(1)} %get-tuple-element.31.refs_0_), channel_id=1, source_target_pairs={{0,32},{32,0},{64,96},{96,64},{128,160},{160,128},{192,224},{224,1... | collective-permute-start | bytes 3145736 | tf_op jit(solution)/shard_map/ppermute | solution.py:462
  115.7 24.2 %collective-permute-start.6 = (bf16[2048,256]{1,0:T(8,128)(2,1)S(1)}, bf16[2048,256]{1,0:T(8,128)(2,1)}, u32[]{:S(2)}, u32[]{:S(2)}) collective-permute-start(bf16[2048,256]{1,0:T(8,128)(2,1)S(1)} %get-tuple-element.29.refs_0_), channel_id=1, source_target_pairs={{0,32},{32,0},{64,96},{96,64},{128,160},{160,128},{192,224},{224,1... | collective-permute-start | bytes 3145736 | tf_op jit(solution)/shard_map/ppermute | solution.py:462
  116.2 0.6 copy-start.8
  117.5 17.4 %all-to-all-start.3 = ((bf16[32,16,256]{2,1,0:T(8,128)(2,1)}), bf16[32,16,256]{2,1,0:T(8,128)(2,1)S(1)}, u32[]{:S(2)}, u32[]{:S(2)}) async-start(bf16[32,16,256]{2,1,0:T(8,128)(2,1)} %broadcast_in_dim.15), calls=%async_computation.3 | async-start | bytes 524288 | tf_op jit(solution)/shard_map/all_to_all | solution.py:470
  122.1 13.7 %collective-permute-start.9 = (bf16[128,2048]{1,0:T(8,128)(2,1)}, bf16[128,2048]{1,0:T(8,128)(2,1)}, u32[]{:S(2)}, u32[]{:S(2)}) collective-permute-start(bf16[128,2048]{1,0:T(8,128)(2,1)} %copy-done), channel_id=1, source_target_pairs={{0,32},{32,0},{64,96},{96,64},{128,160},{160,128},{192,224},{224,1... | collective-permute-start | bytes 1572872 | tf_op jit(solution)/shard_map/ppermute | solution.py:462
  122.2 17.6 %collective-permute-start.7 = (bf16[128,2048]{1,0:T(8,128)(2,1)S(1)}, bf16[128,2048]{1,0:T(8,128)(2,1)S(1)}, u32[]{:S(2)}, u32[]{:S(2)}) collective-permute-start(bf16[128,2048]{1,0:T(8,128)(2,1)S(1)} %get-tuple-element.30.refs_2_), channel_id=1, source_target_pairs={{0,32},{32,0},{64,96},{96,64},{128,160},{160,128},{192,224},{224,1... | collective-permute-start | bytes 1572872 | tf_op jit(solution)/shard_map/ppermute | solution.py:462
  134.9 1.1 copy-start.1

commit v2 on v1

--- a/solution.py
+++ b/solution.py
@@ -248,26 +248,71 @@
     )(users, items, counts, came, iw, weight)
 
 
-def fold_kernel(back_ref, own_ref, part_ref):
-    each, _ = own_ref.shape
+def fold_kernel(back_ref, own_ref, part_ref, score_ref):
+    shards, each, width = own_ref.shape
+    slots = score_ref.shape[1]
+    came = back_ref[:, 2 * each : 2 * each + 4, :].astype(F32)
+    line = lax.broadcasted_iota(jnp.int32, came.shape, 1)
+    three = jnp.sum(jnp.where(line == 2, came, 0.0), axis=1)
+    src = lax.broadcasted_iota(jnp.int32, (width, slots), 0)
+    dst = lax.broadcasted_iota(jnp.int32, (width, slots), 1)
+    pick = jnp.where((src % slots == dst) & (src < 3 * slots), 1.0, 0.0)
+    score_ref[...] = mm(three.astype(BF), pick.astype(BF))
     total = back_ref[0, 0 : 2 * each + 4, :].astype(F32)
     for n in range(1, back_ref.shape[0]):
         total = total + back_ref[n, 0 : 2 * each + 4, :].astype(F32)
-    own_ref[...] = total[0:each].astype(BF)
+    own_ref[...] = jnp.broadcast_to(total[0:each].astype(BF)[None], (shards, each, width))
     part_ref[...] = total[each:].astype(BF)
 
 
-def fold(back, each):
-    width = back.shape[2]
+def fold(back, each, slots):
+    shards, width = back.shape[0], back.shape[2]
     return pl.pallas_call(
         fold_kernel,
         out_shape=(
-            jax.ShapeDtypeStruct((each, width), BF),
+            jax.ShapeDtypeStruct((shards, each, width), BF),
             jax.ShapeDtypeStruct((each + 4, width), BF),
+            jax.ShapeDtypeStruct((shards, slots), F32),
         ),
         compiler_params=pltpu.CompilerParams(vmem_limit_bytes=6 << 20),
         name="fold",
     )(back)
+
+
+def tie_kernel(p0, pa, pb, pc, t0, ta, tb, tc, after_ref, inter_ref, out_ref, column_ref):
+    shards, each, width = inter_ref.shape
+    f = [x[...].astype(F32) for x in (p0, pa, pb, pc)]
+    total = (f[0] + f[3]) + (f[1] + f[2])
+    inter_ref[...] = jnp.broadcast_to(total[0:each].astype(BF)[None], (shards, each, width))
+    out_ref[:, 0:width] = total[each : each + 1]
+    out_ref[:, width:] = total[each + 1 : each + 2]
+    t = [x[...].astype(F32) for x in (t0, ta, tb, tc)]
+    column_ref[...] = ((t[0] + t[3]) + (t[1] + t[2])).astype(BF)
+
+
+def tie(parts, shares, after, shards, each):
+    width = parts[0].shape[1]
+    rows = shares[0].shape[0] // 2
+    lower = pl.BlockSpec((rows, width), lambda i: (1, 0))
+    return pl.pallas_call(
+        tie_kernel,
+        grid=(1,),
+        in_specs=[pl.BlockSpec(parts[0].shape, lambda i: (0, 0))] * 4
+        + [lower] * 4
+        + [pl.BlockSpec(memory_space=pl.ANY)],
+        out_specs=(
+            pl.BlockSpec((shards, each, width), lambda i: (0, 0, 0)),
+            pl.BlockSpec((1, 2 * width), lambda i: (0, 0)),
+            pl.BlockSpec((rows, width), lambda i: (0, 0)),
+        ),
+        out_shape=(
+            jax.ShapeDtypeStruct((shards, each, width), BF),
+            jax.ShapeDtypeStruct((1, 2 * width), F32),
+            jax.ShapeDtypeStruct((rows, width), BF),
+        ),
+        compiler_params=pltpu.CompilerParams(vmem_limit_bytes=8 << 20),
+        name="tie",
+    )(*parts, *shares, after)
 
 
 def own_kernel(d_ref, feats_ref, win_ref, wout_ref, gout_ref, gin_ref):
@@ -308,9 +353,19 @@
     )(d, feats, hbm(win_t), hbm(tower_out))
 
 
-def far_kernel(count, *refs):
+def finish_half(out_a, out_b, in_a, in_b, gout_ref, gin_ref):
+    gout_ref[...] = out_a[...].astype(F32) + out_b[...].astype(F32)
+    gin_ref[...] = in_a[...].astype(F32) + in_b[...].astype(F32)
+
+
+def far_kernel(count, finishing, *refs):
     d, feats = refs[0:count], refs[count : 2 * count]
-    win_ref, wout_ref, old_out, old_in, gout_ref, gin_ref = refs[2 * count :]
+    win_ref, wout_ref, old_out, old_in = refs[2 * count : 2 * count + 4]
+    rest = refs[2 * count + 4 :]
+    if finishing:
+        finish_half(*rest[0:4], *rest[6:8])
+        rest = rest[4:6]
+    gout_ref, gin_ref = rest
     wout = wout_ref[...]
     win = win_ref[...]
     d_all = jnp.concatenate([x[...] for x in d], axis=0)
@@ -327,15 +382,17 @@
     gin_ref[...] = (back.T + old_in[...]).astype(BF)
 
 
-def dense_far(d, feats, win_t, tower_out, before, first, units):
-    _, width = tower_out.shape
+def dense_far(d, feats, win_t, tower_out, before, first, units, pieces):
+    wide, width = tower_out.shape
     reqs = d[0].shape[0]
     uf = win_t.shape[1]
     count = len(d)
     block = 512
     base = first // block
-    return pl.pallas_call(
-        lambda *refs: far_kernel(count, *refs),
+    out_spec = pl.BlockSpec((block, width), lambda i: (i, 0))
+    in_spec = pl.BlockSpec((uf, block), lambda i: (0, i))
+    return pl.pallas_call(
+        lambda *refs: far_kernel(count, pieces is not None, *refs),
         grid=(units // block,),
         in_specs=[pl.BlockSpec((reqs, width), lambda i: (0, 0))] * count
         + [pl.BlockSpec((reqs // 2, 2 * uf), lambda i: (0, 0))] * count
@@ -344,15 +401,14 @@
             pl.BlockSpec((block, width), lambda i: (base + i, 0)),
             pl.BlockSpec((block, width), lambda i: (base + i, 0)),
             pl.BlockSpec((uf, block), lambda i: (0, base + i)),
-        ],
-        out_specs=(
-            pl.BlockSpec((block, width), lambda i: (i, 0)),
-            pl.BlockSpec((uf, block), lambda i: (0, i)),
-        ),
+        ]
+        + ([out_spec] * 2 + [in_spec] * 2 if pieces else []),
+        out_specs=(out_spec, in_spec) * (2 if pieces else 1),
         out_shape=(
             jax.ShapeDtypeStruct((units, width), BF),
             jax.ShapeDtypeStruct((uf, units), BF),
-        ),
+        )
+        + ((pltpu.HBM((wide, width), F32), pltpu.HBM((uf, wide), F32)) if pieces else ()),
         compiler_params=pltpu.CompilerParams(vmem_limit_bytes=36 << 20),
         cost_estimate=pl.CostEstimate(
             flops=2 * count * reqs * units * (2 * width + 2 * uf),
@@ -360,37 +416,56 @@
             transcendentals=count * reqs * units,
         ),
         name="dense_far",
-    )(*[hbm(x) for x in (*d, *feats, win_t, tower_out, *before)])
+    )(*[hbm(x) for x in (*d, *feats, win_t, tower_out, *before)], *(pieces or ()))
 
 
 def finish_kernel(*refs):
-    out_a, out_b, in_a, in_b = refs[0:4]
-    gout_ref, gin_ref = refs[-2:]
-    gout_ref[...] = out_a[...].astype(F32) + out_b[...].astype(F32)
-    gin_ref[...] = in_a[...].astype(F32) + in_b[...].astype(F32)
-
-
-def finish(outs, ins, before, first, wide):
-    units, width = outs[0].shape
-    uf = ins[0].shape[0]
+    gout_ref, gin_ref, table_ref, inter_ref = refs[-4:]
+    finish_half(*refs[0:4], gout_ref, gin_ref)
+    table_ref[...] = refs[4][...].astype(F32) + refs[5][...].astype(F32)
+    width = table_ref.shape[1]
+    inter_ref[:, 0:width] = refs[6][...].astype(F32).reshape(inter_ref.shape[0], width)
+    inter_ref[:, width:] = refs[7][...].astype(F32).reshape(inter_ref.shape[0], width)
+
+
+def finish(pieces, column, other, inter, before, first):
+    units, width = pieces[0].shape
+    uf = pieces[2].shape[0]
+    wide = before[0].shape[0]
+    shards, each, _ = inter.shape
     block = 512
     base = first // block
+    steps = units // block
+    part = column.shape[0] // steps
+    near = shards // 2 // steps
     spec_o = pl.BlockSpec((block, width), lambda i: (i, 0))
     spec_i = pl.BlockSpec((uf, block), lambda i: (0, i))
-    extra = [] if before is None else [pl.BlockSpec(memory_space=pl.ANY)] * 2
+    spec_t = pl.BlockSpec((part, width), lambda i: (i, 0))
     return pl.pallas_call(
         finish_kernel,
-        grid=(units // block,),
-        in_specs=[spec_o, spec_o, spec_i, spec_i] + extra,
+        grid=(steps,),
+        in_specs=[spec_o, spec_o, spec_i, spec_i, spec_t, spec_t]
+        + [
+            pl.BlockSpec((near, each, width), lambda i: (i, 0, 0)),
+            pl.BlockSpec((near, each, width), lambda i: (steps + i, 0, 0)),
+        ]
+        + [pl.BlockSpec(memory_space=pl.ANY)] * 2,
         out_specs=(
             pl.BlockSpec((block, width), lambda i: (base + i, 0)),
             pl.BlockSpec((uf, block), lambda i: (0, base + i)),
-        ),
-        out_shape=(pltpu.HBM((wide, width), F32), pltpu.HBM((uf, wide), F32)),
-        input_output_aliases={} if before is None else {4: 0, 5: 1},
-        compiler_params=pltpu.CompilerParams(vmem_limit_bytes=8 << 20),
+            spec_t,
+            pl.BlockSpec((near * each, 2 * width), lambda i: (i, 0)),
+        ),
+        out_shape=(
+            pltpu.HBM((wide, width), F32),
+            pltpu.HBM((uf, wide), F32),
+            jax.ShapeDtypeStruct(column.shape, F32),
+            jax.ShapeDtypeStruct((shards // 2 * each, 2 * width), F32),
+        ),
+        input_output_aliases={8: 0, 9: 1},
+        compiler_params=pltpu.CompilerParams(vmem_limit_bytes=12 << 20),
         name="finish",
-    )(*outs, *ins, *(before or ()))
+    )(*pieces, column, other, inter, inter, *before)
 
 
 def pack_kernel(feats_ref, req_ref, lab_ref, live_ref, out_ref):
@@ -461,11 +536,6 @@
     def swap(x):
         return lax.ppermute(x, "grp", ring(0, 1))
 
-    def group_sum(x):
-        pair = (x.astype(F32) + swap(x).astype(F32)).astype(BF)
-        a, b, c = from_chips(pair)
-        return (pair.astype(F32) + c.astype(F32)) + (a.astype(F32) + b.astype(F32))
-
     def exchange(x):
         return lax.all_to_all(x, "tbl", split_axis=0, concat_axis=0, tiled=True)
 
@@ -480,36 +550,24 @@
     )
     back = exchange(sent)
     far = from_chips(share)
-    own, part = fold(back, each)
-    third = exchange(jnp.broadcast_to(own, (shards, each, width)))
-    total = group_sum(part)
-    grad_out = total[each : each + 2].reshape(-1)
-    s_back = back[:, 2 * each + 2, : 3 * slots].astype(F32)
-    scores = (s_back[:, :slots] + s_back[:, slots : 2 * slots]) + s_back[:, 2 * slots :]
-    top = reqs // 2
-    a, b, c = (f[top:].astype(F32) for f in far)
-    column = ((share[top:].astype(F32) + c) + (a + b)).astype(BF)
-    grad_table = column.astype(F32) + swap(column).astype(F32)
+    own, part, scores = fold(back, each, slots)
+    third = exchange(own)
+    pair = (part.astype(F32) + swap(part).astype(F32)).astype(BF)
+    parts = [pair] + from_chips(pair)
     d_far = from_chips(third.reshape(reqs, width))
-    inter_all = exchange(
-        jnp.broadcast_to(total[:each].astype(BF), (shards, each, width))
-    )
     before = dense_own(third, arrived, win_t, tower_out, each)
-    half = shards // 2
-    inter_flat = inter_all.astype(F32)
-    grad_inter = jnp.concatenate(
-        [inter_flat[:half].reshape(width, width), inter_flat[half:].reshape(width, width)],
-        axis=1,
-    )
+    inter_part, grad_out, column = tie(parts, [share] + far, hbm(before[1]), shards, each)
+    inter_all = exchange(inter_part)
+    other = swap(column)
     units = tower_out.shape[0] // 2
-    sums = None
-    pieces = []
+    pieces = None
     for k in range(2):
-        g_out, g_in = dense_far(d_far, far, win_t, tower_out, before, k * units, units)
-        pieces.append(((g_out, swap(g_out)), (g_in, swap(g_in))))
-    for k in range(2):
-        sums = finish(*pieces[k], sums, k * units, 2 * units)
-    return (scores[None], sums[1], sums[0], grad_inter, grad_out, grad_table)
+        g_out, g_in, *first = dense_far(
+            d_far, far, win_t, tower_out, before, k * units, units, pieces
+        )
+        pieces = (g_out, swap(g_out), g_in, swap(g_in))
+    sums = finish(pieces, column, other, inter_all, first, units)
+    return (scores[None], sums[1], sums[0], sums[3], grad_out.reshape(-1), sums[2])
 
 
 def solution(mesh):

time: 145 us -> 154 us (1.062)
  blocking collectives: 0 us -> 23.4 us
  waiting for transfers between devices: 44.2 us -> 38.1 us
  Pallas kernels: 48.3 us -> 44.6 us
  other arithmetic: 2.38 us -> 0.01 us
  local copies, waits for them, and re-layouts: 8.84 us -> 6.98 us
    all_to_all x0 -> x1, blocking collectives: none -> 23.4 us  [exchange(): return lax.all_to_all(x, 'tbl', split_axis=0, concat_axis=0, tiled=True)]
    all_to_all x4 -> x3, waiting for transfers between devices: 33.9 us -> 25.6 us  [exchange(): return lax.all_to_all(x, 'tbl', split_axis=0, concat_axis=0, tiled=True)]
    ppermute x6, waiting for transfers between devices: 0.25 us -> 6.27 us  [swap(): return lax.ppermute(x, 'grp', ring(0, 1))]
    ppermute x9, waiting for transfers between devices: 9.97 us -> 6.23 us  [from_chips(): return [lax.ppermute(x, 'grp', ring(turn, 0)) for turn in (1, chips - 1, 2)]]
    pallas_call x5, Pallas kernels: 27.9 us -> 25 us  [the longest x2 21.1 us: dense_far(): pl.pallas_call(lambda *refs: far_kernel(count, pieces is not None, *refs)...]
    all_to_all x4 -> x3, starting transfers between devices: 24.4 us -> 25.8 us  [exchange(): return lax.all_to_all(x, 'tbl', split_axis=0, concat_axis=0, tiled=True)]
    unnamed x27 -> x31, local copies, waits for them, and re-layouts: 5.59 us -> 5.21 us
  transfers between devices with their start and end apart: 19 -> 18, of which waited for: 8 -> 10; matrix products, arithmetic and copies ran while one was open for 6% -> 2% of each run, Pallas kernels for 23% -> 6%
where the time goes in v2:
time: 154 us; the launch traced here: 153 us
  Pallas kernels  44.6 us (29%)
  starting transfers between devices  39.5 us (26%)
  waiting for transfers between devices  38.1 us (25%)
  blocking collectives  23.4 us (15%)
  local copies, waits for them, and re-layouts  6.98 us (5%)
    all_to_all x3, starting transfers between devices, exchange(): return lax.all_to_all(x, 'tbl', split_axis=0, concat_axis=0, tiled=True)  25.8 us
    all_to_all x3, waiting for transfers between devices, exchange(): return lax.all_to_all(x, 'tbl', split_axis=0, concat_axis=0, tiled=True)  25.6 us
    all_to_all x1, blocking collectives, exchange(): return lax.all_to_all(x, 'tbl', split_axis=0, concat_axis=0, tiled=True)  23.4 us
    pallas_call x2, Pallas kernels, dense_far(): pl.pallas_call(lambda *refs: far_kernel(count, pieces is not None, *refs)...  21.1 us
    ppermute x9, starting transfers between devices, from_chips(): return [lax.ppermute(x, 'grp', ring(turn, 0)) for turn in (1, chips - 1, 2)]  12.3 us
    pallas_call x1, Pallas kernels, dense_own(): pl.pallas_call(own_kernel, grid=(wide // block,), in_specs=[feats_spec(d,...  7.78 us
    ppermute x6, waiting for transfers between devices, swap(): return lax.ppermute(x, 'grp', ring(0, 1))  6.27 us
    ppermute x9, waiting for transfers between devices, from_chips(): return [lax.ppermute(x, 'grp', ring(turn, 0)) for turn in (1, chips - 1, 2)]  6.23 us
  transfers between devices with their start and end apart: 18, of which 10 were waited for; matrix products, arithmetic and copies ran while one was open for 2% of the time, Pallas kernels for 6%

profile of v2, /device:TPU:8, one launch (start us, length us, event | category | flops | bytes accessed | tf_op | source)
XLA Modules:
  0.0 153.4 jit_solution(10168220836398614698)
XLA Ops:
  0.6 1.7 %pack.1 = bf16[32,32,128]{2,1,0:T(8,128)(2,1)} custom-call(bf16[16,128]{1,0:T(8,128)(2,1)} %feats_ref.1, s32[32,32]{1,0:T(8,128)} %bitcast.17, f32[32,32]{1,0:T(8,128)} %bitcast.18, s32[1,32]{1,0:T(1,128)} %live_ref.1), custom_call_target="tpu_custom_call" | custom-call | tf_op jit(solution)/shard_map/pack/pallas_call | solution.py:507
  2.3 11.3 %all-to-all-start = ((bf16[32,32,128]{2,1,0:T(8,128)(2,1)}), bf16[32,32,128]{2,1,0:T(8,128)(2,1)S(1)}, u32[]{:S(2)}, u32[]{:S(2)}) async-start(bf16[32,32,128]{2,1,0:T(8,128)(2,1)} %pack.1), calls=%async_computation | async-start | bytes 524288 | tf_op jit(solution)/shard_map/all_to_all | solution.py:540
  13.6 0.8 copy.20
  14.5 0.1 reshape.21.ids_ref
  14.6 0.8 copy.21.refs_5_
  15.4 0.0 copy-start.10
  15.4 0.9 copy-done.10
  16.3 0.7 pool.1
  17.0 9.4 %all-to-all-done.feats_ref.refs_3_ = bf16[32,32,128]{2,1,0:T(8,128)(2,1)S(1)} async-done(((bf16[32,32,128]{2,1,0:T(8,128)(2,1)}), bf16[32,32,128]{2,1,0:T(8,128)(2,1)S(1)}, u32[]{:S(2)}, u32[]{:S(2)}) %all-to-all-start) | async-done | bytes 262176 | tf_op jit(solution)/shard_map/all_to_all | solution.py:540
  26.5 4.4 %users.1.refs_0_ = bf16[256,512]{1,0:T(8,128)(2,1)S(1)} custom-call(bf16[32,32,128]{2,1,0:T(8,128)(2,1)S(1)} %all-to-all-done.feats_ref.refs_3_, bf16[128,4096]{1,0:T(8,128)(2,1)} %win_ref.1, bf16[4096,256]{1,0:T(8,128)(2,1)} %refs_7_.3), custom_call_target="tpu_custom_call" | custom-call | flops 1610612736 | bytes 4194304 | tf_op jit(solution)/shard_map/users/pallas_call | solution.py:96
  30.8 5.1 %rank.1 = (bf16[32,36,256]{2,1,0:T(8,128)(2,1)S(1)}, bf16[512,256]{1,0:T(8,128)(2,1)S(1)}) custom-call(bf16[256,512]{1,0:T(8,128)(2,1)S(1)} %users.1.refs_0_, bf16[256,1024]{1,0:T(8,128)(2,1)S(1)} %get-tuple-element.28.refs_1_, bf16[256,1024]{1,0:T(8,128)(2,1)S(1)} %get-tuple-element.29.refs_2_, bf16[32,32,128]{2,1,0:T(8,128)(2,1)S(1)} %all-to-all-done.feats_ref.refs_3_, ...), custom_call_target="tpu_custom_call" | custom-call | flops 1476395008 | bytes 4194304 | tf_op jit(solution)/shard_map/rank/pallas_call | solution.py:228
  36.0 23.4 %all_to_all.20.back_ref = bf16[32,36,256]{2,1,0:T(8,128)(2,1)S(1)} all-to-all(bf16[32,36,256]{2,1,0:T(8,128)(2,1)S(1)} %get-tuple-element.30), channel_id=1, replica_groups=mesh['grp'=8,'tbl'=32] {'tbl'}, dimensions={0} | all-to-all | bytes 1179648 | tf_op jit(solution)/shard_map/all_to_all | solution.py:540
  59.3 0.9 fold.1
  60.2 5.0 %all-to-all-start.2 = ((bf16[32,16,256]{2,1,0:T(8,128)(2,1)}), bf16[32,16,256]{2,1,0:T(8,128)(2,1)S(1)}, u32[]{:S(2)}, u32[]{:S(2)}) async-start(bf16[32,16,256]{2,1,0:T(8,128)(2,1)} %get-tuple-element.32), calls=%async_computation.2 | async-start | bytes 524288 | tf_op jit(solution)/shard_map/all_to_all | solution.py:540
  65.2 1.6 %collective-permute-start.3 = (bf16[512,256]{1,0:T(8,128)(2,1)S(1)}, bf16[512,256]{1,0:T(8,128)(2,1)S(1)}, u32[]{:S(2)}, u32[]{:S(2)}) collective-permute-start(bf16[512,256]{1,0:T(8,128)(2,1)S(1)} %get-tuple-element.33.t0), channel_id=1, source_target_pairs={{0,64},{32,96},{64,128},{96,160},{128,192},{160,224},{192,0},{224,... | collective-permute-start | bytes 786440 | tf_op jit(solution)/shard_map/ppermute | solution.py:534
  66.9 1.3 copy.22
  68.2 0.5 collective-permute-start.4
  68.6 2.3 %collective-permute-start.5 = (bf16[512,256]{1,0:T(8,128)(2,1)S(1)}, bf16[512,256]{1,0:T(8,128)(2,1)S(1)}, u32[]{:S(2)}, u32[]{:S(2)}) collective-permute-start(bf16[512,256]{1,0:T(8,128)(2,1)S(1)} %get-tuple-element.33.t0), channel_id=1, source_target_pairs={{0,128},{32,160},{64,192},{96,224},{128,0},{160,32},{192,64},{224,... | collective-permute-start | bytes 786440 | tf_op jit(solution)/shard_map/ppermute | solution.py:534
  70.9 6.5 %all-to-all-done.2.d_ref = bf16[32,16,256]{2,1,0:T(8,128)(2,1)S(1)} async-done(((bf16[32,16,256]{2,1,0:T(8,128)(2,1)}), bf16[32,16,256]{2,1,0:T(8,128)(2,1)S(1)}, u32[]{:S(2)}, u32[]{:S(2)}) %all-to-all-start.2) | async-done | bytes 262176 | tf_op jit(solution)/shard_map/all_to_all | solution.py:540
  77.4 1.6 %collective-permute-start = (bf16[512,256]{1,0:T(8,128)(2,1)S(1)}, bf16[512,256]{1,0:T(8,128)(2,1)S(1)}, u32[]{:S(2)}, u32[]{:S(2)}) collective-permute-start(bf16[512,256]{1,0:T(8,128)(2,1)S(1)} %bitcast.10), channel_id=1, source_target_pairs={{0,64},{32,96},{64,128},{96,160},{128,192},{160,224},{192,0},{224,... | collective-permute-start | bytes 786440 | tf_op jit(solution)/shard_map/ppermute | solution.py:534
  79.0 0.5 collective-permute-start.1
  79.5 2.3 %collective-permute-start.2 = (bf16[512,256]{1,0:T(8,128)(2,1)S(1)}, bf16[512,256]{1,0:T(8,128)(2,1)S(1)}, u32[]{:S(2)}, u32[]{:S(2)}) collective-permute-start(bf16[512,256]{1,0:T(8,128)(2,1)S(1)} %bitcast.12), channel_id=1, source_target_pairs={{0,128},{32,160},{64,192},{96,224},{128,0},{160,32},{192,64},{224,... | collective-permute-start | bytes 786440 | tf_op jit(solution)/shard_map/ppermute | solution.py:534
  81.8 7.8 %dense_own.1 = (f32[4096,256]{1,0:T(8,128)}, f32[128,4096]{1,0:T(8,128)}) custom-call(bf16[32,16,256]{2,1,0:T(8,128)(2,1)S(1)} %all-to-all-done.2.d_ref, bf16[32,32,128]{2,1,0:T(8,128)(2,1)S(1)} %all-to-all-done.feats_ref.refs_3_, bf16[4096,128]{1,0:T(8,128)(2,1)} %bitcast.13, bf16[4096,256]{1,0:T(8,128)(2,1)} %refs_7_.3), custom_call_target="tpu_custom_call" | custom-call | flops 3221225472 | bytes 10485760 | tf_op jit(solution)/shard_map/dense_own/pallas_call | solution.py:332
  89.6 2.6 %collective-permute-done.2.refs_2_ = bf16[512,256]{1,0:T(8,128)(2,1)S(1)} collective-permute-done((bf16[512,256]{1,0:T(8,128)(2,1)S(1)}, bf16[512,256]{1,0:T(8,128)(2,1)S(1)}, u32[]{:S(2)}, u32[]{:S(2)}) %collective-permute-start.2) | collective-permute-done | bytes 262176 | tf_op jit(solution)/shard_map/ppermute | solution.py:534
  92.3 0.7 copy-done.14
  93.0 10.0 %dense_far.2 = (bf16[2048,256]{1,0:T(8,128)(2,1)S(1)}, bf16[128,2048]{1,0:T(8,128)(2,1)S(1)}) custom-call(bf16[512,256]{1,0:T(8,128)(2,1)} %copy-done.12, bf16[512,256]{1,0:T(8,128)(2,1)} %copy-done.13, bf16[512,256]{1,0:T(8,128)(2,1)} %copy-done.14, bf16[512,256]{1,0:T(8,128)(2,1)} %copy-done, bf16[512,256]{1,0:T(8,128)(2,1)} %copy-done.2, ...), custom_call_target="tpu_custom_call" | custom-call | flops 4831838208 | bytes 10485760 | tf_op jit(solution)/shard_map/dense_far/pallas_call | solution.py:394
  103.0 0.1 collective-permute-start.6
  103.1 0.5 collective-permute-start.7
  103.6 2.9 %collective-permute-done.7.refs_13_ = bf16[128,2048]{1,0:T(8,128)(2,1)S(1)} collective-permute-done((bf16[128,2048]{1,0:T(8,128)(2,1)S(1)}, bf16[128,2048]{1,0:T(8,128)(2,1)S(1)}, u32[]{:S(2)}, u32[]{:S(2)}) %collective-permute-start.7) | collective-permute-done | bytes 524320 | tf_op jit(solution)/shard_map/ppermute | solution.py:537
  106.5 11.1 %dense_far.3 = (bf16[2048,256]{1,0:T(8,128)(2,1)S(1)}, bf16[128,2048]{1,0:T(8,128)(2,1)S(1)}, f32[4096,256]{1,0:T(8,128)}, f32[128,4096]{1,0:T(8,128)}) custom-call(bf16[512,256]{1,0:T(8,128)(2,1)} %copy-done.12, bf16[512,256]{1,0:T(8,128)(2,1)} %copy-done.13, bf16[512,256]{1,0:T(8,128)(2,1)} %copy-done.14, bf16[512,256]{1,0:T(8,128)(2,1)} %copy-done, ...), custom_call_target="tpu_custom_call" | custom-call | flops 4831838208 | bytes 10485760 | tf_op jit(solution)/shard_map/dense_far/pallas_call | solution.py:394
  117.6 0.2 collective-permute-start.8
  117.8 0.4 collective-permute-start.10
  118.2 0.1 collective-permute-start.9
  118.3 2.0 %collective-permute-done.10 = bf16[20,256]{1,0:T(8,128)(2,1)S(1)} collective-permute-done((bf16[20,256]{1,0:T(8,128)(2,1)S(1)}, bf16[20,256]{1,0:T(8,128)(2,1)S(1)}, u32[]{:S(2)}, u32[]{:S(2)}) %collective-permute-start.10) | collective-permute-done | bytes 10272 | tf_op jit(solution)/shard_map/ppermute | solution.py:537
  120.3 2.0 %collective-permute-start.12 = (bf16[20,256]{1,0:T(8,128)(2,1)S(1)}, bf16[20,256]{1,0:T(8,128)(2,1)S(1)}, u32[]{:S(2)}, u32[]{:S(2)}) collective-permute-start(bf16[20,256]{1,0:T(8,128)(2,1)S(1)} %add_convert_fusion.p0), channel_id=1, source_target_pairs={{0,192},{32,224},{64,0},{96,32},{128,64},{160,96},{192,128},{224,1... | collective-permute-start | bytes 30728 | tf_op jit(solution)/shard_map/ppermute | solution.py:534
  122.4 1.6 %collective-permute-start.13 = (bf16[20,256]{1,0:T(8,128)(2,1)S(1)}, bf16[20,256]{1,0:T(8,128)(2,1)S(1)}, u32[]{:S(2)}, u32[]{:S(2)}) collective-permute-start(bf16[20,256]{1,0:T(8,128)(2,1)S(1)} %add_convert_fusion.p0), channel_id=1, source_target_pairs={{0,128},{32,160},{64,192},{96,224},{128,0},{160,32},{192,64},{224,... | collective-permute-start | bytes 30728 | tf_op jit(solution)/shard_map/ppermute | solution.py:534
  124.0 0.1 collective-permute-done.11.pa
  124.0 0.1 collective-permute-done.12.pb
  124.2 3.4 %collective-permute-done.13.pc = bf16[20,256]{1,0:T(8,128)(2,1)S(1)} collective-permute-done((bf16[20,256]{1,0:T(8,128)(2,1)S(1)}, bf16[20,256]{1,0:T(8,128)(2,1)S(1)}, u32[]{:S(2)}, u32[]{:S(2)}) %collective-permute-start.13) | collective-permute-done | bytes 10272 | tf_op jit(solution)/shard_map/ppermute | solution.py:534
  127.6 0.6 tie.1
  128.2 0.7 copy-done.6
  128.9 9.5 %all-to-all-start.3 = ((bf16[32,16,256]{2,1,0:T(8,128)(2,1)}), bf16[32,16,256]{2,1,0:T(8,128)(2,1)S(1)}, u32[]{:S(2)}, u32[]{:S(2)}) async-start(bf16[32,16,256]{2,1,0:T(8,128)(2,1)} %copy-done.6), calls=%async_computation.3 | async-start | bytes 524288 | tf_op jit(solution)/shard_map/all_to_all | solution.py:540
  138.4 0.1 collective-permute-start.14
  138.5 1.3 collective-permute-done.14.refs_5_
  139.8 0.7 copy-done.7
  140.5 9.6 %all-to-all-done.3.refs_6_.refs_7_ = bf16[32,16,256]{2,1,0:T(8,128)(2,1)S(1)} async-done(((bf16[32,16,256]{2,1,0:T(8,128)(2,1)}), bf16[32,16,256]{2,1,0:T(8,128)(2,1)S(1)}, u32[]{:S(2)}, u32[]{:S(2)}) %all-to-all-start.3) | async-done | bytes 262176 | tf_op jit(solution)/shard_map/all_to_all | solution.py:540
  150.1 0.9 copy-done.8
  151.0 2.4 %finish.1 = (f32[4096,256]{1,0:T(8,128)}, f32[128,4096]{1,0:T(8,128)}, f32[256,256]{1,0:T(8,128)}, f32[256,512]{1,0:T(8,128)}) custom-call(bf16[2048,256]{1,0:T(8,128)(2,1)S(1)} %get-tuple-element.38.refs_0_, bf16[2048,256]{1,0:T(8,128)(2,1)S(1)} %collective-permute-done.8.refs_1_, ...), custom_call_target="tpu_custom_call", output_to_operand_aliasing={{0}: (8, {}), {1}: (9, {})} | custom-call | tf_op jit(solution)/shard_map/finish/pallas_call | solution.py:444
  (34 shorter events, 0.1 us)
Async XLA Ops:
  2.3 24.1 %all-to-all-start = ((bf16[32,32,128]{2,1,0:T(8,128)(2,1)}), bf16[32,32,128]{2,1,0:T(8,128)(2,1)S(1)}, u32[]{:S(2)}, u32[]{:S(2)}) async-start(bf16[32,32,128]{2,1,0:T(8,128)(2,1)} %pack.1), calls=%async_computation | async-start | bytes 524288 | tf_op jit(solution)/shard_map/all_to_all | solution.py:540
  15.4 0.9 copy-start.10
  17.0 13.8 %copy-start.9 = (bf16[256,512]{1,0:T(8,128)(2,1)S(1)}, bf16[256,512]{1,0:T(8,128)(2,1)}, u32[]{:S(2)}) copy-start(bf16[256,512]{1,0:T(8,128)(2,1)} %refs_4_.1) | copy-start | bytes 786436
  35.9 30.9 %copy-start.11 = (bf16[128,4096]{1,0:T(8,128)(2,1)S(1)}, bf16[128,4096]{1,0:T(8,128)(2,1)}, u32[]{:S(2)}) copy-start(bf16[128,4096]{1,0:T(8,128)(2,1)} %win_ref.1) | copy-start | bytes 3145732
  60.2 17.2 %all-to-all-start.2 = ((bf16[32,16,256]{2,1,0:T(8,128)(2,1)}), bf16[32,16,256]{2,1,0:T(8,128)(2,1)S(1)}, u32[]{:S(2)}, u32[]{:S(2)}) async-start(bf16[32,16,256]{2,1,0:T(8,128)(2,1)} %get-tuple-element.32), calls=%async_computation.2 | async-start | bytes 524288 | tf_op jit(solution)/shard_map/all_to_all | solution.py:540
  65.2 14.2 %collective-permute-start.3 = (bf16[512,256]{1,0:T(8,128)(2,1)S(1)}, bf16[512,256]{1,0:T(8,128)(2,1)S(1)}, u32[]{:S(2)}, u32[]{:S(2)}) collective-permute-start(bf16[512,256]{1,0:T(8,128)(2,1)S(1)} %get-tuple-element.33.t0), channel_id=1, source_target_pairs={{0,64},{32,96},{64,128},{96,160},{128,192},{160,224},{192,0},{224,... | collective-permute-start | bytes 786440 | tf_op jit(solution)/shard_map/ppermute | solution.py:534
  68.2 21.4 %collective-permute-start.4 = (bf16[512,256]{1,0:T(8,128)(2,1)S(1)}, bf16[512,256]{1,0:T(8,128)(2,1)S(1)}, u32[]{:S(2)}, u32[]{:S(2)}) collective-permute-start(bf16[512,256]{1,0:T(8,128)(2,1)S(1)} %get-tuple-element.33.t0), channel_id=1, source_target_pairs={{0,192},{32,224},{64,0},{96,32},{128,64},{160,96},{192,128},{224,1... | collective-permute-start | bytes 786440 | tf_op jit(solution)/shard_map/ppermute | solution.py:534
  68.6 20.9 %collective-permute-start.5 = (bf16[512,256]{1,0:T(8,128)(2,1)S(1)}, bf16[512,256]{1,0:T(8,128)(2,1)S(1)}, u32[]{:S(2)}, u32[]{:S(2)}) collective-permute-start(bf16[512,256]{1,0:T(8,128)(2,1)S(1)} %get-tuple-element.33.t0), channel_id=1, source_target_pairs={{0,128},{32,160},{64,192},{96,224},{128,0},{160,32},{192,64},{224,... | collective-permute-start | bytes 786440 | tf_op jit(solution)/shard_map/ppermute | solution.py:534
  77.4 12.1 %collective-permute-start = (bf16[512,256]{1,0:T(8,128)(2,1)S(1)}, bf16[512,256]{1,0:T(8,128)(2,1)S(1)}, u32[]{:S(2)}, u32[]{:S(2)}) collective-permute-start(bf16[512,256]{1,0:T(8,128)(2,1)S(1)} %bitcast.10), channel_id=1, source_target_pairs={{0,64},{32,96},{64,128},{96,160},{128,192},{160,224},{192,0},{224,... | collective-permute-start | bytes 786440 | tf_op jit(solution)/shard_map/ppermute | solution.py:534
  79.0 10.6 %collective-permute-start.1 = (bf16[512,256]{1,0:T(8,128)(2,1)S(1)}, bf16[512,256]{1,0:T(8,128)(2,1)S(1)}, u32[]{:S(2)}, u32[]{:S(2)}) collective-permute-start(bf16[512,256]{1,0:T(8,128)(2,1)S(1)} %bitcast.11), channel_id=1, source_target_pairs={{0,192},{32,224},{64,0},{96,32},{128,64},{160,96},{192,128},{224,1... | collective-permute-start | bytes 786440 | tf_op jit(solution)/shard_map/ppermute | solution.py:534
  79.5 10.1 %copy-start = (bf16[512,256]{1,0:T(8,128)(2,1)}, bf16[512,256]{1,0:T(8,128)(2,1)S(1)}, u32[]{:S(2)}) copy-start(bf16[512,256]{1,0:T(8,128)(2,1)S(1)} %collective-permute-done.3.refs_3_.ta) | copy-start | bytes 786436
  79.5 12.8 %collective-permute-start.2 = (bf16[512,256]{1,0:T(8,128)(2,1)S(1)}, bf16[512,256]{1,0:T(8,128)(2,1)S(1)}, u32[]{:S(2)}, u32[]{:S(2)}) collective-permute-start(bf16[512,256]{1,0:T(8,128)(2,1)S(1)} %bitcast.12), channel_id=1, source_target_pairs={{0,128},{32,160},{64,192},{96,224},{128,0},{160,32},{192,64},{224,... | collective-permute-start | bytes 786440 | tf_op jit(solution)/shard_map/ppermute | solution.py:534
  89.5 2.7 %copy-start.2 = (bf16[512,256]{1,0:T(8,128)(2,1)}, bf16[512,256]{1,0:T(8,128)(2,1)S(1)}, u32[]{:S(2)}) copy-start(bf16[512,256]{1,0:T(8,128)(2,1)S(1)} %collective-permute-done.4.refs_4_.tb) | copy-start | bytes 786436
  89.6 2.7 %copy-start.4 = (bf16[512,256]{1,0:T(8,128)(2,1)}, bf16[512,256]{1,0:T(8,128)(2,1)S(1)}, u32[]{:S(2)}) copy-start(bf16[512,256]{1,0:T(8,128)(2,1)S(1)} %collective-permute-done.5.refs_5_.tc) | copy-start | bytes 786436
  89.6 2.7 %copy-start.12 = (bf16[512,256]{1,0:T(8,128)(2,1)}, bf16[512,256]{1,0:T(8,128)(2,1)S(1)}, u32[]{:S(2)}) copy-start(bf16[512,256]{1,0:T(8,128)(2,1)S(1)} %collective-permute-done.refs_0_) | copy-start | bytes 786436
  89.6 2.6 %copy-start.13 = (bf16[512,256]{1,0:T(8,128)(2,1)}, bf16[512,256]{1,0:T(8,128)(2,1)S(1)}, u32[]{:S(2)}) copy-start(bf16[512,256]{1,0:T(8,128)(2,1)S(1)} %collective-permute-done.1.refs_1_) | copy-start | bytes 786436
  92.2 0.7 copy-start.14
  103.0 3.5 %collective-permute-start.6 = (bf16[2048,256]{1,0:T(8,128)(2,1)S(1)}, bf16[2048,256]{1,0:T(8,128)(2,1)S(1)}, u32[]{:S(2)}, u32[]{:S(2)}) collective-permute-start(bf16[2048,256]{1,0:T(8,128)(2,1)S(1)} %get-tuple-element.36.refs_10_), channel_id=1, source_target_pairs={{0,32},{32,0},{64,96},{96,64},{128,160},{160,128},{192,224},{224,1... | collective-permute-start | bytes 3145736 | tf_op jit(solution)/shard_map/ppermute | solution.py:537
  103.1 24.5 %copy-start.1 = (bf16[512,256]{1,0:T(8,128)(2,1)S(1)}, bf16[512,256]{1,0:T(8,128)(2,1)}, u32[]{:S(2)}) copy-start(bf16[512,256]{1,0:T(8,128)(2,1)} %copy-done) | copy-start | bytes 786436
  103.1 24.5 %copy-start.3 = (bf16[512,256]{1,0:T(8,128)(2,1)S(1)}, bf16[512,256]{1,0:T(8,128)(2,1)}, u32[]{:S(2)}) copy-start(bf16[512,256]{1,0:T(8,128)(2,1)} %copy-done.2) | copy-start | bytes 786436
  103.1 24.5 %copy-start.5 = (bf16[512,256]{1,0:T(8,128)(2,1)S(1)}, bf16[512,256]{1,0:T(8,128)(2,1)}, u32[]{:S(2)}) copy-start(bf16[512,256]{1,0:T(8,128)(2,1)} %copy-done.4) | copy-start | bytes 786436
  103.1 3.4 %collective-permute-start.7 = (bf16[128,2048]{1,0:T(8,128)(2,1)S(1)}, bf16[128,2048]{1,0:T(8,128)(2,1)S(1)}, u32[]{:S(2)}, u32[]{:S(2)}) collective-permute-start(bf16[128,2048]{1,0:T(8,128)(2,1)S(1)} %get-tuple-element.37.refs_12_), channel_id=1, source_target_pairs={{0,32},{32,0},{64,96},{96,64},{128,160},{160,128},{192,224},{224,1... | collective-permute-start | bytes 1572872 | tf_op jit(solution)/shard_map/ppermute | solution.py:537
  117.6 32.5 %collective-permute-start.8 = (bf16[2048,256]{1,0:T(8,128)(2,1)S(1)}, bf16[2048,256]{1,0:T(8,128)(2,1)S(1)}, u32[]{:S(2)}, u32[]{:S(2)}) collective-permute-start(bf16[2048,256]{1,0:T(8,128)(2,1)S(1)} %get-tuple-element.38.refs_0_), channel_id=1, source_target_pairs={{0,32},{32,0},{64,96},{96,64},{128,160},{160,128},{192,224},{224,1... | collective-permute-start | bytes 3145736 | tf_op jit(solution)/shard_map/ppermute | solution.py:537
  117.8 2.5 %collective-permute-start.10 = (bf16[20,256]{1,0:T(8,128)(2,1)S(1)}, bf16[20,256]{1,0:T(8,128)(2,1)S(1)}, u32[]{:S(2)}, u32[]{:S(2)}) collective-permute-start(bf16[20,256]{1,0:T(8,128)(2,1)S(1)} %get-tuple-element.40), channel_id=1, source_target_pairs={{0,32},{32,0},{64,96},{96,64},{128,160},{160,128},{192,224},{224,1... | collective-permute-start | bytes 30728 | tf_op jit(solution)/shard_map/ppermute | solution.py:537
  118.2 32.0 %collective-permute-start.9 = (bf16[128,2048]{1,0:T(8,128)(2,1)S(1)}, bf16[128,2048]{1,0:T(8,128)(2,1)S(1)}, u32[]{:S(2)}, u32[]{:S(2)}) collective-permute-start(bf16[128,2048]{1,0:T(8,128)(2,1)S(1)} %get-tuple-element.39.refs_2_), channel_id=1, source_target_pairs={{0,32},{32,0},{64,96},{96,64},{128,160},{160,128},{192,224},{224,1... | collective-permute-start | bytes 1572872 | tf_op jit(solution)/shard_map/ppermute | solution.py:537
  120.3 3.7 %collective-permute-start.11 = (bf16[20,256]{1,0:T(8,128)(2,1)S(1)}, bf16[20,256]{1,0:T(8,128)(2,1)S(1)}, u32[]{:S(2)}, u32[]{:S(2)}) collective-permute-start(bf16[20,256]{1,0:T(8,128)(2,1)S(1)} %add_convert_fusion.p0), channel_id=1, source_target_pairs={{0,64},{32,96},{64,128},{96,160},{128,192},{160,224},{192,0},{224,... | collective-permute-start | bytes 30728 | tf_op jit(solution)/shard_map/ppermute | solution.py:534
  120.3 3.8 %collective-permute-start.12 = (bf16[20,256]{1,0:T(8,128)(2,1)S(1)}, bf16[20,256]{1,0:T(8,128)(2,1)S(1)}, u32[]{:S(2)}, u32[]{:S(2)}) collective-permute-start(bf16[20,256]{1,0:T(8,128)(2,1)S(1)} %add_convert_fusion.p0), channel_id=1, source_target_pairs={{0,192},{32,224},{64,0},{96,32},{128,64},{160,96},{192,128},{224,1... | collective-permute-start | bytes 30728 | tf_op jit(solution)/shard_map/ppermute | solution.py:534
  122.4 5.2 %collective-permute-start.13 = (bf16[20,256]{1,0:T(8,128)(2,1)S(1)}, bf16[20,256]{1,0:T(8,128)(2,1)S(1)}, u32[]{:S(2)}, u32[]{:S(2)}) collective-permute-start(bf16[20,256]{1,0:T(8,128)(2,1)S(1)} %add_convert_fusion.p0), channel_id=1, source_target_pairs={{0,128},{32,160},{64,192},{96,224},{128,0},{160,32},{192,64},{224,... | collective-permute-start | bytes 30728 | tf_op jit(solution)/shard_map/ppermute | solution.py:534
  128.2 0.7 copy-start.6
  128.9 21.2 %all-to-all-start.3 = ((bf16[32,16,256]{2,1,0:T(8,128)(2,1)}), bf16[32,16,256]{2,1,0:T(8,128)(2,1)S(1)}, u32[]{:S(2)}, u32[]{:S(2)}) async-start(bf16[32,16,256]{2,1,0:T(8,128)(2,1)} %copy-done.6), calls=%async_computation.3 | async-start | bytes 524288 | tf_op jit(solution)/shard_map/all_to_all | solution.py:540
  138.4 1.4 collective-permute-start.14
  139.8 0.7 copy-start.7
  150.1 0.9 copy-start.8

commit v3 on v2

--- a/solution.py
+++ b/solution.py
@@ -324,30 +324,31 @@
     gin_ref[...] = mm(d_pre, feats).T
 
 
-def dense_own(d, feats, win_t, tower_out, each):
-    wide, width = tower_out.shape
+def dense_own(d, feats, win_t, tower_out, each, first, units):
+    width = tower_out.shape[1]
     uf = win_t.shape[1]
     reqs = each * feats.shape[0]
     block = 1024
+    base = first // block
     return pl.pallas_call(
         own_kernel,
-        grid=(wide // block,),
+        grid=(units // block,),
         in_specs=[
             feats_spec(d, each, width),
             feats_spec(feats, each, uf),
-            pl.BlockSpec((block, uf), lambda i: (i, 0)),
-            pl.BlockSpec((block, width), lambda i: (i, 0)),
+            pl.BlockSpec((block, uf), lambda i: (base + i, 0)),
+            pl.BlockSpec((block, width), lambda i: (base + i, 0)),
         ],
         out_specs=(
             pl.BlockSpec((block, width), lambda i: (i, 0)),
             pl.BlockSpec((uf, block), lambda i: (0, i)),
         ),
-        out_shape=(pltpu.HBM((wide, width), F32), pltpu.HBM((uf, wide), F32)),
+        out_shape=(pltpu.HBM((units, width), F32), pltpu.HBM((uf, units), F32)),
         compiler_params=pltpu.CompilerParams(vmem_limit_bytes=28 << 20),
         cost_estimate=pl.CostEstimate(
-            flops=2 * reqs * wide * (2 * width + 2 * uf),
+            flops=2 * reqs * units * (2 * width + 2 * uf),
             bytes_accessed=10 << 20,
-            transcendentals=reqs * wide,
+            transcendentals=reqs * units,
         ),
         name="dense_own",
     )(d, feats, hbm(win_t), hbm(tower_out))
@@ -399,8 +400,8 @@
         + [
             pl.BlockSpec((block, uf), lambda i: (base + i, 0)),
             pl.BlockSpec((block, width), lambda i: (base + i, 0)),
-            pl.BlockSpec((block, width), lambda i: (base + i, 0)),
-            pl.BlockSpec((uf, block), lambda i: (0, base + i)),
+            out_spec,
+            in_spec,
         ]
         + ([out_spec] * 2 + [in_spec] * 2 if pieces else []),
         out_specs=(out_spec, in_spec) * (2 if pieces else 1),
@@ -465,7 +466,7 @@
         input_output_aliases={8: 0, 9: 1},
         compiler_params=pltpu.CompilerParams(vmem_limit_bytes=12 << 20),
         name="finish",
-    )(*pieces, column, other, inter, inter, *before)
+    )(*pieces, hbm(column), hbm(other), inter, inter, *before)
 
 
 def pack_kernel(feats_ref, req_ref, lab_ref, live_ref, out_ref):
@@ -555,15 +556,17 @@
     pair = (part.astype(F32) + swap(part).astype(F32)).astype(BF)
     parts = [pair] + from_chips(pair)
     d_far = from_chips(third.reshape(reqs, width))
-    before = dense_own(third, arrived, win_t, tower_out, each)
-    inter_part, grad_out, column = tie(parts, [share] + far, hbm(before[1]), shards, each)
+    units = tower_out.shape[0] // 2
+    before = []
+    for k in range(2):
+        before.append(dense_own(third, arrived, win_t, tower_out, each, k * units, units))
+    inter_part, grad_out, column = tie(parts, [share] + far, hbm(before[0][1]), shards, each)
     inter_all = exchange(inter_part)
     other = swap(column)
-    units = tower_out.shape[0] // 2
     pieces = None
     for k in range(2):
         g_out, g_in, *first = dense_far(
-            d_far, far, win_t, tower_out, before, k * units, units, pieces
+            d_far, far, win_t, tower_out, before[k], k * units, units, pieces
         )
         pieces = (g_out, swap(g_out), g_in, swap(g_in))
     sums = finish(pieces, column, other, inter_all, first, units)

time: 154 us -> 156 us (1.013)
  Pallas kernels: 44.6 us -> 48.1 us
  local copies, waits for them, and re-layouts: 6.98 us -> 5.42 us
    ppermute x6, waiting for transfers between devices: 6.27 us -> 3.54 us  [swap(): return lax.ppermute(x, 'grp', ring(0, 1))]
    all_to_all x3, waiting for transfers between devices: 25.6 us -> 27.8 us  [exchange(): return lax.all_to_all(x, 'tbl', split_axis=0, concat_axis=0, tiled=True)]
    pallas_call x1 -> x2, Pallas kernels: 7.78 us -> 9.67 us  [dense_own(): pl.pallas_call(own_kernel, grid=(units // block,), in_specs=[feats_spec(d...]
    unnamed x31 -> x33, local copies, waits for them, and re-layouts: 5.21 us -> 3.66 us
  transfers between devices with their start and end apart: 18 -> 18, of which waited for: 10 -> 10; matrix products, arithmetic and copies ran while one was open for 2% -> 2% of each run, Pallas kernels for 6% -> 7%
where the time goes in v3:
time: 156 us; the launch traced here: 155 us
  Pallas kernels  48.1 us (31%)
  starting transfers between devices  40.1 us (26%)
  waiting for transfers between devices  36.9 us (24%)
  blocking collectives  23.4 us (15%)
  local copies, waits for them, and re-layouts  5.42 us (3%)
    all_to_all x3, waiting for transfers between devices, exchange(): return lax.all_to_all(x, 'tbl', split_axis=0, concat_axis=0, tiled=True)  27.8 us
    all_to_all x3, starting transfers between devices, exchange(): return lax.all_to_all(x, 'tbl', split_axis=0, concat_axis=0, tiled=True)  25.8 us
    all_to_all x1, blocking collectives, exchange(): return lax.all_to_all(x, 'tbl', split_axis=0, concat_axis=0, tiled=True)  23.4 us
    pallas_call x2, Pallas kernels, dense_far(): pl.pallas_call(lambda *refs: far_kernel(count, pieces is not None, *refs)...  21.5 us
    ppermute x9, starting transfers between devices, from_chips(): return [lax.ppermute(x, 'grp', ring(turn, 0)) for turn in (1, chips - 1, 2)]  12.9 us
    pallas_call x2, Pallas kernels, dense_own(): pl.pallas_call(own_kernel, grid=(units // block,), in_specs=[feats_spec(d...  9.67 us
    ppermute x9, waiting for transfers between devices, from_chips(): return [lax.ppermute(x, 'grp', ring(turn, 0)) for turn in (1, chips - 1, 2)]  5.59 us
    pallas_call x1, Pallas kernels, rank(): pl.pallas_call(lambda *refs: rank_kernel(factor, slots, *refs), out_shape...  5.09 us
  transfers between devices with their start and end apart: 18, of which 10 were waited for; matrix products, arithmetic and copies ran while one was open for 2% of the time, Pallas kernels for 7%

profile of v3, /device:TPU:8, one launch (start us, length us, event | category | flops | bytes accessed | tf_op | source)
XLA Modules:
  0.0 154.7 jit_solution(11473302403590868206)
XLA Ops:
  0.6 1.7 %pack.1 = bf16[32,32,128]{2,1,0:T(8,128)(2,1)} custom-call(bf16[16,128]{1,0:T(8,128)(2,1)} %feats_ref.1, s32[32,32]{1,0:T(8,128)} %bitcast.18, f32[32,32]{1,0:T(8,128)} %bitcast.19, s32[1,32]{1,0:T(1,128)} %live_ref.1), custom_call_target="tpu_custom_call" | custom-call | tf_op jit(solution)/shard_map/pack/pallas_call | solution.py:508
  2.3 11.3 %all-to-all-start = ((bf16[32,32,128]{2,1,0:T(8,128)(2,1)}), bf16[32,32,128]{2,1,0:T(8,128)(2,1)S(1)}, u32[]{:S(2)}, u32[]{:S(2)}) async-start(bf16[32,32,128]{2,1,0:T(8,128)(2,1)} %pack.1), calls=%async_computation | async-start | bytes 524288 | tf_op jit(solution)/shard_map/all_to_all | solution.py:541
  13.6 0.8 copy.20
  14.5 0.1 reshape.21.ids_ref
  14.6 0.8 copy.21.refs_5_
  15.4 0.9 copy-done.11
  16.3 0.7 pool.1
  17.0 9.4 %all-to-all-done.feats_ref.refs_3_ = bf16[32,32,128]{2,1,0:T(8,128)(2,1)S(1)} async-done(((bf16[32,32,128]{2,1,0:T(8,128)(2,1)}), bf16[32,32,128]{2,1,0:T(8,128)(2,1)S(1)}, u32[]{:S(2)}, u32[]{:S(2)}) %all-to-all-start) | async-done | bytes 262176 | tf_op jit(solution)/shard_map/all_to_all | solution.py:541
  26.5 4.4 %users.1.refs_0_ = bf16[256,512]{1,0:T(8,128)(2,1)S(1)} custom-call(bf16[32,32,128]{2,1,0:T(8,128)(2,1)S(1)} %all-to-all-done.feats_ref.refs_3_, bf16[128,4096]{1,0:T(8,128)(2,1)} %win_ref.1, bf16[4096,256]{1,0:T(8,128)(2,1)} %refs_7_.3), custom_call_target="tpu_custom_call" | custom-call | flops 1610612736 | bytes 4194304 | tf_op jit(solution)/shard_map/users/pallas_call | solution.py:96
  30.8 5.1 %rank.1 = (bf16[32,36,256]{2,1,0:T(8,128)(2,1)S(1)}, bf16[512,256]{1,0:T(8,128)(2,1)S(1)}) custom-call(bf16[256,512]{1,0:T(8,128)(2,1)S(1)} %users.1.refs_0_, bf16[256,1024]{1,0:T(8,128)(2,1)S(1)} %get-tuple-element.30.refs_1_, bf16[256,1024]{1,0:T(8,128)(2,1)S(1)} %get-tuple-element.31.refs_2_, bf16[32,32,128]{2,1,0:T(8,128)(2,1)S(1)} %all-to-all-done.feats_ref.refs_3_, ...), custom_call_target="tpu_custom_call" | custom-call | flops 1476395008 | bytes 4194304 | tf_op jit(solution)/shard_map/rank/pallas_call | solution.py:228
  36.0 23.4 %all_to_all.20.back_ref = bf16[32,36,256]{2,1,0:T(8,128)(2,1)S(1)} all-to-all(bf16[32,36,256]{2,1,0:T(8,128)(2,1)S(1)} %get-tuple-element.32), channel_id=1, replica_groups=mesh['grp'=8,'tbl'=32] {'tbl'}, dimensions={0} | all-to-all | bytes 1179648 | tf_op jit(solution)/shard_map/all_to_all | solution.py:541
  59.3 0.9 fold.1
  60.2 5.0 %all-to-all-start.2 = ((bf16[32,16,256]{2,1,0:T(8,128)(2,1)}), bf16[32,16,256]{2,1,0:T(8,128)(2,1)S(1)}, u32[]{:S(2)}, u32[]{:S(2)}) async-start(bf16[32,16,256]{2,1,0:T(8,128)(2,1)} %get-tuple-element.34), calls=%async_computation.2 | async-start | bytes 524288 | tf_op jit(solution)/shard_map/all_to_all | solution.py:541
  65.2 2.4 %collective-permute-start.5 = (bf16[512,256]{1,0:T(8,128)(2,1)S(1)}, bf16[512,256]{1,0:T(8,128)(2,1)S(1)}, u32[]{:S(2)}, u32[]{:S(2)}) collective-permute-start(bf16[512,256]{1,0:T(8,128)(2,1)S(1)} %get-tuple-element.35.t0), channel_id=1, source_target_pairs={{0,128},{32,160},{64,192},{96,224},{128,0},{160,32},{192,64},{224,... | collective-permute-start | bytes 786440 | tf_op jit(solution)/shard_map/ppermute | solution.py:535
  67.6 1.3 collective-permute-start.4
  69.0 0.7 collective-permute-start.3
  69.6 7.8 %all-to-all-done.2.d_ref = bf16[32,16,256]{2,1,0:T(8,128)(2,1)S(1)} async-done(((bf16[32,16,256]{2,1,0:T(8,128)(2,1)}), bf16[32,16,256]{2,1,0:T(8,128)(2,1)S(1)}, u32[]{:S(2)}, u32[]{:S(2)}) %all-to-all-start.2) | async-done | bytes 262176 | tf_op jit(solution)/shard_map/all_to_all | solution.py:541
  77.4 2.3 %collective-permute-start.2 = (bf16[512,256]{1,0:T(8,128)(2,1)S(1)}, bf16[512,256]{1,0:T(8,128)(2,1)S(1)}, u32[]{:S(2)}, u32[]{:S(2)}) collective-permute-start(bf16[512,256]{1,0:T(8,128)(2,1)S(1)} %bitcast.10), channel_id=1, source_target_pairs={{0,128},{32,160},{64,192},{96,224},{128,0},{160,32},{192,64},{224,... | collective-permute-start | bytes 786440 | tf_op jit(solution)/shard_map/ppermute | solution.py:535
  79.7 1.3 collective-permute-start.1
  81.1 0.7 collective-permute-start
  81.8 1.3 copy.22
  83.1 4.9 %dense_own.3 = (f32[2048,256]{1,0:T(8,128)}, f32[128,2048]{1,0:T(8,128)}) custom-call(bf16[32,16,256]{2,1,0:T(8,128)(2,1)S(1)} %all-to-all-done.2.d_ref, bf16[32,32,128]{2,1,0:T(8,128)(2,1)S(1)} %all-to-all-done.feats_ref.refs_3_, bf16[4096,128]{1,0:T(8,128)(2,1)} %bitcast.13, bf16[4096,256]{1,0:T(8,128)(2,1)} %refs_7_.3), custom_call_target="tpu_custom_call" | custom-call | flops 1610612736 | bytes 10485760 | tf_op jit(solution)/shard_map/dense_own/pallas_call | solution.py:333
  88.0 2.5 %collective-permute-done.1.refs_1_ = bf16[512,256]{1,0:T(8,128)(2,1)S(1)} collective-permute-done((bf16[512,256]{1,0:T(8,128)(2,1)S(1)}, bf16[512,256]{1,0:T(8,128)(2,1)S(1)}, u32[]{:S(2)}, u32[]{:S(2)}) %collective-permute-start.1) | collective-permute-done | bytes 262176 | tf_op jit(solution)/shard_map/ppermute | solution.py:535
  90.4 0.2 collective-permute-done.refs_0_
  90.6 0.5 copy-done.14
  91.2 0.2 copy-done.15
  91.4 10.0 %dense_far.2 = (bf16[2048,256]{1,0:T(8,128)(2,1)S(1)}, bf16[128,2048]{1,0:T(8,128)(2,1)S(1)}) custom-call(bf16[512,256]{1,0:T(8,128)(2,1)} %copy-done.15, bf16[512,256]{1,0:T(8,128)(2,1)} %copy-done.14, bf16[512,256]{1,0:T(8,128)(2,1)} %copy-done.13, bf16[512,256]{1,0:T(8,128)(2,1)} %copy-done.7, bf16[512,256]{1,0:T(8,128)(2,1)} %copy-done.5, ...), custom_call_target="tpu_custom_call" | custom-call | flops 4831838208 | bytes 10485760 | tf_op jit(solution)/shard_map/dense_far/pallas_call | solution.py:395
  101.4 0.1 collective-permute-start.6
  101.5 0.5 collective-permute-start.7
  102.0 4.8 %dense_own.2 = (f32[2048,256]{1,0:T(8,128)}, f32[128,2048]{1,0:T(8,128)}) custom-call(bf16[32,16,256]{2,1,0:T(8,128)(2,1)S(1)} %all-to-all-done.2.d_ref, bf16[32,32,128]{2,1,0:T(8,128)(2,1)S(1)} %all-to-all-done.feats_ref.refs_3_, bf16[4096,128]{1,0:T(8,128)(2,1)} %bitcast.15, bf16[4096,256]{1,0:T(8,128)(2,1)} %refs_7_.3), custom_call_target="tpu_custom_call" | custom-call | flops 1610612736 | bytes 10485760 | tf_op jit(solution)/shard_map/dense_own/pallas_call | solution.py:333
  106.9 11.5 %dense_far.3 = (bf16[2048,256]{1,0:T(8,128)(2,1)S(1)}, bf16[128,2048]{1,0:T(8,128)(2,1)S(1)}, f32[4096,256]{1,0:T(8,128)}, f32[128,4096]{1,0:T(8,128)}) custom-call(bf16[512,256]{1,0:T(8,128)(2,1)} %copy-done.15, bf16[512,256]{1,0:T(8,128)(2,1)} %copy-done.14, bf16[512,256]{1,0:T(8,128)(2,1)} %copy-done.13, bf16[512,256]{1,0:T(8,128)(2,1)} %copy-done.7, ...), custom_call_target="tpu_custom_call" | custom-call | flops 4831838208 | bytes 10485760 | tf_op jit(solution)/shard_map/dense_far/pallas_call | solution.py:395
  118.3 0.1 collective-permute-start.8
  118.5 0.4 collective-permute-start.10
  118.9 0.1 collective-permute-start.9
  119.0 2.1 %collective-permute-done.10 = bf16[20,256]{1,0:T(8,128)(2,1)S(1)} collective-permute-done((bf16[20,256]{1,0:T(8,128)(2,1)S(1)}, bf16[20,256]{1,0:T(8,128)(2,1)S(1)}, u32[]{:S(2)}, u32[]{:S(2)}) %collective-permute-start.10) | collective-permute-done | bytes 10272 | tf_op jit(solution)/shard_map/ppermute | solution.py:538
  121.1 2.2 %collective-permute-start.13 = (bf16[20,256]{1,0:T(8,128)(2,1)S(1)}, bf16[20,256]{1,0:T(8,128)(2,1)S(1)}, u32[]{:S(2)}, u32[]{:S(2)}) collective-permute-start(bf16[20,256]{1,0:T(8,128)(2,1)S(1)} %add_convert_fusion.p0), channel_id=1, source_target_pairs={{0,128},{32,160},{64,192},{96,224},{128,0},{160,32},{192,64},{224,... | collective-permute-start | bytes 30728 | tf_op jit(solution)/shard_map/ppermute | solution.py:535
  123.2 1.3 collective-permute-start.12
  124.5 0.8 collective-permute-start.11
  125.3 1.0 collective-permute-done.13.pc
  126.3 0.7 collective-permute-done.12.pb
  126.9 1.3 collective-permute-done.11.pa
  128.2 0.6 tie.1
  128.8 0.7 copy-done
  129.5 9.5 %all-to-all-start.3 = ((bf16[32,16,256]{2,1,0:T(8,128)(2,1)}), bf16[32,16,256]{2,1,0:T(8,128)(2,1)S(1)}, u32[]{:S(2)}, u32[]{:S(2)}) async-start(bf16[32,16,256]{2,1,0:T(8,128)(2,1)} %copy-done), calls=%async_computation.3 | async-start | bytes 524288 | tf_op jit(solution)/shard_map/all_to_all | solution.py:541
  139.0 0.1 collective-permute-start.14
  139.1 1.5 collective-permute-done.14.refs_5_
  140.6 10.5 %all-to-all-done.3.refs_6_.refs_7_ = bf16[32,16,256]{2,1,0:T(8,128)(2,1)S(1)} async-done(((bf16[32,16,256]{2,1,0:T(8,128)(2,1)}), bf16[32,16,256]{2,1,0:T(8,128)(2,1)S(1)}, u32[]{:S(2)}, u32[]{:S(2)}) %all-to-all-start.3) | async-done | bytes 262176 | tf_op jit(solution)/shard_map/all_to_all | solution.py:541
  151.1 3.6 %finish.1 = (f32[4096,256]{1,0:T(8,128)}, f32[128,4096]{1,0:T(8,128)}, f32[256,256]{1,0:T(8,128)}, f32[256,512]{1,0:T(8,128)}) custom-call(bf16[2048,256]{1,0:T(8,128)(2,1)S(1)} %get-tuple-element.42.refs_0_, bf16[2048,256]{1,0:T(8,128)(2,1)S(1)} %collective-permute-done.8.refs_1_, ...), custom_call_target="tpu_custom_call", output_to_operand_aliasing={{0}: (8, {}), {1}: (9, {})} | custom-call | tf_op jit(solution)/shard_map/finish/pallas_call | solution.py:445
  (37 shorter events, 0.1 us)
Async XLA Ops:
  2.3 24.1 %all-to-all-start = ((bf16[32,32,128]{2,1,0:T(8,128)(2,1)}), bf16[32,32,128]{2,1,0:T(8,128)(2,1)S(1)}, u32[]{:S(2)}, u32[]{:S(2)}) async-start(bf16[32,32,128]{2,1,0:T(8,128)(2,1)} %pack.1), calls=%async_computation | async-start | bytes 524288 | tf_op jit(solution)/shard_map/all_to_all | solution.py:541
  15.4 0.9 copy-start.11
  17.0 13.8 %copy-start.10 = (bf16[256,512]{1,0:T(8,128)(2,1)S(1)}, bf16[256,512]{1,0:T(8,128)(2,1)}, u32[]{:S(2)}) copy-start(bf16[256,512]{1,0:T(8,128)(2,1)} %refs_4_.1) | copy-start | bytes 786436
  35.9 47.1 %copy-start.1 = (bf16[512,256]{1,0:T(8,128)(2,1)}, bf16[512,256]{1,0:T(8,128)(2,1)S(1)}, u32[]{:S(2)}) copy-start(bf16[512,256]{1,0:T(8,128)(2,1)S(1)} %get-tuple-element.35.t0) | copy-start | bytes 786436
  35.9 45.8 %copy-start.12 = (bf16[128,4096]{1,0:T(8,128)(2,1)S(1)}, bf16[128,4096]{1,0:T(8,128)(2,1)}, u32[]{:S(2)}) copy-start(bf16[128,4096]{1,0:T(8,128)(2,1)} %win_ref.1) | copy-start | bytes 3145732
  60.2 17.2 %all-to-all-start.2 = ((bf16[32,16,256]{2,1,0:T(8,128)(2,1)}), bf16[32,16,256]{2,1,0:T(8,128)(2,1)S(1)}, u32[]{:S(2)}, u32[]{:S(2)}) async-start(bf16[32,16,256]{2,1,0:T(8,128)(2,1)} %get-tuple-element.34), calls=%async_computation.2 | async-start | bytes 524288 | tf_op jit(solution)/shard_map/all_to_all | solution.py:541
  65.2 15.9 %collective-permute-start.5 = (bf16[512,256]{1,0:T(8,128)(2,1)S(1)}, bf16[512,256]{1,0:T(8,128)(2,1)S(1)}, u32[]{:S(2)}, u32[]{:S(2)}) collective-permute-start(bf16[512,256]{1,0:T(8,128)(2,1)S(1)} %get-tuple-element.35.t0), channel_id=1, source_target_pairs={{0,128},{32,160},{64,192},{96,224},{128,0},{160,32},{192,64},{224,... | collective-permute-start | bytes 786440 | tf_op jit(solution)/shard_map/ppermute | solution.py:535
  67.6 20.3 %collective-permute-start.4 = (bf16[512,256]{1,0:T(8,128)(2,1)S(1)}, bf16[512,256]{1,0:T(8,128)(2,1)S(1)}, u32[]{:S(2)}, u32[]{:S(2)}) collective-permute-start(bf16[512,256]{1,0:T(8,128)(2,1)S(1)} %get-tuple-element.35.t0), channel_id=1, source_target_pairs={{0,192},{32,224},{64,0},{96,32},{128,64},{160,96},{192,128},{224,1... | collective-permute-start | bytes 786440 | tf_op jit(solution)/shard_map/ppermute | solution.py:535
  69.0 19.0 %collective-permute-start.3 = (bf16[512,256]{1,0:T(8,128)(2,1)S(1)}, bf16[512,256]{1,0:T(8,128)(2,1)S(1)}, u32[]{:S(2)}, u32[]{:S(2)}) collective-permute-start(bf16[512,256]{1,0:T(8,128)(2,1)S(1)} %get-tuple-element.35.t0), channel_id=1, source_target_pairs={{0,64},{32,96},{64,128},{96,160},{128,192},{160,224},{192,0},{224,... | collective-permute-start | bytes 786440 | tf_op jit(solution)/shard_map/ppermute | solution.py:535
  77.4 10.5 %collective-permute-start.2 = (bf16[512,256]{1,0:T(8,128)(2,1)S(1)}, bf16[512,256]{1,0:T(8,128)(2,1)S(1)}, u32[]{:S(2)}, u32[]{:S(2)}) collective-permute-start(bf16[512,256]{1,0:T(8,128)(2,1)S(1)} %bitcast.10), channel_id=1, source_target_pairs={{0,128},{32,160},{64,192},{96,224},{128,0},{160,32},{192,64},{224,... | collective-permute-start | bytes 786440 | tf_op jit(solution)/shard_map/ppermute | solution.py:535
  79.7 10.7 %collective-permute-start.1 = (bf16[512,256]{1,0:T(8,128)(2,1)S(1)}, bf16[512,256]{1,0:T(8,128)(2,1)S(1)}, u32[]{:S(2)}, u32[]{:S(2)}) collective-permute-start(bf16[512,256]{1,0:T(8,128)(2,1)S(1)} %bitcast.11), channel_id=1, source_target_pairs={{0,192},{32,224},{64,0},{96,32},{128,64},{160,96},{192,128},{224,1... | collective-permute-start | bytes 786440 | tf_op jit(solution)/shard_map/ppermute | solution.py:535
  81.1 6.8 %copy-start.3 = (bf16[512,256]{1,0:T(8,128)(2,1)}, bf16[512,256]{1,0:T(8,128)(2,1)S(1)}, u32[]{:S(2)}) copy-start(bf16[512,256]{1,0:T(8,128)(2,1)S(1)} %collective-permute-done.5.refs_5_.tc) | copy-start | bytes 786436
  81.1 9.6 %collective-permute-start = (bf16[512,256]{1,0:T(8,128)(2,1)S(1)}, bf16[512,256]{1,0:T(8,128)(2,1)S(1)}, u32[]{:S(2)}, u32[]{:S(2)}) collective-permute-start(bf16[512,256]{1,0:T(8,128)(2,1)S(1)} %bitcast.12), channel_id=1, source_target_pairs={{0,64},{32,96},{64,128},{96,160},{128,192},{160,224},{192,0},{224,... | collective-permute-start | bytes 786440 | tf_op jit(solution)/shard_map/ppermute | solution.py:535
  87.9 3.4 %copy-start.5 = (bf16[512,256]{1,0:T(8,128)(2,1)}, bf16[512,256]{1,0:T(8,128)(2,1)S(1)}, u32[]{:S(2)}) copy-start(bf16[512,256]{1,0:T(8,128)(2,1)S(1)} %collective-permute-done.4.refs_4_.tb) | copy-start | bytes 786436
  88.0 3.4 %copy-start.7 = (bf16[512,256]{1,0:T(8,128)(2,1)}, bf16[512,256]{1,0:T(8,128)(2,1)S(1)}, u32[]{:S(2)}) copy-start(bf16[512,256]{1,0:T(8,128)(2,1)S(1)} %collective-permute-done.3.refs_3_.ta) | copy-start | bytes 786436
  88.0 3.4 %copy-start.13 = (bf16[512,256]{1,0:T(8,128)(2,1)}, bf16[512,256]{1,0:T(8,128)(2,1)S(1)}, u32[]{:S(2)}) copy-start(bf16[512,256]{1,0:T(8,128)(2,1)S(1)} %collective-permute-done.2.refs_2_) | copy-start | bytes 786436
  90.4 0.7 copy-start.14
  90.6 0.7 copy-start.15
  101.4 5.4 %collective-permute-start.6 = (bf16[2048,256]{1,0:T(8,128)(2,1)S(1)}, bf16[2048,256]{1,0:T(8,128)(2,1)S(1)}, u32[]{:S(2)}, u32[]{:S(2)}) collective-permute-start(bf16[2048,256]{1,0:T(8,128)(2,1)S(1)} %get-tuple-element.40.refs_10_), channel_id=1, source_target_pairs={{0,32},{32,0},{64,96},{96,64},{128,160},{160,128},{192,224},{224,1... | collective-permute-start | bytes 3145736 | tf_op jit(solution)/shard_map/ppermute | solution.py:538
  101.5 5.3 %collective-permute-start.7 = (bf16[128,2048]{1,0:T(8,128)(2,1)S(1)}, bf16[128,2048]{1,0:T(8,128)(2,1)S(1)}, u32[]{:S(2)}, u32[]{:S(2)}) collective-permute-start(bf16[128,2048]{1,0:T(8,128)(2,1)S(1)} %get-tuple-element.41.refs_12_), channel_id=1, source_target_pairs={{0,32},{32,0},{64,96},{96,64},{128,160},{160,128},{192,224},{224,1... | collective-permute-start | bytes 1572872 | tf_op jit(solution)/shard_map/ppermute | solution.py:538
  106.8 21.4 %copy-start.2 = (bf16[512,256]{1,0:T(8,128)(2,1)S(1)}, bf16[512,256]{1,0:T(8,128)(2,1)}, u32[]{:S(2)}) copy-start(bf16[512,256]{1,0:T(8,128)(2,1)} %copy-done.1) | copy-start | bytes 786436
  106.8 21.4 %copy-start.4 = (bf16[512,256]{1,0:T(8,128)(2,1)S(1)}, bf16[512,256]{1,0:T(8,128)(2,1)}, u32[]{:S(2)}) copy-start(bf16[512,256]{1,0:T(8,128)(2,1)} %copy-done.3) | copy-start | bytes 786436
  106.8 21.4 %copy-start.6 = (bf16[512,256]{1,0:T(8,128)(2,1)S(1)}, bf16[512,256]{1,0:T(8,128)(2,1)}, u32[]{:S(2)}) copy-start(bf16[512,256]{1,0:T(8,128)(2,1)} %copy-done.5) | copy-start | bytes 786436
  106.9 21.3 %copy-start.8 = (bf16[512,256]{1,0:T(8,128)(2,1)S(1)}, bf16[512,256]{1,0:T(8,128)(2,1)}, u32[]{:S(2)}) copy-start(bf16[512,256]{1,0:T(8,128)(2,1)} %copy-done.7) | copy-start | bytes 786436
  118.3 32.8 %collective-permute-start.8 = (bf16[2048,256]{1,0:T(8,128)(2,1)S(1)}, bf16[2048,256]{1,0:T(8,128)(2,1)S(1)}, u32[]{:S(2)}, u32[]{:S(2)}) collective-permute-start(bf16[2048,256]{1,0:T(8,128)(2,1)S(1)} %get-tuple-element.42.refs_0_), channel_id=1, source_target_pairs={{0,32},{32,0},{64,96},{96,64},{128,160},{160,128},{192,224},{224,1... | collective-permute-start | bytes 3145736 | tf_op jit(solution)/shard_map/ppermute | solution.py:538
  118.5 2.6 %collective-permute-start.10 = (bf16[20,256]{1,0:T(8,128)(2,1)S(1)}, bf16[20,256]{1,0:T(8,128)(2,1)S(1)}, u32[]{:S(2)}, u32[]{:S(2)}) collective-permute-start(bf16[20,256]{1,0:T(8,128)(2,1)S(1)} %get-tuple-element.44), channel_id=1, source_target_pairs={{0,32},{32,0},{64,96},{96,64},{128,160},{160,128},{192,224},{224,1... | collective-permute-start | bytes 30728 | tf_op jit(solution)/shard_map/ppermute | solution.py:538
  118.9 32.3 %collective-permute-start.9 = (bf16[128,2048]{1,0:T(8,128)(2,1)S(1)}, bf16[128,2048]{1,0:T(8,128)(2,1)S(1)}, u32[]{:S(2)}, u32[]{:S(2)}) collective-permute-start(bf16[128,2048]{1,0:T(8,128)(2,1)S(1)} %get-tuple-element.43.refs_2_), channel_id=1, source_target_pairs={{0,32},{32,0},{64,96},{96,64},{128,160},{160,128},{192,224},{224,1... | collective-permute-start | bytes 1572872 | tf_op jit(solution)/shard_map/ppermute | solution.py:538
  121.1 5.2 %collective-permute-start.13 = (bf16[20,256]{1,0:T(8,128)(2,1)S(1)}, bf16[20,256]{1,0:T(8,128)(2,1)S(1)}, u32[]{:S(2)}, u32[]{:S(2)}) collective-permute-start(bf16[20,256]{1,0:T(8,128)(2,1)S(1)} %add_convert_fusion.p0), channel_id=1, source_target_pairs={{0,128},{32,160},{64,192},{96,224},{128,0},{160,32},{192,64},{224,... | collective-permute-start | bytes 30728 | tf_op jit(solution)/shard_map/ppermute | solution.py:535
  123.2 3.7 %collective-permute-start.12 = (bf16[20,256]{1,0:T(8,128)(2,1)S(1)}, bf16[20,256]{1,0:T(8,128)(2,1)S(1)}, u32[]{:S(2)}, u32[]{:S(2)}) collective-permute-start(bf16[20,256]{1,0:T(8,128)(2,1)S(1)} %add_convert_fusion.p0), channel_id=1, source_target_pairs={{0,192},{32,224},{64,0},{96,32},{128,64},{160,96},{192,128},{224,1... | collective-permute-start | bytes 30728 | tf_op jit(solution)/shard_map/ppermute | solution.py:535
  124.5 3.7 %collective-permute-start.11 = (bf16[20,256]{1,0:T(8,128)(2,1)S(1)}, bf16[20,256]{1,0:T(8,128)(2,1)S(1)}, u32[]{:S(2)}, u32[]{:S(2)}) collective-permute-start(bf16[20,256]{1,0:T(8,128)(2,1)S(1)} %add_convert_fusion.p0), channel_id=1, source_target_pairs={{0,64},{32,96},{64,128},{96,160},{128,192},{160,224},{192,0},{224,... | collective-permute-start | bytes 30728 | tf_op jit(solution)/shard_map/ppermute | solution.py:535
  128.8 0.7 copy-start
  129.5 21.6 %copy-start.9 = (bf16[256,256]{1,0:T(8,128)(2,1)}, bf16[256,256]{1,0:T(8,128)(2,1)S(1)}, u32[]{:S(2)}) copy-start(bf16[256,256]{1,0:T(8,128)(2,1)S(1)} %get-tuple-element.45.refs_4_) | copy-start | bytes 393220
  129.5 21.6 %all-to-all-start.3 = ((bf16[32,16,256]{2,1,0:T(8,128)(2,1)}), bf16[32,16,256]{2,1,0:T(8,128)(2,1)S(1)}, u32[]{:S(2)}, u32[]{:S(2)}) async-start(bf16[32,16,256]{2,1,0:T(8,128)(2,1)} %copy-done), calls=%async_computation.3 | async-start | bytes 524288 | tf_op jit(solution)/shard_map/all_to_all | solution.py:541
  139.0 1.6 %collective-permute-start.14 = (bf16[256,256]{1,0:T(8,128)(2,1)S(1)}, bf16[256,256]{1,0:T(8,128)(2,1)}, u32[]{:S(2)}, u32[]{:S(2)}) collective-permute-start(bf16[256,256]{1,0:T(8,128)(2,1)S(1)} %get-tuple-element.45.refs_4_), channel_id=1, source_target_pairs={{0,32},{32,0},{64,96},{96,64},{128,160},{160,128},{192,224},{224,1... | collective-permute-start | bytes 393224 | tf_op jit(solution)/shard_map/ppermute | solution.py:538

commit v4 on v2

--- a/solution.py
+++ b/solution.py
@@ -312,7 +312,7 @@
         ),
         compiler_params=pltpu.CompilerParams(vmem_limit_bytes=8 << 20),
         name="tie",
-    )(*parts, *shares, after)
+    )(*parts, *[hbm(x) for x in shares], hbm(after))
 
 
 def own_kernel(d_ref, feats_ref, win_ref, wout_ref, gout_ref, gin_ref):
@@ -405,8 +405,8 @@
         + ([out_spec] * 2 + [in_spec] * 2 if pieces else []),
         out_specs=(out_spec, in_spec) * (2 if pieces else 1),
         out_shape=(
-            jax.ShapeDtypeStruct((units, width), BF),
-            jax.ShapeDtypeStruct((uf, units), BF),
+            (jax.ShapeDtypeStruct if pieces else pltpu.HBM)((units, width), BF),
+            (jax.ShapeDtypeStruct if pieces else pltpu.HBM)((uf, units), BF),
         )
         + ((pltpu.HBM((wide, width), F32), pltpu.HBM((uf, wide), F32)) if pieces else ()),
         compiler_params=pltpu.CompilerParams(vmem_limit_bytes=36 << 20),
@@ -556,9 +556,6 @@
     parts = [pair] + from_chips(pair)
     d_far = from_chips(third.reshape(reqs, width))
     before = dense_own(third, arrived, win_t, tower_out, each)
-    inter_part, grad_out, column = tie(parts, [share] + far, hbm(before[1]), shards, each)
-    inter_all = exchange(inter_part)
-    other = swap(column)
     units = tower_out.shape[0] // 2
     pieces = None
     for k in range(2):
@@ -566,6 +563,10 @@
             d_far, far, win_t, tower_out, before, k * units, units, pieces
         )
         pieces = (g_out, swap(g_out), g_in, swap(g_in))
+        if k == 0:
+            inter_part, grad_out, column = tie(parts, [share] + far, g_in, shards, each)
+            inter_all = exchange(inter_part)
+            other = swap(column)
     sums = finish(pieces, column, other, inter_all, first, units)
     return (scores[None], sums[1], sums[0], sums[3], grad_out.reshape(-1), sums[2])
 

time: 154 us -> 158 us (1.026)
  local copies, waits for them, and re-layouts: 6.98 us -> 9.22 us
  Pallas kernels: 44.6 us -> 46.3 us
    unnamed x31, local copies, waits for them, and re-layouts: 5.21 us -> 7.45 us
  transfers between devices with their start and end apart: 18 -> 18, of which waited for: 10 -> 9; matrix products, arithmetic and copies ran while one was open for 2% -> 2% of each run, Pallas kernels for 6% -> 6%
where the time goes in v4:
time: 158 us
  Pallas kernels  46.3 us (29%)
  starting transfers between devices  39.5 us (25%)
  waiting for transfers between devices  38.3 us (24%)
  blocking collectives  23.3 us (15%)
  local copies, waits for them, and re-layouts  9.22 us (6%)
    all_to_all x3, starting transfers between devices, exchange(): return lax.all_to_all(x, 'tbl', split_axis=0, concat_axis=0, tiled=True)  25.8 us
    all_to_all x3, waiting for transfers between devices, exchange(): return lax.all_to_all(x, 'tbl', split_axis=0, concat_axis=0, tiled=True)  25.6 us
    all_to_all x1, blocking collectives, exchange(): return lax.all_to_all(x, 'tbl', split_axis=0, concat_axis=0, tiled=True)  23.3 us
    pallas_call x2, Pallas kernels, dense_far(): pl.pallas_call(lambda *refs: far_kernel(count, pieces is not None, *refs)...  21.8 us
    ppermute x9, starting transfers between devices, from_chips(): return [lax.ppermute(x, 'grp', ring(turn, 0)) for turn in (1, chips - 1, 2)]  12.4 us
    pallas_call x1, Pallas kernels, dense_own(): pl.pallas_call(own_kernel, grid=(wide // block,), in_specs=[feats_spec(d,...  7.77 us
    unnamed x31, local copies, waits for them, and re-layouts  7.45 us
    ppermute x6, waiting for transfers between devices, swap(): return lax.ppermute(x, 'grp', ring(0, 1))  6.48 us
  transfers between devices with their start and end apart: 18, of which 9 were waited for; matrix products, arithmetic and copies ran while one was open for 2% of the time, Pallas kernels for 6%

profile of v4, /device:TPU:8, one launch (start us, length us, event | category | flops | bytes accessed | tf_op | source)
XLA Modules:
  0.0 157.5 jit_solution(13660472431709225001)
XLA Ops:
  0.6 1.7 %pack.1 = bf16[32,32,128]{2,1,0:T(8,128)(2,1)} custom-call(bf16[16,128]{1,0:T(8,128)(2,1)} %feats_ref.1, s32[32,32]{1,0:T(8,128)} %bitcast.17, f32[32,32]{1,0:T(8,128)} %bitcast.18, s32[1,32]{1,0:T(1,128)} %live_ref.1), custom_call_target="tpu_custom_call" | custom-call | tf_op jit(solution)/shard_map/pack/pallas_call | solution.py:507
  2.3 11.3 %all-to-all-start = ((bf16[32,32,128]{2,1,0:T(8,128)(2,1)}), bf16[32,32,128]{2,1,0:T(8,128)(2,1)S(1)}, u32[]{:S(2)}, u32[]{:S(2)}) async-start(bf16[32,32,128]{2,1,0:T(8,128)(2,1)} %pack.1), calls=%async_computation | async-start | bytes 524288 | tf_op jit(solution)/shard_map/all_to_all | solution.py:540
  13.6 0.8 copy.20
  14.5 0.1 reshape.21.ids_ref
  14.6 0.8 copy.21.refs_5_
  15.4 0.9 copy-done.7
  16.3 0.7 pool.1
  17.0 9.4 %all-to-all-done.feats_ref.refs_3_ = bf16[32,32,128]{2,1,0:T(8,128)(2,1)S(1)} async-done(((bf16[32,32,128]{2,1,0:T(8,128)(2,1)}), bf16[32,32,128]{2,1,0:T(8,128)(2,1)S(1)}, u32[]{:S(2)}, u32[]{:S(2)}) %all-to-all-start) | async-done | bytes 262176 | tf_op jit(solution)/shard_map/all_to_all | solution.py:540
  26.5 4.4 %users.1.refs_0_ = bf16[256,512]{1,0:T(8,128)(2,1)S(1)} custom-call(bf16[32,32,128]{2,1,0:T(8,128)(2,1)S(1)} %all-to-all-done.feats_ref.refs_3_, bf16[128,4096]{1,0:T(8,128)(2,1)} %win_ref.1, bf16[4096,256]{1,0:T(8,128)(2,1)} %refs_7_.3), custom_call_target="tpu_custom_call" | custom-call | flops 1610612736 | bytes 4194304 | tf_op jit(solution)/shard_map/users/pallas_call | solution.py:96
  30.8 5.1 %rank.1 = (bf16[32,36,256]{2,1,0:T(8,128)(2,1)S(1)}, bf16[512,256]{1,0:T(8,128)(2,1)S(1)}) custom-call(bf16[256,512]{1,0:T(8,128)(2,1)S(1)} %users.1.refs_0_, bf16[256,1024]{1,0:T(8,128)(2,1)S(1)} %get-tuple-element.28.refs_1_, bf16[256,1024]{1,0:T(8,128)(2,1)S(1)} %get-tuple-element.29.refs_2_, bf16[32,32,128]{2,1,0:T(8,128)(2,1)S(1)} %all-to-all-done.feats_ref.refs_3_, ...), custom_call_target="tpu_custom_call" | custom-call | flops 1476395008 | bytes 4194304 | tf_op jit(solution)/shard_map/rank/pallas_call | solution.py:228
  36.0 23.3 %all_to_all.20.back_ref = bf16[32,36,256]{2,1,0:T(8,128)(2,1)S(1)} all-to-all(bf16[32,36,256]{2,1,0:T(8,128)(2,1)S(1)} %get-tuple-element.30), channel_id=1, replica_groups=mesh['grp'=8,'tbl'=32] {'tbl'}, dimensions={0} | all-to-all | bytes 1179648 | tf_op jit(solution)/shard_map/all_to_all | solution.py:540
  59.3 0.9 fold.1
  60.2 5.0 %all-to-all-start.2 = ((bf16[32,16,256]{2,1,0:T(8,128)(2,1)}), bf16[32,16,256]{2,1,0:T(8,128)(2,1)S(1)}, u32[]{:S(2)}, u32[]{:S(2)}) async-start(bf16[32,16,256]{2,1,0:T(8,128)(2,1)} %get-tuple-element.32), calls=%async_computation.2 | async-start | bytes 524288 | tf_op jit(solution)/shard_map/all_to_all | solution.py:540
  65.2 1.6 %collective-permute-start.3 = (bf16[512,256]{1,0:T(8,128)(2,1)S(1)}, bf16[512,256]{1,0:T(8,128)(2,1)S(1)}, u32[]{:S(2)}, u32[]{:S(2)}) collective-permute-start(bf16[512,256]{1,0:T(8,128)(2,1)S(1)} %get-tuple-element.33.t0), channel_id=1, source_target_pairs={{0,64},{32,96},{64,128},{96,160},{128,192},{160,224},{192,0},{224,... | collective-permute-start | bytes 786440 | tf_op jit(solution)/shard_map/ppermute | solution.py:534
  66.9 1.3 copy.22
  68.2 0.5 collective-permute-start.4
  68.6 2.3 %collective-permute-start.5 = (bf16[512,256]{1,0:T(8,128)(2,1)S(1)}, bf16[512,256]{1,0:T(8,128)(2,1)S(1)}, u32[]{:S(2)}, u32[]{:S(2)}) collective-permute-start(bf16[512,256]{1,0:T(8,128)(2,1)S(1)} %get-tuple-element.33.t0), channel_id=1, source_target_pairs={{0,128},{32,160},{64,192},{96,224},{128,0},{160,32},{192,64},{224,... | collective-permute-start | bytes 786440 | tf_op jit(solution)/shard_map/ppermute | solution.py:534
  70.9 6.5 %all-to-all-done.2.d_ref = bf16[32,16,256]{2,1,0:T(8,128)(2,1)S(1)} async-done(((bf16[32,16,256]{2,1,0:T(8,128)(2,1)}), bf16[32,16,256]{2,1,0:T(8,128)(2,1)S(1)}, u32[]{:S(2)}, u32[]{:S(2)}) %all-to-all-start.2) | async-done | bytes 262176 | tf_op jit(solution)/shard_map/all_to_all | solution.py:540
  77.4 1.6 collective-permute-start
  79.0 0.5 collective-permute-start.1
  79.5 2.3 %collective-permute-start.2 = (bf16[512,256]{1,0:T(8,128)(2,1)S(1)}, bf16[512,256]{1,0:T(8,128)(2,1)S(1)}, u32[]{:S(2)}, u32[]{:S(2)}) collective-permute-start(bf16[512,256]{1,0:T(8,128)(2,1)S(1)} %bitcast.12), channel_id=1, source_target_pairs={{0,128},{32,160},{64,192},{96,224},{128,0},{160,32},{192,64},{224,... | collective-permute-start | bytes 786440 | tf_op jit(solution)/shard_map/ppermute | solution.py:534
  81.8 7.8 %dense_own.1 = (f32[4096,256]{1,0:T(8,128)}, f32[128,4096]{1,0:T(8,128)}) custom-call(bf16[32,16,256]{2,1,0:T(8,128)(2,1)S(1)} %all-to-all-done.2.d_ref, bf16[32,32,128]{2,1,0:T(8,128)(2,1)S(1)} %all-to-all-done.feats_ref.refs_3_, bf16[4096,128]{1,0:T(8,128)(2,1)} %bitcast.13, bf16[4096,256]{1,0:T(8,128)(2,1)} %refs_7_.3), custom_call_target="tpu_custom_call" | custom-call | flops 3221225472 | bytes 10485760 | tf_op jit(solution)/shard_map/dense_own/pallas_call | solution.py:332
  89.6 2.6 %collective-permute-done.2.refs_2_ = bf16[512,256]{1,0:T(8,128)(2,1)S(1)} collective-permute-done((bf16[512,256]{1,0:T(8,128)(2,1)S(1)}, bf16[512,256]{1,0:T(8,128)(2,1)S(1)}, u32[]{:S(2)}, u32[]{:S(2)}) %collective-permute-start.2) | collective-permute-done | bytes 262176 | tf_op jit(solution)/shard_map/ppermute | solution.py:534
  92.3 0.7 copy-done.14
  93.0 10.7 %dense_far.2 = (bf16[2048,256]{1,0:T(8,128)(2,1)}, bf16[128,2048]{1,0:T(8,128)(2,1)}) custom-call(bf16[512,256]{1,0:T(8,128)(2,1)} %copy-done.12, bf16[512,256]{1,0:T(8,128)(2,1)} %copy-done.13, bf16[512,256]{1,0:T(8,128)(2,1)} %copy-done.14, bf16[512,256]{1,0:T(8,128)(2,1)} %copy-done.9, bf16[512,256]{1,0:T(8,128)(2,1)} %copy-done.10, ...), custom_call_target="tpu_custom_call" | custom-call | flops 4831838208 | bytes 10485760 | tf_op jit(solution)/shard_map/dense_far/pallas_call | solution.py:394
  103.6 0.1 collective-permute-start.6
  103.7 0.5 collective-permute-start.7
  104.2 3.1 %collective-permute-done.7.refs_13_ = bf16[128,2048]{1,0:T(8,128)(2,1)S(1)} collective-permute-done((bf16[128,2048]{1,0:T(8,128)(2,1)}, bf16[128,2048]{1,0:T(8,128)(2,1)S(1)}, u32[]{:S(2)}, u32[]{:S(2)}) %collective-permute-start.7) | collective-permute-done | bytes 524320 | tf_op jit(solution)/shard_map/ppermute | solution.py:537
  107.3 1.0 copy-done
  108.3 1.2 copy-done.5
  109.6 11.1 %dense_far.3 = (bf16[2048,256]{1,0:T(8,128)(2,1)S(1)}, bf16[128,2048]{1,0:T(8,128)(2,1)S(1)}, f32[4096,256]{1,0:T(8,128)}, f32[128,4096]{1,0:T(8,128)}) custom-call(bf16[512,256]{1,0:T(8,128)(2,1)} %copy-done.12, bf16[512,256]{1,0:T(8,128)(2,1)} %copy-done.13, bf16[512,256]{1,0:T(8,128)(2,1)} %copy-done.14, bf16[512,256]{1,0:T(8,128)(2,1)} %copy-done.9, ...), custom_call_target="tpu_custom_call" | custom-call | flops 4831838208 | bytes 10485760 | tf_op jit(solution)/shard_map/dense_far/pallas_call | solution.py:394
  120.7 0.2 collective-permute-start.8
  120.8 0.4 collective-permute-start.10
  121.2 0.1 collective-permute-start.9
  121.4 2.0 %collective-permute-done.10 = bf16[20,256]{1,0:T(8,128)(2,1)S(1)} collective-permute-done((bf16[20,256]{1,0:T(8,128)(2,1)S(1)}, bf16[20,256]{1,0:T(8,128)(2,1)S(1)}, u32[]{:S(2)}, u32[]{:S(2)}) %collective-permute-start.10) | collective-permute-done | bytes 10272 | tf_op jit(solution)/shard_map/ppermute | solution.py:537
  123.4 2.0 %collective-permute-start.12 = (bf16[20,256]{1,0:T(8,128)(2,1)S(1)}, bf16[20,256]{1,0:T(8,128)(2,1)S(1)}, u32[]{:S(2)}, u32[]{:S(2)}) collective-permute-start(bf16[20,256]{1,0:T(8,128)(2,1)S(1)} %add_convert_fusion.p0), channel_id=1, source_target_pairs={{0,192},{32,224},{64,0},{96,32},{128,64},{160,96},{192,128},{224,1... | collective-permute-start | bytes 30728 | tf_op jit(solution)/shard_map/ppermute | solution.py:534
  125.4 1.6 %collective-permute-start.13 = (bf16[20,256]{1,0:T(8,128)(2,1)S(1)}, bf16[20,256]{1,0:T(8,128)(2,1)S(1)}, u32[]{:S(2)}, u32[]{:S(2)}) collective-permute-start(bf16[20,256]{1,0:T(8,128)(2,1)S(1)} %add_convert_fusion.p0), channel_id=1, source_target_pairs={{0,128},{32,160},{64,192},{96,224},{128,0},{160,32},{192,64},{224,... | collective-permute-start | bytes 30728 | tf_op jit(solution)/shard_map/ppermute | solution.py:534
  127.1 0.2 collective-permute-done.12.pb
  127.3 3.4 %collective-permute-done.13.pc = bf16[20,256]{1,0:T(8,128)(2,1)S(1)} collective-permute-done((bf16[20,256]{1,0:T(8,128)(2,1)S(1)}, bf16[20,256]{1,0:T(8,128)(2,1)S(1)}, u32[]{:S(2)}, u32[]{:S(2)}) %collective-permute-start.13) | collective-permute-done | bytes 10272 | tf_op jit(solution)/shard_map/ppermute | solution.py:534
  130.6 1.7 %tie.1 = (bf16[32,16,256]{2,1,0:T(8,128)(2,1)S(1)}, f32[1,512]{1,0:T(1,128)}, bf16[256,256]{1,0:T(8,128)(2,1)S(1)}) custom-call(bf16[20,256]{1,0:T(8,128)(2,1)S(1)} %add_convert_fusion.p0, bf16[20,256]{1,0:T(8,128)(2,1)S(1)} %collective-permute-done.11.pa, bf16[20,256]{1,0:T(8,128)(2,1)S(1)} %collective-permute-done.12.pb, ...), custom_call_target="tpu_custom_call" | custom-call | tf_op jit(solution)/shard_map/tie/pallas_call | solution.py:297
  132.3 0.7 copy-done.2
  133.0 9.5 %all-to-all-start.3 = ((bf16[32,16,256]{2,1,0:T(8,128)(2,1)}), bf16[32,16,256]{2,1,0:T(8,128)(2,1)S(1)}, u32[]{:S(2)}, u32[]{:S(2)}) async-start(bf16[32,16,256]{2,1,0:T(8,128)(2,1)} %copy-done.2), calls=%async_computation.3 | async-start | bytes 524288 | tf_op jit(solution)/shard_map/all_to_all | solution.py:540
  142.5 0.1 collective-permute-start.14
  142.6 1.3 collective-permute-done.14.refs_5_
  143.9 0.7 copy-done.3
  144.6 9.6 %all-to-all-done.3.refs_6_.refs_7_ = bf16[32,16,256]{2,1,0:T(8,128)(2,1)S(1)} async-done(((bf16[32,16,256]{2,1,0:T(8,128)(2,1)}), bf16[32,16,256]{2,1,0:T(8,128)(2,1)S(1)}, u32[]{:S(2)}, u32[]{:S(2)}) %all-to-all-start.3) | async-done | bytes 262176 | tf_op jit(solution)/shard_map/all_to_all | solution.py:540
  154.2 0.9 copy-done.4
  155.1 2.4 %finish.1 = (f32[4096,256]{1,0:T(8,128)}, f32[128,4096]{1,0:T(8,128)}, f32[256,256]{1,0:T(8,128)}, f32[256,512]{1,0:T(8,128)}) custom-call(bf16[2048,256]{1,0:T(8,128)(2,1)S(1)} %get-tuple-element.38.refs_0_, bf16[2048,256]{1,0:T(8,128)(2,1)S(1)} %collective-permute-done.8.refs_1_, ...), custom_call_target="tpu_custom_call", output_to_operand_aliasing={{0}: (8, {}), {1}: (9, {})} | custom-call | tf_op jit(solution)/shard_map/finish/pallas_call | solution.py:444
  (34 shorter events, 0.1 us)
Async XLA Ops:
  2.3 24.1 %all-to-all-start = ((bf16[32,32,128]{2,1,0:T(8,128)(2,1)}), bf16[32,32,128]{2,1,0:T(8,128)(2,1)S(1)}, u32[]{:S(2)}, u32[]{:S(2)}) async-start(bf16[32,32,128]{2,1,0:T(8,128)(2,1)} %pack.1), calls=%async_computation | async-start | bytes 524288 | tf_op jit(solution)/shard_map/all_to_all | solution.py:540
  15.4 0.9 copy-start.7
  17.0 13.8 %copy-start.6 = (bf16[256,512]{1,0:T(8,128)(2,1)S(1)}, bf16[256,512]{1,0:T(8,128)(2,1)}, u32[]{:S(2)}) copy-start(bf16[256,512]{1,0:T(8,128)(2,1)} %refs_4_.1) | copy-start | bytes 786436
  35.9 32.7 %copy-start.1 = (bf16[512,256]{1,0:T(8,128)(2,1)}, bf16[512,256]{1,0:T(8,128)(2,1)S(1)}, u32[]{:S(2)}) copy-start(bf16[512,256]{1,0:T(8,128)(2,1)S(1)} %get-tuple-element.33.t0) | copy-start | bytes 786436
  35.9 30.9 %copy-start.8 = (bf16[128,4096]{1,0:T(8,128)(2,1)S(1)}, bf16[128,4096]{1,0:T(8,128)(2,1)}, u32[]{:S(2)}) copy-start(bf16[128,4096]{1,0:T(8,128)(2,1)} %win_ref.1) | copy-start | bytes 3145732
  60.2 17.2 %all-to-all-start.2 = ((bf16[32,16,256]{2,1,0:T(8,128)(2,1)}), bf16[32,16,256]{2,1,0:T(8,128)(2,1)S(1)}, u32[]{:S(2)}, u32[]{:S(2)}) async-start(bf16[32,16,256]{2,1,0:T(8,128)(2,1)} %get-tuple-element.32), calls=%async_computation.2 | async-start | bytes 524288 | tf_op jit(solution)/shard_map/all_to_all | solution.py:540
  65.2 14.2 %collective-permute-start.3 = (bf16[512,256]{1,0:T(8,128)(2,1)S(1)}, bf16[512,256]{1,0:T(8,128)(2,1)S(1)}, u32[]{:S(2)}, u32[]{:S(2)}) collective-permute-start(bf16[512,256]{1,0:T(8,128)(2,1)S(1)} %get-tuple-element.33.t0), channel_id=1, source_target_pairs={{0,64},{32,96},{64,128},{96,160},{128,192},{160,224},{192,0},{224,... | collective-permute-start | bytes 786440 | tf_op jit(solution)/shard_map/ppermute | solution.py:534
  68.2 21.4 %collective-permute-start.4 = (bf16[512,256]{1,0:T(8,128)(2,1)S(1)}, bf16[512,256]{1,0:T(8,128)(2,1)S(1)}, u32[]{:S(2)}, u32[]{:S(2)}) collective-permute-start(bf16[512,256]{1,0:T(8,128)(2,1)S(1)} %get-tuple-element.33.t0), channel_id=1, source_target_pairs={{0,192},{32,224},{64,0},{96,32},{128,64},{160,96},{192,128},{224,1... | collective-permute-start | bytes 786440 | tf_op jit(solution)/shard_map/ppermute | solution.py:534
  68.6 20.9 %collective-permute-start.5 = (bf16[512,256]{1,0:T(8,128)(2,1)S(1)}, bf16[512,256]{1,0:T(8,128)(2,1)S(1)}, u32[]{:S(2)}, u32[]{:S(2)}) collective-permute-start(bf16[512,256]{1,0:T(8,128)(2,1)S(1)} %get-tuple-element.33.t0), channel_id=1, source_target_pairs={{0,128},{32,160},{64,192},{96,224},{128,0},{160,32},{192,64},{224,... | collective-permute-start | bytes 786440 | tf_op jit(solution)/shard_map/ppermute | solution.py:534
  77.4 12.1 %collective-permute-start = (bf16[512,256]{1,0:T(8,128)(2,1)S(1)}, bf16[512,256]{1,0:T(8,128)(2,1)S(1)}, u32[]{:S(2)}, u32[]{:S(2)}) collective-permute-start(bf16[512,256]{1,0:T(8,128)(2,1)S(1)} %bitcast.10), channel_id=1, source_target_pairs={{0,64},{32,96},{64,128},{96,160},{128,192},{160,224},{192,0},{224,... | collective-permute-start | bytes 786440 | tf_op jit(solution)/shard_map/ppermute | solution.py:534
  79.0 10.6 %collective-permute-start.1 = (bf16[512,256]{1,0:T(8,128)(2,1)S(1)}, bf16[512,256]{1,0:T(8,128)(2,1)S(1)}, u32[]{:S(2)}, u32[]{:S(2)}) collective-permute-start(bf16[512,256]{1,0:T(8,128)(2,1)S(1)} %bitcast.11), channel_id=1, source_target_pairs={{0,192},{32,224},{64,0},{96,32},{128,64},{160,96},{192,128},{224,1... | collective-permute-start | bytes 786440 | tf_op jit(solution)/shard_map/ppermute | solution.py:534
  79.5 10.1 %copy-start.9 = (bf16[512,256]{1,0:T(8,128)(2,1)}, bf16[512,256]{1,0:T(8,128)(2,1)S(1)}, u32[]{:S(2)}) copy-start(bf16[512,256]{1,0:T(8,128)(2,1)S(1)} %collective-permute-done.3.refs_3_.ta) | copy-start | bytes 786436
  79.5 12.8 %collective-permute-start.2 = (bf16[512,256]{1,0:T(8,128)(2,1)S(1)}, bf16[512,256]{1,0:T(8,128)(2,1)S(1)}, u32[]{:S(2)}, u32[]{:S(2)}) collective-permute-start(bf16[512,256]{1,0:T(8,128)(2,1)S(1)} %bitcast.12), channel_id=1, source_target_pairs={{0,128},{32,160},{64,192},{96,224},{128,0},{160,32},{192,64},{224,... | collective-permute-start | bytes 786440 | tf_op jit(solution)/shard_map/ppermute | solution.py:534
  89.5 2.7 %copy-start.10 = (bf16[512,256]{1,0:T(8,128)(2,1)}, bf16[512,256]{1,0:T(8,128)(2,1)S(1)}, u32[]{:S(2)}) copy-start(bf16[512,256]{1,0:T(8,128)(2,1)S(1)} %collective-permute-done.4.refs_4_.tb) | copy-start | bytes 786436
  89.6 2.7 %copy-start.11 = (bf16[512,256]{1,0:T(8,128)(2,1)}, bf16[512,256]{1,0:T(8,128)(2,1)S(1)}, u32[]{:S(2)}) copy-start(bf16[512,256]{1,0:T(8,128)(2,1)S(1)} %collective-permute-done.5.refs_5_.tc) | copy-start | bytes 786436
  89.6 2.7 %copy-start.12 = (bf16[512,256]{1,0:T(8,128)(2,1)}, bf16[512,256]{1,0:T(8,128)(2,1)S(1)}, u32[]{:S(2)}) copy-start(bf16[512,256]{1,0:T(8,128)(2,1)S(1)} %collective-permute-done.refs_0_) | copy-start | bytes 786436
  89.6 2.6 %copy-start.13 = (bf16[512,256]{1,0:T(8,128)(2,1)}, bf16[512,256]{1,0:T(8,128)(2,1)S(1)}, u32[]{:S(2)}) copy-start(bf16[512,256]{1,0:T(8,128)(2,1)S(1)} %collective-permute-done.1.refs_1_) | copy-start | bytes 786436
  92.2 0.7 copy-start.14
  103.6 3.7 %collective-permute-start.6 = (bf16[2048,256]{1,0:T(8,128)(2,1)}, bf16[2048,256]{1,0:T(8,128)(2,1)S(1)}, u32[]{:S(2)}, u32[]{:S(2)}) collective-permute-start(bf16[2048,256]{1,0:T(8,128)(2,1)} %get-tuple-element.36.refs_10_), channel_id=1, source_target_pairs={{0,32},{32,0},{64,96},{96,64},{128,160},{160,128},{192,224},{224,1... | collective-permute-start | bytes 3145736 | tf_op jit(solution)/shard_map/ppermute | solution.py:537
  103.7 3.6 %collective-permute-start.7 = (bf16[128,2048]{1,0:T(8,128)(2,1)}, bf16[128,2048]{1,0:T(8,128)(2,1)S(1)}, u32[]{:S(2)}, u32[]{:S(2)}) collective-permute-start(bf16[128,2048]{1,0:T(8,128)(2,1)} %get-tuple-element.37.refs_12_.after_ref), channel_id=1, source_target_pairs={{0,32},{32,0},{64,96},{96,64},{128,160},{160,128},{192,224},{224,1... | collective-permute-start | bytes 1572872 | tf_op jit(solution)/shard_map/ppermute | solution.py:537
  107.3 1.0 copy-start
  108.3 1.2 copy-start.5
  120.7 33.6 %collective-permute-start.8 = (bf16[2048,256]{1,0:T(8,128)(2,1)S(1)}, bf16[2048,256]{1,0:T(8,128)(2,1)S(1)}, u32[]{:S(2)}, u32[]{:S(2)}) collective-permute-start(bf16[2048,256]{1,0:T(8,128)(2,1)S(1)} %get-tuple-element.38.refs_0_), channel_id=1, source_target_pairs={{0,32},{32,0},{64,96},{96,64},{128,160},{160,128},{192,224},{224,1... | collective-permute-start | bytes 3145736 | tf_op jit(solution)/shard_map/ppermute | solution.py:537
  120.8 2.5 %collective-permute-start.10 = (bf16[20,256]{1,0:T(8,128)(2,1)S(1)}, bf16[20,256]{1,0:T(8,128)(2,1)S(1)}, u32[]{:S(2)}, u32[]{:S(2)}) collective-permute-start(bf16[20,256]{1,0:T(8,128)(2,1)S(1)} %get-tuple-element.40), channel_id=1, source_target_pairs={{0,32},{32,0},{64,96},{96,64},{128,160},{160,128},{192,224},{224,1... | collective-permute-start | bytes 30728 | tf_op jit(solution)/shard_map/ppermute | solution.py:537
  121.2 33.0 %collective-permute-start.9 = (bf16[128,2048]{1,0:T(8,128)(2,1)S(1)}, bf16[128,2048]{1,0:T(8,128)(2,1)S(1)}, u32[]{:S(2)}, u32[]{:S(2)}) collective-permute-start(bf16[128,2048]{1,0:T(8,128)(2,1)S(1)} %get-tuple-element.39.refs_2_), channel_id=1, source_target_pairs={{0,32},{32,0},{64,96},{96,64},{128,160},{160,128},{192,224},{224,1... | collective-permute-start | bytes 1572872 | tf_op jit(solution)/shard_map/ppermute | solution.py:537
  123.4 3.7 %collective-permute-start.11 = (bf16[20,256]{1,0:T(8,128)(2,1)S(1)}, bf16[20,256]{1,0:T(8,128)(2,1)S(1)}, u32[]{:S(2)}, u32[]{:S(2)}) collective-permute-start(bf16[20,256]{1,0:T(8,128)(2,1)S(1)} %add_convert_fusion.p0), channel_id=1, source_target_pairs={{0,64},{32,96},{64,128},{96,160},{128,192},{160,224},{192,0},{224,... | collective-permute-start | bytes 30728 | tf_op jit(solution)/shard_map/ppermute | solution.py:534
  123.4 3.9 %collective-permute-start.12 = (bf16[20,256]{1,0:T(8,128)(2,1)S(1)}, bf16[20,256]{1,0:T(8,128)(2,1)S(1)}, u32[]{:S(2)}, u32[]{:S(2)}) collective-permute-start(bf16[20,256]{1,0:T(8,128)(2,1)S(1)} %add_convert_fusion.p0), channel_id=1, source_target_pairs={{0,192},{32,224},{64,0},{96,32},{128,64},{160,96},{192,128},{224,1... | collective-permute-start | bytes 30728 | tf_op jit(solution)/shard_map/ppermute | solution.py:534
  125.4 5.2 %collective-permute-start.13 = (bf16[20,256]{1,0:T(8,128)(2,1)S(1)}, bf16[20,256]{1,0:T(8,128)(2,1)S(1)}, u32[]{:S(2)}, u32[]{:S(2)}) collective-permute-start(bf16[20,256]{1,0:T(8,128)(2,1)S(1)} %add_convert_fusion.p0), channel_id=1, source_target_pairs={{0,128},{32,160},{64,192},{96,224},{128,0},{160,32},{192,64},{224,... | collective-permute-start | bytes 30728 | tf_op jit(solution)/shard_map/ppermute | solution.py:534
  132.3 0.7 copy-start.2
  133.0 21.2 %all-to-all-start.3 = ((bf16[32,16,256]{2,1,0:T(8,128)(2,1)}), bf16[32,16,256]{2,1,0:T(8,128)(2,1)S(1)}, u32[]{:S(2)}, u32[]{:S(2)}) async-start(bf16[32,16,256]{2,1,0:T(8,128)(2,1)} %copy-done.2), calls=%async_computation.3 | async-start | bytes 524288 | tf_op jit(solution)/shard_map/all_to_all | solution.py:540
  142.5 1.4 collective-permute-start.14
  143.9 0.7 copy-start.3
  154.2 0.9 copy-start.4
